TPU v7x, 32 devices: a whole 2x2x4 slice. The times are simulated.
32 devices in a mesh: dp: 8 (over y, x, core), tensor: 4 (over z).
Axes of the slice: x: 2, y: 2, z: 4, core: 2. Of those that a mesh axis runs over, the one named last changes fastest.
Arguments:
- tokens: bfloat16 [8192, 1024], P(('dp', 'tensor')), may hold values from -6 to 6
- lengths: int32 [32], replicated, may hold values from 64 to 832, as said below
- seq_order: int32 [32], replicated, may hold values from 0 to 31, as said below
- gain_attn: bfloat16 [1024], P('dp'), may hold values from 0.5 to 1.5
- w_qkv: bfloat16 [3, 1024, 1024], P(None, 'dp', 'tensor'), may hold values from -0.25 to 0.25
- w_attn_out: bfloat16 [1024, 1024], P('tensor', 'dp'), may hold values from -0.375 to 0.375
- gain_mlp: bfloat16 [1024], P('dp'), may hold values from 0.5 to 1.5
- w_in: bfloat16 [1024, 2, 2624], P('dp', None, 'tensor'), may hold values from -0.1875 to 0.1875
- w_mlp_out: bfloat16 [2624, 1024], P('tensor', 'dp'), may hold values from -0.15625 to 0.15625
- cotangent: bfloat16 [8192, 1024], P(('dp', 'tensor')), may hold values from -6 to 6
Outputs:
- output: bfloat16 [8192, 1024], P(('dp', 'tensor'))
- d_tokens: float32 [8192, 1024], P(('dp', 'tensor'))
- d_gain_attn: float32 [1024], P('dp')
- d_w_qkv: float32 [3, 1024, 1024], P(None, 'dp', 'tensor')
- d_w_attn_out: float32 [1024, 1024], P('tensor', 'dp')
- d_gain_mlp: float32 [1024], P('dp')
- d_w_in: float32 [1024, 2, 2624], P('dp', None, 'tensor')
- d_w_mlp_out: float32 [2624, 1024], P('tensor', 'dp')
Inputs may be any that keep to these rules, and one draw needn't show every extreme that they name: For every g the lengths of the sequences seq_order[g * 4] to seq_order[g * 4 + 3] add up to 1024; in every draw some g holds one sequence of the greatest length and 3 of the least. `seq_order`: each sequence number stands once.
All inputs are finite; a program needn't handle non-finite values.
Results may differ from a plain program's by a relative error of at most 0.017.
Values may be sent and summed in bfloat16 or wider, within the bound.
A program may use at most 128 MiB of HBM per device.

v0:
```python
import jax
import jax.numpy as jnp
from jax import lax
from jax.sharding import PartitionSpec as P

HEAD_DIM = 64
SEQ_GRP = 4


rope_base = 160000.0
norm_eps = 1e-05
masked_fill = -1e30


def layer_norm(field_in, norm_gain):
    row_mean = jnp.mean(field_in, axis=-1, keepdims=True)
    centered = field_in - row_mean
    variance = jnp.mean(centered * centered, axis=-1, keepdims=True)
    return centered * lax.rsqrt(variance + norm_eps) * norm_gain


def rotate(field_in, position):
    half_size = field_in.shape[-1] // 2
    index_range = jnp.arange(half_size, dtype=jnp.float32)
    frequency = rope_base ** (-2.0 * index_range / field_in.shape[-1])
    angles = position[:, None] * frequency[None, :]
    cosine = jnp.cos(angles)[:, None, :]
    sine_part = jnp.sin(angles)[:, None, :]
    first_half = field_in[..., :half_size]
    second_half = field_in[..., half_size:]
    return jnp.concatenate(
        [
            first_half * cosine - second_half * sine_part,
            second_half * cosine + first_half * sine_part,
        ],
        axis=-1,
    )


def geglu(act_part, up_part):
    return jax.nn.gelu(act_part, approximate=False) * up_part


def layout(lengths, seq_order, group_rows):
    seq_total = seq_order.shape[0]
    first_seq = lax.axis_index("dp") * SEQ_GRP
    chosen = lax.dynamic_slice_in_dim(seq_order, first_seq, SEQ_GRP)
    matched = chosen[:, None] == jnp.arange(seq_total, dtype=jnp.int32)[None, :]
    dealt_lengths = jnp.sum(jnp.where(matched, lengths[None, :], 0), axis=1)
    seq_ends = jnp.cumsum(dealt_lengths)
    row_index = jnp.arange(group_rows, dtype=jnp.int32)
    passed = row_index[:, None] >= seq_ends[None, :]
    segment = jnp.sum(passed.astype(jnp.int32), axis=1)
    row_start = jnp.sum(jnp.where(passed, dealt_lengths[None, :], 0), axis=1)
    return (segment, (row_index - row_start).astype(jnp.float32))


def item_layout(array_in, block_rows):
    group_rows, head_count, head_size = array_in.shape
    block_count = group_rows // block_rows
    shaped = array_in.reshape(block_count, block_rows, head_count, head_size)
    return shaped.transpose(2, 0, 1, 3).reshape(head_count * block_count, block_rows, head_size)


def from_items(items, group_rows):
    item_count, block_rows, head_size = items.shape
    block_count = group_rows // block_rows
    head_count = item_count // block_count
    shaped = items.reshape(head_count, block_count, block_rows, head_size)
    return shaped.transpose(1, 2, 0, 3).reshape(group_rows, head_count, head_size)


def masked_scores(query_block, key_head, segment_block, segment):
    score_scale = query_block.shape[-1] ** (-0.5)
    raw_scores = lax.dot_general(
        query_block, key_head, (((1,), (1,)), ((), ())), preferred_element_type=jnp.float32
    )
    allowed = segment_block[:, None] == segment[None, :]
    return jnp.where(allowed, raw_scores * score_scale, masked_fill)


def attend_forward(query_rot, key_rot, value_low, segment, block_rows):
    group_rows, head_count, head_size = query_rot.shape
    block_count = group_rows // block_rows
    query_items = item_layout(query_rot, block_rows)
    key_heads = key_rot.transpose(1, 0, 2)
    value_heads = value_low.transpose(1, 0, 2)
    segment_blocks = segment.reshape(block_count, block_rows)

    def one_item(item_index):
        head_index = item_index // block_count
        block_index = item_index % block_count
        query_block = lax.dynamic_index_in_dim(query_items, item_index, 0, False)
        key_head = lax.dynamic_index_in_dim(key_heads, head_index, 0, False)
        value_head = lax.dynamic_index_in_dim(value_heads, head_index, 0, False)
        segment_block = lax.dynamic_index_in_dim(segment_blocks, block_index, 0, False)
        scores = masked_scores(query_block, key_head, segment_block, segment)
        row_top = jnp.max(scores, axis=1, keepdims=True)
        weights = jnp.exp(scores - row_top)
        row_total = jnp.sum(weights, axis=1, keepdims=True)
        probs_low = (weights / row_total).astype(jnp.bfloat16)
        result = jnp.dot(probs_low, value_head, preferred_element_type=jnp.float32)
        return (result, row_top[:, 0] + jnp.log(row_total[:, 0]))

    results, log_totals = lax.map(one_item, jnp.arange(head_count * block_count, dtype=jnp.int32))
    return (from_items(results, group_rows), log_totals)


def attend_backward(query_rot, key_rot, value_low, grad_out, log_totals, segment, block_rows):
    group_rows, head_count, head_size = query_rot.shape
    block_count = group_rows // block_rows
    score_scale = head_size ** (-0.5)
    query_items = item_layout(query_rot, block_rows)
    grad_items = item_layout(grad_out, block_rows)
    key_heads = key_rot.transpose(1, 0, 2)
    value_heads = value_low.transpose(1, 0, 2)
    segment_blocks = segment.reshape(block_count, block_rows)

    def one_item(carried, item_index):
        key_grads, value_grads = carried
        head_index = item_index // block_count
        block_index = item_index % block_count
        query_block = lax.dynamic_index_in_dim(query_items, item_index, 0, False)
        grad_block = lax.dynamic_index_in_dim(grad_items, item_index, 0, False)
        log_row = lax.dynamic_index_in_dim(log_totals, item_index, 0, False)
        key_head = lax.dynamic_index_in_dim(key_heads, head_index, 0, False)
        value_head = lax.dynamic_index_in_dim(value_heads, head_index, 0, False)
        segment_block = lax.dynamic_index_in_dim(segment_blocks, block_index, 0, False)
        scores = masked_scores(query_block, key_head, segment_block, segment)
        prob_full = jnp.exp(scores - log_row[:, None])
        probs_low = prob_full.astype(jnp.bfloat16)
        grad_probs = lax.dot_general(
            grad_block, value_head, (((1,), (1,)), ((), ())), preferred_element_type=jnp.float32
        )
        row_delta = jnp.sum(prob_full * grad_probs, axis=1, keepdims=True)
        grad_scores = (prob_full * (grad_probs - row_delta)).astype(jnp.bfloat16)
        grad_query = (
            jnp.dot(grad_scores, key_head, preferred_element_type=jnp.float32) * score_scale
        )
        grad_key = (
            lax.dot_general(
                grad_scores,
                query_block,
                (((0,), (0,)), ((), ())),
                preferred_element_type=jnp.float32,
            )
            * score_scale
        )
        grad_value = lax.dot_general(
            probs_low, grad_block, (((0,), (0,)), ((), ())), preferred_element_type=jnp.float32
        )
        key_grads = lax.dynamic_update_index_in_dim(
            key_grads,
            lax.dynamic_index_in_dim(key_grads, head_index, 0, False) + grad_key,
            head_index,
            0,
        )
        value_grads = lax.dynamic_update_index_in_dim(
            value_grads,
            lax.dynamic_index_in_dim(value_grads, head_index, 0, False) + grad_value,
            head_index,
            0,
        )
        return ((key_grads, value_grads), grad_query)

    zero_heads = jnp.zeros((head_count, group_rows, head_size), jnp.float32)
    (key_grads, value_grads), query_grads = lax.scan(
        one_item, (zero_heads, zero_heads), jnp.arange(head_count * block_count, dtype=jnp.int32)
    )
    return (
        from_items(query_grads, group_rows),
        key_grads.transpose(1, 0, 2),
        value_grads.transpose(1, 0, 2),
    )


def spread_rows(local_rows):
    return lax.all_gather(local_rows, "tensor", axis=0, tiled=True)


def spread_grads(local_grads):
    return lax.all_gather(local_grads, "tensor", axis=0, tiled=True)


def sum_heads(activations, weight_part, row_count):

    def row_term(first_row, row_number):
        return jnp.dot(activations, weight_part, preferred_element_type=jnp.float32)

    return lax.psum_scatter(
        row_term(jnp.int32(0), row_count * lax.axis_size("tensor")),
        "tensor",
        scatter_dimension=0,
        tiled=True,
    )


def sum_grads(grads_low, weight_full, einsum_form, row_count):

    def row_term(first_row, row_number):
        return jnp.einsum(einsum_form, grads_low, weight_full, preferred_element_type=jnp.float32)

    return lax.psum_scatter(
        row_term(jnp.int32(0), row_count * lax.axis_size("tensor")),
        "tensor",
        scatter_dimension=0,
        tiled=True,
    )


def local(
    tokens, lengths, seq_order, gain_attn, w_qkv, w_attn_out, gain_mlp, w_in, w_mlp_out, cotangent
):
    row_count = tokens.shape[0]
    group_rows = row_count * lax.axis_size("tensor")
    block_rows = min(512, group_rows)
    segment, position = layout(lengths, seq_order, group_rows)
    gain_low_one, qkv_weight, out_weight, gain_low_two, in_weight, down_weight = (
        lax.all_gather(gain_attn, "dp", axis=0, tiled=True),
        lax.all_gather(w_qkv, "dp", axis=1, tiled=True),
        lax.all_gather(w_attn_out, "dp", axis=1, tiled=True),
        lax.all_gather(gain_mlp, "dp", axis=0, tiled=True),
        lax.all_gather(w_in, "dp", axis=0, tiled=True),
        lax.all_gather(w_mlp_out, "dp", axis=1, tiled=True),
    )
    gain_one = gain_low_one.astype(jnp.float32)
    gain_two = gain_low_two.astype(jnp.float32)
    residual = tokens.astype(jnp.float32)
    normed_one = spread_rows(layer_norm(residual, gain_one).astype(jnp.bfloat16))
    qkv = jnp.einsum("rd,pdc->rpc", normed_one, qkv_weight, preferred_element_type=jnp.float32)
    head_count = qkv.shape[2] // HEAD_DIM
    head_shape = (group_rows, head_count, HEAD_DIM)
    query_rot = rotate(qkv[:, 0].reshape(head_shape), position).astype(jnp.bfloat16)
    key_rot = rotate(qkv[:, 1].reshape(head_shape), position).astype(jnp.bfloat16)
    value_low = qkv[:, 2].reshape(head_shape).astype(jnp.bfloat16)
    attended, log_totals = attend_forward(query_rot, key_rot, value_low, segment, block_rows)
    attn_low = attended.reshape(group_rows, head_count * HEAD_DIM).astype(jnp.bfloat16)
    resid_mid = residual + sum_heads(attn_low, out_weight, row_count)
    normed_two = spread_rows(layer_norm(resid_mid, gain_two).astype(jnp.bfloat16))
    gate_up = jnp.einsum("rd,dpc->rpc", normed_two, in_weight, preferred_element_type=jnp.float32)
    hidden = geglu(gate_up[:, 0], gate_up[:, 1]).astype(jnp.bfloat16)
    output = (resid_mid + sum_heads(hidden, down_weight, row_count)).astype(jnp.bfloat16)
    grad_two = spread_grads(cotangent)
    d_hidden = lax.dot_general(
        grad_two, down_weight, (((1,), (1,)), ((), ())), preferred_element_type=jnp.float32
    )
    d_down = lax.dot_general(
        hidden, grad_two, (((0,), (0,)), ((), ())), preferred_element_type=jnp.float32
    )
    geglu_pull = jax.vjp(geglu, gate_up[:, 0], gate_up[:, 1])[1]
    d_act, d_up = geglu_pull(d_hidden)
    d_gate_up = jnp.stack([d_act, d_up], axis=1).astype(jnp.bfloat16)
    d_in = jnp.einsum("rd,rpc->dpc", normed_two, d_gate_up, preferred_element_type=jnp.float32)
    d_normed_two = sum_grads(d_gate_up, in_weight, "rpc,dpc->rd", row_count)
    norm_pull_two = jax.vjp(layer_norm, resid_mid, gain_two)[1]
    d_mid_norm, d_gain_two = norm_pull_two(d_normed_two)
    d_mid = cotangent.astype(jnp.float32) + d_mid_norm
    grad_one = spread_grads(d_mid.astype(jnp.bfloat16))
    d_out = lax.dot_general(
        attn_low, grad_one, (((0,), (0,)), ((), ())), preferred_element_type=jnp.float32
    )
    d_att = lax.dot_general(
        grad_one, out_weight, (((1,), (1,)), ((), ())), preferred_element_type=jnp.float32
    ).astype(jnp.bfloat16)
    d_query_rot, d_key_rot, d_value = attend_backward(
        query_rot, key_rot, value_low, d_att.reshape(head_shape), log_totals, segment, block_rows
    )
    rotate_pull = jax.vjp(lambda field_in: rotate(field_in, position), d_query_rot)[1]
    d_query = rotate_pull(d_query_rot)[0]
    d_key = rotate_pull(d_key_rot)[0]
    flat_shape = (group_rows, head_count * HEAD_DIM)
    d_qkv = jnp.stack(
        [d_query.reshape(flat_shape), d_key.reshape(flat_shape), d_value.reshape(flat_shape)],
        axis=1,
    ).astype(jnp.bfloat16)
    d_qkv_weight = jnp.einsum("rd,rpc->pdc", normed_one, d_qkv, preferred_element_type=jnp.float32)
    d_normed_one = sum_grads(d_qkv, qkv_weight, "rpc,pdc->rd", row_count)
    norm_pull_one = jax.vjp(layer_norm, residual, gain_one)[1]
    d_first, d_gain_one = norm_pull_one(d_normed_one)
    d_tokens = d_mid + d_first
    gain_sums = lax.psum((d_gain_one, d_gain_two), "tensor")
    shares = (
        lax.psum_scatter(gain_sums[0], "dp", scatter_dimension=0, tiled=True),
        lax.psum_scatter(d_qkv_weight, "dp", scatter_dimension=1, tiled=True),
        lax.psum_scatter(d_out, "dp", scatter_dimension=1, tiled=True),
        lax.psum_scatter(gain_sums[1], "dp", scatter_dimension=0, tiled=True),
        lax.psum_scatter(d_in, "dp", scatter_dimension=0, tiled=True),
        lax.psum_scatter(d_down, "dp", scatter_dimension=1, tiled=True),
    )
    return (output, d_tokens, shares[0], shares[1], shares[2], shares[3], shares[4], shares[5])


def solution(mesh):
    return jax.shard_map(
        local,
        mesh=mesh,
        in_specs=(
            P(("dp", "tensor"), None),
            P(),
            P(),
            P("dp"),
            P(None, "dp", "tensor"),
            P("tensor", "dp"),
            P("dp"),
            P("dp", None, "tensor"),
            P("tensor", "dp"),
            P(("dp", "tensor"), None),
        ),
        out_specs=(
            P(("dp", "tensor"), None),
            P(("dp", "tensor"), None),
            P("dp"),
            P(None, "dp", "tensor"),
            P("tensor", "dp"),
            P("dp"),
            P("dp", None, "tensor"),
            P("tensor", "dp"),
        ),
        check_vma=False,
    )
```

profile of v0, /device:TPU:0, one launch (start us, length us, event | category | flops | bytes accessed | tf_op | source)
XLA Modules:
  0.0 1052.8 jit_solution(94516916821931615)
XLA Ops:
  9.1 10.3 all-gather
  24.8 12.0 %all_gather.33 = bf16[256,1024]{1,0:T(8,128)(2,1)} all-gather(bf16[256,128]{1,0:T(8,128)(2,1)S(1)} %copy-done.20), channel_id=1, replica_groups=mesh['dp'=8,'tensor'=4] {'dp'}, dimensions={1}, use_global_device_ids=true | all-gather | bytes 589824 | tf_op jit(solution)/shard_map/all_gather | solution.py:221
  39.8 48.1 %all-gather.10.cloned.1.call-done = bf16[1024,1024]{1,0:T(8,128)(2,1)} async-done(((bf16[256,1024]{1,0:T(8,128)(2,1)}), bf16[1024,1024]{1,0:T(8,128)(2,1)}) %all-gather.10.cloned.1.call-update) | async-done | bytes 2097168 | tf_op jit(solution)/shard_map/all_gather | solution.py:178
  96.9 70.1 %while.32 = (s32[]{:T(128)}, bf16[8,512,64]{1,2,0:T(8,128)(2,1)}, f32[8,512]{1,0:T(8,128)S(1)}, s32[8]{0:T(128)S(1)}, s32[2,512]{1,0:T(2,128)S(1)}, /*index=5*/s...) while((s32[]{:T(128)}, bf16[8,512,64]{1,2,0:T(8,128)(2,1)}, ...), condition=%wide.region_9.10_spmd.clone, body=%wide.region_6.9_spmd.sunk.clone | while | flops 138935840 | bytes 7109525 | solution.py:105
  174.6 8.7 all-gather.1
  183.3 65.1 %reduce-scatter.9.cloned.1.call-done = f32[256,1024]{1,0:T(8,128)} async-done(((f32[1024,1024]{1,0:T(8,128)}), f32[256,1024]{1,0:T(8,128)}) %reduce-scatter.9.cloned.1.call-update) | async-done | bytes 1048592 | tf_op jit(solution)/shard_map/reduce_scatter | solution.py:190
  251.4 24.4 %all-gather.18.cloned.1.call-done = bf16[656,1024]{1,0:T(8,128)(2,1)} async-done(((bf16[656,128]{1,0:T(8,128)(2,1)}), bf16[656,1024]{1,0:T(8,128)(2,1)}) %all-gather.18.cloned.1.call-update) | async-done | bytes 1343504 | tf_op jit(solution)/shard_map/all_gather | solution.py:224
  275.7 47.5 %all-gather.20.cloned.1.call-done = bf16[1024,1024]{1,0:T(8,128)(2,1)} async-done(((bf16[256,1024]{1,0:T(8,128)(2,1)}), bf16[1024,1024]{1,0:T(8,128)(2,1)}) %all-gather.20.cloned.1.call-update) | async-done | bytes 2097168 | tf_op jit(solution)/shard_map/all_gather | solution.py:182
  328.3 26.4 %all-gather.16.cloned.1.call-done = bf16[1024,2,656]{0,2,1:T(8,128)(2,1)} async-done(((bf16[128,2,656]{0,2,1:T(8,128)(2,1)}), bf16[1024,2,656]{0,2,1:T(8,128)(2,1)}) %all-gather.16.cloned.1.call-update) | async-done | bytes 2686992 | tf_op jit(solution)/shard_map/all_gather | solution.py:223
  354.6 48.2 %all-gather.14.cloned.1.call-done = bf16[1024,1024]{1,0:T(8,128)(2,1)} async-done(((bf16[256,1024]{1,0:T(8,128)(2,1)}), bf16[1024,1024]{1,0:T(8,128)(2,1)}) %all-gather.14.cloned.1.call-update) | async-done | bytes 2097168 | tf_op jit(solution)/shard_map/all_gather | solution.py:178
  402.8 5.5 fusion.60
  408.4 6.5 fusion.74
  427.8 70.2 %reduce-scatter.13.cloned.1.call-done = f32[256,1024]{1,0:T(8,128)} async-done(((f32[1024,1024]{1,0:T(8,128)}), f32[256,1024]{1,0:T(8,128)}) %reduce-scatter.13.cloned.1.call-update) | async-done | bytes 1048592 | tf_op jit(solution)/shard_map/reduce_scatter | solution.py:203
  499.6 78.0 %reduce-scatter.11.cloned.1.call-done = f32[256,1024]{1,0:T(8,128)} async-done(((f32[1024,1024]{1,0:T(8,128)}), f32[256,1024]{1,0:T(8,128)}) %reduce-scatter.11.cloned.1.call-update) | async-done | bytes 1048592 | tf_op jit(solution)/shard_map/reduce_scatter | solution.py:190
  582.7 46.3 %all-gather.22.cloned.1.call-done = bf16[1024,1024]{1,0:T(8,128)(2,1)} async-done(((bf16[256,1024]{1,0:T(8,128)(2,1)}), bf16[1024,1024]{1,0:T(8,128)(2,1)}) %all-gather.22.cloned.1.call-update) | async-done | bytes 2097168 | tf_op jit(solution)/shard_map/all_gather | solution.py:182
  635.5 122.5 %while.33 = (s32[]{:T(128)}, f32[4,1024,64]{1,2,0:T(8,128)}, f32[4,1024,64]{1,2,0:T(8,128)}, f32[8,512,64]{1,2,0:T(8,128)}, s32[8]{0:T(128)S(1)}, /*index=5*/s32...) while((s32[]{:T(128)}, f32[4,1024,64]{1,2,0:T(8,128)}, ...), condition=%wide.region_19.20_spmd.clone, body=%wide.region_17.19_spmd.sunk.clone | while | flops 341016096 | bytes 19289032 | solution.py:167
  783.7 7.2 fusion.58
  795.7 20.2 %reduce-scatter.17.cloned.1.call-done = f32[3,128,256]{1,2,0:T(8,128)} async-done(((f32[3,1024,256]{1,2,0:T(8,128)}), f32[3,128,256]{1,2,0:T(8,128)}) %reduce-scatter.17.cloned.1.call-update) | async-done | bytes 393232 | tf_op jit(solution)/shard_map/reduce_scatter | solution.py:284
  817.8 77.0 %reduce-scatter.15.cloned.1.call-done = f32[256,1024]{1,0:T(8,128)} async-done(((f32[1024,1024]{1,0:T(8,128)}), f32[256,1024]{1,0:T(8,128)}) %reduce-scatter.15.cloned.1.call-update) | async-done | bytes 1048592 | tf_op jit(solution)/shard_map/reduce_scatter | solution.py:203
  898.2 14.0 %all-reduce.6 = (f32[1024]{0:T(1024)S(1)}, f32[1024]{0:T(1024)S(1)}) all-reduce(f32[1024]{0:T(1024)S(1)} %get-tuple-element.431, f32[1024]{0:T(1024)S(1)} %get-tuple-element.429), channel_id=6, replica_groups=mesh['dp'=8,'tensor'=4] {'dp'}, use_global_device_ids=true, to_apply=%region_25.26.clone | all-reduce | flops 2048 | bytes 16384
  912.3 11.6 %all-reduce.7 = (f32[128]{0:T(128)}, f32[128]{0:T(128)}) all-reduce(f32[128]{0:T(128)S(1)} %dynamic-slice.1, f32[128]{0:T(128)S(1)} %dynamic-slice.3), channel_id=1, replica_groups=mesh['dp'=8,'tensor'=4] {'tensor'}, use_global_device_ids=true, to_apply=%region_24.25 | all-reduce | flops 256 | bytes 2048 | tf_op jit(solution)/shard_map/psum | solution.py:281
  925.4 19.0 %reduce-scatter.23.cloned.1.call-done = f32[656,128]{1,0:T(8,128)} async-done(((f32[656,1024]{1,0:T(8,128)}), f32[656,128]{1,0:T(8,128)}) %reduce-scatter.23.cloned.1.call-update) | async-done | bytes 335888 | tf_op jit(solution)/shard_map/reduce_scatter | solution.py:288
  944.4 61.5 %reduce-scatter.21.cloned.1.call-done = f32[128,2,656]{0,2,1:T(8,128)} async-done(((f32[1024,2,656]{0,2,1:T(8,128)}), f32[128,2,656]{0,2,1:T(8,128)}) %reduce-scatter.21.cloned.1.call-update) | async-done | bytes 671760 | tf_op jit(solution)/shard_map/reduce_scatter | solution.py:287
  1005.9 40.0 %reduce-scatter.19.cloned.1.call-done = f32[256,128]{1,0:T(8,128)} async-done(((f32[256,1024]{1,0:T(8,128)}), f32[256,128]{1,0:T(8,128)}) %reduce-scatter.19.cloned.1.call-update) | async-done | bytes 131088 | tf_op jit(solution)/shard_map/reduce_scatter | solution.py:285
  (295 shorter events, 226.5 us)
Async XLA Ops:
  7.2 17.6 %copy-start.20 = (bf16[256,128]{1,0:T(8,128)(2,1)S(1)}, bf16[256,128]{1,0:T(8,128)(2,1)}, u32[]{:S(2)}) copy-start(bf16[256,128]{1,0:T(8,128)(2,1)} %param.19) | copy-start | bytes 196612
  7.2 32.6 %all-gather.12.cloned.1.call-start = ((), (), s32[]{:S(2)}) async-start(), calls=%async_computation.9 | async-start | bytes 1769472 | tf_op jit(solution)/shard_map/all_gather | solution.py:220
  9.0 78.9 %all-gather.10.cloned.1.call-start = ((), (), s32[]{:S(2)}) async-start(), calls=%async_computation.8 | async-start | bytes 2621440 | tf_op jit(solution)/shard_map/all_gather | solution.py:178
  24.1 224.3 %reduce-scatter.9.cloned.1.call-start = ((), (), s32[]{:S(2)}) async-start(), calls=%async_computation.10 | async-start | bytes 5242880 | tf_op jit(solution)/shard_map/reduce_scatter | solution.py:190
  38.2 53.8 %copy-start.16 = (f32[1024,32]{0,1:T(8,128)}, f32[1024,32]{0,1:T(8,128)S(1)}, u32[]{:S(2)}) copy-start(f32[1024,32]{0,1:T(8,128)S(1)} %get-tuple-element.510) | copy-start | bytes 393220
  38.2 53.8 %copy-start.18 = (f32[1024,32]{0,1:T(8,128)}, f32[1024,32]{0,1:T(8,128)S(1)}, u32[]{:S(2)}) copy-start(f32[1024,32]{0,1:T(8,128)S(1)} %get-tuple-element.511) | copy-start | bytes 393220
  172.8 75.7 %copy-start = (bf16[256,1024]{1,0:T(8,128)(2,1)S(1)}, bf16[256,1024]{1,0:T(8,128)(2,1)}, u32[]{:S(2)}) copy-start(bf16[256,1024]{1,0:T(8,128)(2,1)} %param.14) | copy-start | bytes 1572868
  172.8 102.9 %all-gather.18.cloned.1.call-start = ((), (), s32[]{:S(2)}) async-start(), calls=%async_computation.13 | async-start | bytes 1511424 | tf_op jit(solution)/shard_map/all_gather | solution.py:224
  173.4 149.8 %all-gather.20.cloned.1.call-start = ((), (), s32[]{:S(2)}) async-start(), calls=%async_computation.15 | async-start | bytes 2621440 | tf_op jit(solution)/shard_map/all_gather | solution.py:182
  174.0 180.7 %all-gather.16.cloned.1.call-start = ((), (), s32[]{:S(2)}) async-start(), calls=%async_computation.12 | async-start | bytes 3022848 | tf_op jit(solution)/shard_map/all_gather | solution.py:223
  174.5 228.3 %all-gather.14.cloned.1.call-start = ((), (), s32[]{:S(2)}) async-start(), calls=%async_computation.11 | async-start | bytes 2621440 | tf_op jit(solution)/shard_map/all_gather | solution.py:178
  251.2 246.9 %reduce-scatter.13.cloned.1.call-start = ((), (), s32[]{:S(2)}) async-start(), calls=%async_computation.16 | async-start | bytes 5242880 | tf_op jit(solution)/shard_map/reduce_scatter | solution.py:203
  422.4 155.3 %reduce-scatter.11.cloned.1.call-start = ((), (), s32[]{:S(2)}) async-start(), calls=%async_computation.14 | async-start | bytes 5242880 | tf_op jit(solution)/shard_map/reduce_scatter | solution.py:190
  427.8 201.2 %all-gather.22.cloned.1.call-start = ((), (), s32[]{:S(2)}) async-start(), calls=%async_computation.17 | async-start | bytes 2621440 | tf_op jit(solution)/shard_map/all_gather | solution.py:182
  499.6 81.7 %copy-start.7 = (bf16[256,1024]{1,0:T(8,128)(2,1)S(1)}, bf16[256,1024]{1,0:T(8,128)(2,1)}, u32[]{:S(2)}) copy-start(bf16[256,1024]{1,0:T(8,128)(2,1)} %param.23) | copy-start | bytes 1572868
  499.6 129.3 %copy-start.10 = (bf16[256,1024]{1,0:T(8,128)(2,1)S(1)}, bf16[256,1024]{1,0:T(8,128)(2,1)}, u32[]{:S(2)}) copy-start(bf16[256,1024]{1,0:T(8,128)(2,1)} %all_gather.33) | copy-start | bytes 1572868
  582.4 233.5 %reduce-scatter.17.cloned.1.call-start = ((), (), s32[]{:S(2)}) async-start(), calls=%async_computation.19 | async-start | bytes 3538944 | tf_op jit(solution)/shard_map/reduce_scatter | solution.py:284
  770.8 124.1 %reduce-scatter.15.cloned.1.call-start = ((), (), s32[]{:S(2)}) async-start(), calls=%async_computation.18 | async-start | bytes 5242880 | tf_op jit(solution)/shard_map/reduce_scatter | solution.py:203
  776.1 168.4 %reduce-scatter.23.cloned.1.call-start = ((), (), s32[]{:S(2)}) async-start(), calls=%async_computation.22 | async-start | bytes 3022848 | tf_op jit(solution)/shard_map/reduce_scatter | solution.py:288
  782.3 223.6 %reduce-scatter.21.cloned.1.call-start = ((), (), s32[]{:S(2)}) async-start(), calls=%async_computation.21 | async-start | bytes 6045696 | tf_op jit(solution)/shard_map/reduce_scatter | solution.py:287
  790.9 254.9 %reduce-scatter.19.cloned.1.call-start = ((), (), s32[]{:S(2)}) async-start(), calls=%async_computation.20 | async-start | bytes 1179648 | tf_op jit(solution)/shard_map/reduce_scatter | solution.py:285
  794.4 129.6 %copy-start.5 = (f32[256,1024]{1,0:T(8,128)S(1)}, f32[256,1024]{1,0:T(8,128)}, u32[]{:S(2)}) copy-start(f32[256,1024]{1,0:T(8,128)} %copy-done.4) | copy-start | bytes 3145732
  794.4 129.6 %copy-start.8 = (bf16[256,1024]{1,0:T(8,128)(2,1)S(1)}, bf16[256,1024]{1,0:T(8,128)(2,1)}, u32[]{:S(2)}) copy-start(bf16[256,1024]{1,0:T(8,128)(2,1)} %param.23) | copy-start | bytes 1572868
  894.8 29.2 %copy-start.3 = (f32[256,1024]{1,0:T(8,128)S(1)}, f32[256,1024]{1,0:T(8,128)}, u32[]{:S(2)}) copy-start(f32[256,1024]{1,0:T(8,128)} %reduce-scatter.15.cloned.1.call-done) | copy-start | bytes 3145732
  (17 other events, 79.5 us)
Sparse Core Ops, SparseCore 0:
  10.5 29.2 all-gather.11
  42.0 45.9 all-gather.9
  172.9 75.4 reduce-scatter.8
  250.3 25.3 all-gather.17
  277.2 45.9 all-gather.19
  325.1 29.4 all-gather.15
  356.9 45.9 all-gather.13
  422.5 75.4 reduce-scatter.12
  500.3 77.2 reduce-scatter.10
  582.5 46.4 all-gather.21
  770.9 44.9 reduce-scatter.16
  818.0 76.7 reduce-scatter.14
  899.2 45.1 reduce-scatter.22
  948.7 57.1 reduce-scatter.20
  1009.8 35.9 reduce-scatter.18
where the time goes:
time: 1060 us; the launch traced here: 1050 us
  waiting for transfers between devices  675 us (64%)
  matrix products  159 us (15%)
  loops' own time  63.2 us (6%)
  blocking collectives  56.6 us (5%)
  local copies, waits for them, and re-layouts  45.3 us (4%)
  other arithmetic  37.3 us (4%)
  between operations  15.5 us (1%)
    reduce_scatter x2, waiting for transfers between devices, sum_grads(): lax.psum_scatter(row_term(jnp.int32(0), row_count * lax.axis_size('tensor...  147 us
    reduce_scatter x2, waiting for transfers between devices, sum_heads(): lax.psum_scatter(row_term(jnp.int32(0), row_count * lax.axis_size('tensor...  143 us
    all_gather x2, waiting for transfers between devices, spread_rows(): return lax.all_gather(local_rows, 'tensor', axis=0, tiled=True)  96.3 us
    all_gather x2, waiting for transfers between devices, spread_grads(): return lax.all_gather(local_grads, 'tensor', axis=0, tiled=True)  93.8 us
    reduce_scatter x1, waiting for transfers between devices, local(): lax.psum_scatter(d_in, 'dp', scatter_dimension=0, tiled=True)  61.5 us
    reduce_scatter x1, waiting for transfers between devices, local(): lax.psum_scatter(d_out, 'dp', scatter_dimension=1, tiled=True)  40 us
    another operation x1, loops' own time, attend_backward(): lax.scan(one_item, (zero_heads, zero_heads), jnp.arange(head_count * bloc...  31.6 us
    another operation x1, loops' own time, attend_forward(): lax.map(one_item, jnp.arange(head_count * block_count, dtype=jnp.int32))  31.5 us
  transfers between devices with their start and end apart: 15, of which 15 were waited for; matrix products, arithmetic and copies ran while one was open for 5% of the time, Pallas kernels for 0%

commit v1 on v0

--- a/solution.py
+++ b/solution.py
@@ -1,15 +1,1033 @@
+import functools
+
 import jax
 import jax.numpy as jnp
 from jax import lax
+from jax.experimental import pallas as pl
+from jax.experimental.pallas import tpu as pltpu
 from jax.sharding import PartitionSpec as P
 
 HEAD_DIM = 64
 SEQ_GRP = 4
-
-
 rope_base = 160000.0
 norm_eps = 1e-05
 masked_fill = -1e30
+MESH = pl.DeviceIdType.MESH
+BF = jnp.bfloat16
+F32 = jnp.float32
+
+NT = (((1,), (1,)), ((), ()))
+TN = (((0,), (0,)), ((), ()))
+
+
+def place():
+    dp = lax.axis_index("dp")
+    z = lax.axis_index("tensor")
+    c = lax.rem(dp, 2)
+    x = lax.rem(lax.div(dp, 2), 2)
+    y = lax.div(dp, 4)
+    return dp, z, c, x, y
+
+
+def flip(dp, bits, distance):
+    out = dp
+    for b, bit in enumerate(bits):
+        if (distance >> b) & 1:
+            out = out + (1 << b) - (2 << b) * bit
+    return out
+
+
+def remote(src, dst, send, recv, dev):
+    return pltpu.make_async_remote_copy(
+        src_ref=src, dst_ref=dst, send_sem=send, recv_sem=recv, device_id=dev, device_id_type=MESH
+    )
+
+
+def cols(start, size):
+    return pl.ds(pl.multiple_of(start, size), size)
+
+
+def greet(dp, z, bits):
+    c = bits[0]
+    barrier = pltpu.get_barrier_semaphore()
+    peers = [(flip(dp, bits, d), z) for d in range(1, 8)]
+    core = flip(dp, bits, 1)
+    for k in range(1, 4):
+        peers.append((dp, lax.rem(z + k, 4)))
+        peers.append((core, lax.rem(z + k, 4)))
+    for p in peers:
+        pl.semaphore_signal(barrier, inc=1, device_id=p, device_id_type=MESH)
+    pl.semaphore_wait(barrier, len(peers))
+
+
+def norm_rows(v):
+    mean = jnp.mean(v, axis=-1, keepdims=True)
+    centered = v - mean
+    var = jnp.mean(centered * centered, axis=-1, keepdims=True)
+    rstd = lax.rsqrt(var + norm_eps)
+    return centered * rstd, rstd
+
+
+def turn(v, cs, sn):
+    lane = lax.broadcasted_iota(jnp.int32, cs.shape, 1)
+    low_half = lax.rem(lane, HEAD_DIM) < HEAD_DIM // 2
+    parts = []
+    for t in range(v.shape[1] // 128):
+        piece = v[:, t * 128 : (t + 1) * 128]
+        swapped = jnp.where(low_half, pltpu.roll(piece, 96, 1), pltpu.roll(piece, 32, 1))
+        parts.append(piece * cs + swapped * sn)
+    return jnp.concatenate(parts, axis=1)
+
+
+def gain_row(gains, row):
+    return jnp.concatenate([gains[p, row : row + 1, :] for p in range(8)], axis=1)
+
+
+HID = 656
+PACK = 3 * HID + 256
+CUTS = ((0, 560), (560, 560), (1120, 560), (1680, 544))
+
+
+def forward_kernel(
+    tok, wqkv, w4, gains, cs, sn, segc, segr, cot,
+    q_o, k_o, v_o, lse_o, att_o, attn2_o, h1_o, wq_o, G_o, gains_o, cot2_o,
+    tall, km, vT, S, Pm, oT,
+    us, ds, rb, ra, wr_s, wr_r, wc_s, wc_r, g_s, g_r, co_s, co_r, hop_s, hop_r,
+    zu_s, zd_s, zr, pa_s, pb_s, pf_s, pa_r, pb_r, at_s, at_r, lc,
+):
+    dp, z, c, x, y = place()
+    bits = (c, x, y)
+    core = flip(dp, bits, 1)
+    px, py = flip(dp, bits, 2), flip(dp, bits, 4)
+    a = (1 - c) * px + c * py
+    b = (1 - c) * py + c * px
+    chip, chip_a, chip_b = lax.div(dp, 2), lax.div(a, 2), lax.div(b, 2)
+    chip_d = 3 - chip
+    home = lax.div(z, 2)
+    org = c == home
+    zq = lax.rem(z, 2)
+    greet(dp, z, bits)
+
+    def tok_up(k, h):
+        ref = tall.at[z - k, pl.ds(h * 128, 128)]
+        src = tok.at[pl.ds(h * 128, 128)] if k == 0 else ref
+        return remote(src, ref, us.at[k, h], rb.at[k + 1, h], (dp, z + 1))
+
+    def tok_down(k, h):
+        ref = tall.at[z + k, pl.ds(h * 128, 128)]
+        src = tok.at[pl.ds(h * 128, 128)] if k == 0 else ref
+        return remote(src, ref, ds.at[k, h], ra.at[k + 1, h], (dp, z - 1))
+
+    def up_ok(k):
+        return (z >= k) & (z < 3)
+
+    def down_ok(k):
+        return (z + k <= 3) & (z > 0)
+
+    for h in range(2):
+        pl.when(up_ok(0))(lambda h=h: tok_up(0, h).start())
+        pl.when(down_ok(0))(lambda h=h: tok_down(0, h).start())
+
+    for d in range(1, 8):
+        remote(gains, gains_o.at[dp], g_s.at[d], g_r.at[d], (flip(dp, bits, d), z)).start()
+    own_rows = cols(dp * 128, 128)
+    for j, d in enumerate((2, 4, 6)):
+        remote(wqkv, wq_o.at[:, own_rows], wr_s.at[j], wr_r.at[j], (flip(dp, bits, d), z)).start()
+    remote(wqkv, wq_o.at[:, own_rows], wc_s.at[3], wc_r.at[3], (core, z)).start()
+    mine = G_o.at[zq, :, cols(dp * 128, 128)]
+    local_pack = pltpu.make_async_copy(w4, mine, lc.at[0])
+    hop = remote(w4, mine, hop_s, hop_r, (core, z))
+    pl.when(org)(lambda: local_pack.start())
+    pl.when(jnp.logical_not(org))(lambda: hop.start())
+    cot_copy = remote(cot, cot2_o.at[cols(c * 256, 256)], co_s, co_r, (core, z))
+    cot_copy.start()
+
+    gains_o[dp] = gains[...]
+    wq_o[:, own_rows, :] = wqkv[...]
+    tall[z] = tok[...]
+    cot2_o[cols(c * 256, 256), :] = cot[...]
+
+    def piece(q, u, where):
+        r0, n = CUTS[u]
+        return G_o.at[q, pl.ds(r0, n), cols(where * 256, 256)]
+
+    def send_up(q, u):
+        return remote(piece(q, u, chip), piece(q, u, chip), zu_s.at[q, u], zr.at[q, u], (dp, z + 1))
+
+    def send_down(q, u):
+        return remote(piece(q, u, chip), piece(q, u, chip), zd_s.at[q, u], zr.at[q, u], (dp, z - 1))
+
+    def plane_a(q, u):
+        return remote(piece(q, u, chip), piece(q, u, chip), pa_s.at[q, u], pa_r.at[q, u], (a, z))
+
+    def plane_b(q, u):
+        return remote(piece(q, u, chip), piece(q, u, chip), pb_s.at[q, u], pb_r.at[q, 0, u], (b, z))
+
+    def plane_f(q, u):
+        return remote(piece(q, u, chip_a), piece(q, u, chip_a), pf_s.at[q, u], pb_r.at[q, 1, u], (b, z))
+
+    def goes_up(q):
+        return (z >= 2 * c + q) & (z < 3)
+
+    def goes_down(q):
+        return (z <= 2 * c + q) & (z > 0)
+
+    def spread(q, u):
+        plane_a(q, u).start()
+        plane_b(q, u).start()
+
+    def arrive(q, u):
+        remote(piece(q, u, chip), piece(q, u, chip), zu_s.at[q, u], zr.at[q, u], (core, z)).wait_recv()
+
+    def onward(q, u):
+        pl.when(goes_up(q))(lambda: send_up(q, u).start())
+        pl.when(goes_down(q))(lambda: send_down(q, u).start())
+
+    def across(q, u):
+        remote(piece(q, u, chip_a), piece(q, u, chip_a), pa_s.at[q, u], pa_r.at[q, u], (a, z)).wait_recv()
+        plane_f(q, u).start()
+
+    near = (1 - c) * lax.div(z + 2, 3) + c * lax.div(z, 3)
+    far = 1 - near
+
+    for d in range(1, 8):
+        p = flip(dp, bits, d)
+        remote(gains, gains_o.at[p], g_s.at[d], g_r.at[d], (p, z)).wait_recv()
+
+    @pl.when(org)
+    def _():
+        local_pack.wait()
+        remote(w4, G_o.at[zq, :, cols(core * 128, 128)], hop_s, hop_r, (core, z)).wait_recv()
+        for u in range(4):
+            spread(near, u)
+
+    for j, d in enumerate((2, 4, 6)):
+        p = flip(dp, bits, d)
+        rows = wq_o.at[:, cols(p * 128, 128)]
+        remote(wqkv, rows, wr_s.at[j], wr_r.at[j], (p, z)).wait_recv()
+        remote(rows, rows, wc_s.at[j], wc_r.at[j], (core, z)).start()
+    for j, d in enumerate((3, 5, 7, 1)):
+        p = flip(dp, bits, d)
+        remote(wqkv, wq_o.at[:, cols(p * 128, 128)], wc_s.at[j], wc_r.at[j], (core, z)).wait_recv()
+
+    gain = gain_row(gains_o, 0)
+
+    def project(s):
+        base = s * 256
+
+        @pl.loop(0, 8)
+        def _(r):
+            xhat, _r = norm_rows(tall[s, pl.ds(pl.multiple_of(r * 32, 32), 32), :].astype(F32))
+            h1_o[pl.ds(pl.multiple_of(base + r * 32, 32), 32), :] = (xhat * gain).astype(BF)
+
+        rows = pl.ds(pl.multiple_of(base, 256), 256)
+        hb = h1_o[rows, :]
+        cb, sb = cs[rows, :], sn[rows, :]
+        for p, out in enumerate((q_o, k_o, v_o)):
+            r = jnp.dot(hb, wq_o[p], preferred_element_type=F32)
+            if p < 2:
+                r = turn(r, cb, sb)
+            if p == 0:
+                r = r * (HEAD_DIM**-0.5)
+            out[rows, :] = r.astype(BF)
+
+    project(z)
+    for k in range(1, 4):
+        below, above = z - k >= 0, z + k <= 3
+        for h in range(2):
+
+            @pl.when(below)
+            def _(k=k, h=h):
+                ref = tall.at[z - k, pl.ds(h * 128, 128)]
+                remote(ref, ref, us.at[k, h], rb.at[k, h], (core, z)).wait_recv()
+                if k < 3:
+                    pl.when(up_ok(k))(lambda: tok_up(k, h).start())
+
+            @pl.when(above)
+            def _(k=k, h=h):
+                ref = tall.at[z + k, pl.ds(h * 128, 128)]
+                remote(ref, ref, ds.at[k, h], ra.at[k, h], (core, z)).wait_recv()
+                if k < 3:
+                    pl.when(down_ok(k))(lambda: tok_down(k, h).start())
+
+        @pl.when(org & (z + 1 == k))
+        def _():
+            for u in range(4):
+                send_up(near, u).start()
+
+        @pl.when(org & (4 - z == k))
+        def _():
+            for u in range(4):
+                send_down(near, u).start()
+
+        if k == 1:
+
+            @pl.when(org)
+            def _():
+                for u in range(4):
+                    across(near, u)
+
+        @pl.loop(0, 2)
+        def _(t, k=k):
+            s = z - k + 2 * k * t
+            pl.when((s >= 0) & (s <= 3))(lambda: project(s))
+
+    lane = lax.broadcasted_iota(jnp.int32, (1024, 256), 1)
+    for h in range(4):
+        km[h] = jnp.where(lax.div(lane, HEAD_DIM) == h, k_o[...], jnp.zeros((), BF))
+    for s in range(4):
+        vT[:, s * 256 : (s + 1) * 256] = v_o[s * 256 : (s + 1) * 256, :].T
+
+    def attend(i):
+        rows = pl.ds(pl.multiple_of(i * 256, 256), 256)
+        qb = q_o[rows, :]
+        seg_q = segr[0:1, rows]
+
+        @pl.loop(0, 4)
+        def _(h):
+            top = jnp.full((8, 256), -jnp.inf, F32)
+            for kc in range(4):
+                keys = pl.ds(kc * 256, 256)
+                s = lax.dot_general(km[h, keys, :], qb, NT, preferred_element_type=F32)
+                seg_k = segc[keys, :]
+                same = jnp.concatenate([seg_k, seg_k], axis=1) == seg_q
+                s = jnp.where(same, s, masked_fill)
+                S[keys, :] = s
+                top = jnp.maximum(top, jnp.max(s.reshape(32, 8, 256), axis=0))
+            row_top = jnp.max(top, axis=0, keepdims=True)
+            total = jnp.zeros((8, 256), F32)
+            for kc in range(4):
+                keys = pl.ds(kc * 256, 256)
+                p = jnp.exp(S[keys, :] - row_top)
+                total = total + jnp.sum(p.reshape(32, 8, 256), axis=0)
+                Pm[keys, :] = p.astype(BF)
+            row_total = jnp.sum(total, axis=0, keepdims=True)
+            hr = pl.ds(pl.multiple_of(h * HEAD_DIM, HEAD_DIM), HEAD_DIM)
+            o = jnp.dot(vT[hr, :], Pm[...], preferred_element_type=F32)
+            oT[hr, :] = o * (1.0 / row_total)
+            lse_o[h, i] = jnp.broadcast_to(row_top + jnp.log(row_total), (8, 256))
+
+        att_o[rows, :] = oT[...].T.astype(BF)
+
+    def att_slot(src_core, q):
+        return attn2_o.at[cols(src_core * 256, 256), cols(q * 256, 256)]
+
+    def att_copy(n, i):
+        rows = pl.ds(pl.multiple_of(i * 256, 256), 256)
+        return remote(
+            att_o.at[rows, :], att_slot(c, zq), at_s.at[n], at_r.at[c, zq], (2 * chip + home, i)
+        )
+
+    late1 = jnp.where(org, far, near)
+
+    def stage(q, u):
+        arrive(q, u)
+        onward(q, u)
+        spread(q, u)
+
+    order = [lax.rem(z + 1 + n, 4) for n in range(4)]
+    for n in range(4):
+        i = order[n]
+        attend(i)
+        if n < 3:
+            att_copy(n, i).start()
+        else:
+            pl.when(jnp.logical_not(org))(lambda: att_copy(3, i).start())
+
+            @pl.when(org)
+            def _():
+                attn2_o[cols(c * 256, 256), cols(zq * 256, 256)] = att_o[
+                    pl.ds(pl.multiple_of(z * 256, 256), 256), :
+                ]
+
+        if n == 1:
+            stage(late1, 0)
+            stage(late1, 1)
+        if n == 2:
+            stage(late1, 2)
+            across(late1, 0)
+    stage(late1, 3)
+    for u in range(1, 4):
+        across(late1, u)
+
+    @pl.when(jnp.logical_not(org))
+    def _():
+        for u in range(4):
+            stage(far, u)
+        for u in range(4):
+            across(far, u)
+
+    for src in range(2):
+        for q in range(2):
+            mine_too = (c == src) & (z == 2 * c + q)
+
+            @pl.when(jnp.logical_not(mine_too))
+            def _(src=src, q=q):
+                slot = att_slot(src, q)
+                remote(slot, slot, at_s.at[0], at_r.at[src, q], (core, z)).wait_recv()
+
+    remote(cot, cot2_o.at[cols((1 - c) * 256, 256)], co_s, co_r, (core, z)).wait_recv()
+    for q in range(2):
+        for u in range(4):
+            for w, where in enumerate((chip_b, chip_d)):
+                ref = piece(q, u, where)
+                remote(ref, ref, pb_s.at[q, u], pb_r.at[q, w, u], (b, z)).wait_recv()
+    for k in range(3):
+        for h in range(2):
+            pl.when(up_ok(k))(lambda k=k, h=h: tok_up(k, h).wait_send())
+            pl.when(down_ok(k))(lambda k=k, h=h: tok_down(k, h).wait_send())
+    for d in range(1, 8):
+        remote(gains, gains_o.at[dp], g_s.at[d], g_r.at[d], (core, z)).wait_send()
+    for j in range(3):
+        remote(wqkv, wq_o.at[:, own_rows], wr_s.at[j], wr_r.at[j], (core, z)).wait_send()
+    for j in range(4):
+        remote(wqkv, wq_o.at[:, own_rows], wc_s.at[j], wc_r.at[j], (core, z)).wait_send()
+    pl.when(jnp.logical_not(org))(lambda: hop.wait_send())
+    cot_copy.wait_send()
+    for q in range(2):
+        for u in range(4):
+            pl.when(goes_up(q))(lambda q=q, u=u: send_up(q, u).wait_send())
+            pl.when(goes_down(q))(lambda q=q, u=u: send_down(q, u).wait_send())
+            plane_a(q, u).wait_send()
+            plane_b(q, u).wait_send()
+            plane_f(q, u).wait_send()
+    for n in range(3):
+        att_copy(n, order[n]).wait_send()
+    pl.when(jnp.logical_not(org))(lambda: att_copy(3, order[3]).wait_send())
+
+
+def run_forward(tok, wqkv, w4, gains, cs, sn, segc, segr, cot):
+    V = pl.BlockSpec(memory_space=pltpu.VMEM)
+    A = pl.BlockSpec(memory_space=pl.ANY)
+    dma = pltpu.SemaphoreType.DMA
+    s = jax.ShapeDtypeStruct
+    return pl.pallas_call(
+        forward_kernel,
+        out_shape=(
+            s((1024, 256), BF), s((1024, 256), BF), s((1024, 256), BF), s((4, 4, 8, 256), F32),
+            s((1024, 256), BF), s((512, 512), BF), s((1024, 1024), BF), s((3, 1024, 256), BF),
+            s((2, PACK, 1024), BF), s((8, 8, 128), F32), s((512, 1024), BF),
+        ),
+        in_specs=[V, V, A, V, V, V, V, V, V],
+        out_specs=[V] * 8 + [A, V, V],
+        scratch_shapes=[
+            pltpu.VMEM((4, 256, 1024), BF), pltpu.VMEM((4, 1024, 256), BF), pltpu.VMEM((256, 1024), BF),
+            pltpu.VMEM((1024, 256), F32), pltpu.VMEM((1024, 256), BF), pltpu.VMEM((256, 256), F32),
+            dma((4, 2)), dma((4, 2)), dma((4, 2)), dma((4, 2)),
+            dma((3,)), dma((3,)), dma((4,)), dma((4,)), dma((8,)), dma((8,)), dma, dma, dma, dma,
+            dma((2, 4)), dma((2, 4)), dma((2, 4)), dma((2, 4)), dma((2, 4)), dma((2, 4)),
+            dma((2, 4)), dma((2, 2, 4)), dma((4,)), dma((2, 2)), dma((1,)),
+        ],
+        compiler_params=pltpu.CompilerParams(
+            collective_id=1, has_side_effects=True, vmem_limit_bytes=56 << 20
+        ),
+        name="forward_attention",
+    )(tok, wqkv, w4, gains, cs, sn, segc, segr, cot)
+
+
+def layout(lengths, seq_order, group_rows):
+    seq_total = seq_order.shape[0]
+    first_seq = lax.axis_index("dp") * SEQ_GRP
+    chosen = lax.dynamic_slice_in_dim(seq_order, first_seq, SEQ_GRP)
+    matched = chosen[:, None] == jnp.arange(seq_total, dtype=jnp.int32)[None, :]
+    dealt_lengths = jnp.sum(jnp.where(matched, lengths[None, :], 0), axis=1)
+    seq_ends = jnp.cumsum(dealt_lengths)
+    row_index = jnp.arange(group_rows, dtype=jnp.int32)
+    passed = row_index[:, None] >= seq_ends[None, :]
+    segment = jnp.sum(passed.astype(jnp.int32), axis=1)
+    row_start = jnp.sum(jnp.where(passed, dealt_lengths[None, :], 0), axis=1)
+    return (segment, (row_index - row_start).astype(jnp.float32))
+
+
+def prepare(lengths, seq_order, gain_attn, w_attn_out, gain_mlp, w_in, w_mlp_out):
+    segment, position = layout(lengths, seq_order, 1024)
+    half = HEAD_DIM // 2
+    index_range = jnp.arange(half, dtype=F32)
+    frequency = rope_base ** (-2.0 * index_range / HEAD_DIM)
+    angles = position[:, None] * frequency[None, :]
+    cosine, sine = jnp.cos(angles), jnp.sin(angles)
+    cs = jnp.concatenate([cosine] * 4, axis=1)
+    sn = jnp.concatenate([-sine, sine, -sine, sine], axis=1)
+    seg = segment.astype(F32)
+    segc = jnp.broadcast_to(seg[:, None], (1024, 128))
+    segr = jnp.broadcast_to(seg[None, :], (8, 1024))
+    w4 = jnp.concatenate(
+        [w_in.transpose(1, 2, 0).reshape(2 * HID, 128), w_mlp_out, w_attn_out], axis=0
+    )
+    gains = jnp.concatenate(
+        [gain_attn[None, :].astype(F32), gain_mlp[None, :].astype(F32), jnp.zeros((6, 128), F32)], axis=0
+    )
+    return w4, gains, cs, sn, segc, segr
+
+
+ROWS = ((0, HID), (HID, HID), (2 * HID, HID), (3 * HID, 256))
+UNITS = ((0, 2), (0, 0), (0, 1), (1, 2), (1, 0), (1, 1), (0, 3), (1, 3))
+INV_SQRT2 = 0.7071067811865476
+INV_SQRT_2PI = 0.3989422804014327
+
+
+def backward_kernel(
+    q, k, v, lse, att, attn2, h1, wq, G_in, gains, cot2, tok, cs, sn, segc, segr, wqkv, w4,
+    out_o, dtok_o, dwq_o, dw4_o, dg_o,
+    G, X1, h2a, yr, dr, ur, acc, hidT, daT, duT, dya, dX1, dxo, dsend, datt, delta,
+    dq, dk, dv, dqkvT, Hs, Hi, Hx, Rb, Ra, Z, give, Wp, Wc, Wb, Wa, gz,
+    ld, y_s, y_r, h_s, h_r, d_s, d_r, u_s, u_r, e_s, e_r, t_s, t_r,
+    b_s, b_r, a_s, a_r, zu_s, zd_s, z_r, fin_s, fin_r,
+    hu_s, hd_s, hi_r, hx_r, wc_s, wc_r, wb_s, wb_r, wa_s, wa_r, gz_s, gz_r,
+):
+    dp, z, c, x, y = place()
+    bits = (c, x, y)
+    core = flip(dp, bits, 1)
+    px, py = flip(dp, bits, 2), flip(dp, bits, 4)
+    a = (1 - c) * px + c * py
+    b = (1 - c) * py + c * px
+    chip, chip_a, chip_b = lax.div(dp, 2), lax.div(a, 2), lax.div(b, 2)
+    chip_d = 3 - chip
+    home = lax.div(z, 2)
+    org = c == home
+    zq = lax.rem(z, 2)
+    loads = []
+    for qi in range(2):
+        for n, (r0, m) in enumerate(ROWS):
+            cp = pltpu.make_async_copy(G_in.at[qi, pl.ds(r0, m)], G.at[qi, pl.ds(r0, m)], ld.at[qi, n])
+            cp.start()
+            loads.append(cp)
+    greet(dp, z, bits)
+    own = cols(c * 256, 256)
+    other = cols((1 - c) * 256, 256)
+    gain1, gain2 = gain_row(gains, 0), gain_row(gains, 1)
+
+    def w_rows(qi, m):
+        r0, n = ROWS[m]
+        return pl.ds(r0, n)
+
+    loads[3].wait()
+    loads[7].wait()
+
+    def out_proj(rows):
+        return sum(
+            jnp.dot(
+                attn2[rows, qi * 256 : (qi + 1) * 256], G[qi, w_rows(qi, 3), :], preferred_element_type=F32
+            )
+            for qi in range(2)
+        )
+
+    acc[...] = out_proj(other)
+    y_copy = remote(acc, yr, y_s, y_r, (core, z))
+    y_copy.start()
+    X1[...] = tok[...].astype(F32) + out_proj(own)
+    y_copy.wait()
+
+    def chunk(r):
+        return pl.ds(pl.multiple_of(r * 32, 32), 32)
+
+    def own_chunk(r):
+        return pl.ds(pl.multiple_of(c * 256 + r * 32, 32), 32)
+
+    @pl.loop(0, 8)
+    def _(r):
+        x1 = X1[chunk(r), :] + yr[chunk(r), :]
+        X1[chunk(r), :] = x1
+        xhat, _r = norm_rows(x1)
+        h2a[own_chunk(r), :] = (xhat * gain2).astype(BF)
+
+    h_copy = remote(h2a.at[own], h2a.at[own], h_s, h_r, (core, z))
+    h_copy.start()
+    for n in (0, 1, 2, 4, 5, 6):
+        loads[n].wait()
+    h_copy.wait()
+
+    TILES = ((0, 224), (224, 224), (448, 208))
+    for r0, n in TILES:
+
+        @pl.loop(0, 2)
+        def _(qi, r0=r0, n=n):
+            h2 = h2a[...]
+            act = lax.dot_general(G[qi, pl.ds(r0, n), :], h2, NT, preferred_element_type=F32)
+            up = lax.dot_general(G[qi, pl.ds(HID + r0, n), :], h2, NT, preferred_element_type=F32)
+            dh = lax.dot_general(G[qi, pl.ds(2 * HID + r0, n), :], cot2[...], NT, preferred_element_type=F32)
+            Phi = 0.5 + 0.5 * lax.erf(act * INV_SQRT2)
+            phi = jnp.exp(-0.5 * act * act) * INV_SQRT_2PI
+            gel = act * Phi
+            rr = pl.ds(r0, n)
+            hidT[qi, rr, :] = (gel * up).astype(BF)
+            daT[qi, rr, :] = (dh * up * (Phi + act * phi)).astype(BF)
+            duT[qi, rr, :] = (dh * gel).astype(BF)
+
+    def tn(lhs, rhs):
+        return lax.dot_general(lhs, rhs, TN, preferred_element_type=F32)
+
+    def d_norm(dst, rows):
+        for half in range(2):
+            hc = slice(half * 512, half * 512 + 512)
+            dst[:, hc] = sum(
+                tn(daT[qi, :, rows], G[qi, w_rows(qi, 0), hc]) + tn(duT[qi, :, rows], G[qi, w_rows(qi, 1), hc])
+                for qi in range(2)
+            )
+
+    def mlp_out(dst, rows, plus=None):
+        for half in range(2):
+            hc = slice(half * 512, half * 512 + 512)
+            r = sum(tn(hidT[qi, :, rows], G[qi, w_rows(qi, 2), hc]) for qi in range(2))
+            dst[:, hc] = r if plus is None else r + plus[:, hc]
+
+    def grads(qi, m):
+        lhs, rhs = ((daT, h2a), (duT, h2a), (hidT, cot2))[m]
+
+        @pl.loop(0, 4)
+        def _(t):
+            tc = cols(t * 256, 256)
+            G[qi, w_rows(qi, m), tc] = jnp.dot(lhs[qi], rhs[:, tc], preferred_element_type=F32).astype(BF)
+
+    def part(qi, m, where):
+        return G.at[qi, w_rows(qi, m), cols(where * 256, 256)]
+
+    def unit_b(e, slot):
+        qi, m = UNITS[e]
+        where = chip_b if slot == 0 else chip_d
+        return remote(part(qi, m, where), Rb.at[slot, qi, w_rows(qi, m)], b_s.at[slot, e], b_r.at[slot, e], (b, z))
+
+    def unit_a(e):
+        qi, m = UNITS[e]
+        return remote(part(qi, m, chip_a), Ra.at[qi, w_rows(qi, m)], a_s.at[e], a_r.at[e], (a, z))
+
+    def send_b(e):
+        unit_b(e, 1).start()
+        unit_b(e, 0).start()
+
+    def stage1(e):
+        qi, m = UNITS[e]
+        unit_b(e, 1).wait_recv()
+        ref = part(qi, m, chip_a)
+        ref[...] = (ref[...].astype(F32) + Rb[1, qi, w_rows(qi, m), :].astype(F32)).astype(BF)
+        unit_a(e).start()
+
+    def line_up(e, slot):
+        qi, m = UNITS[e]
+        return remote(part(qi, m, chip), Z.at[slot, w_rows(qi, m)], zu_s.at[e], z_r.at[slot, e], (dp, z + 1))
+
+    def line_down(e):
+        qi, m = UNITS[e]
+        return remote(part(qi, m, chip), Z.at[qi, w_rows(qi, m)], zd_s.at[e], z_r.at[qi, e], (dp, z - 1))
+
+    def target(e):
+        return 2 * c + UNITS[e][0]
+
+    def inward(e):
+        qi = UNITS[e][0]
+        t = target(e)
+        pl.when(z > t)(lambda: line_down(e).start())
+        pl.when(z + 1 == t)(lambda: line_up(e, 2).start())
+        pl.when(z + 1 < t)(lambda: line_up(e, qi).start())
+
+    def stage2(e):
+        qi, m = UNITS[e]
+        unit_b(e, 0).wait_recv()
+        unit_a(e).wait_recv()
+        rows = w_rows(qi, m)
+        ref = part(qi, m, chip)
+        ref[...] = (ref[...].astype(F32) + Rb[0, qi, rows, :].astype(F32) + Ra[qi, rows, :].astype(F32)).astype(BF)
+        t = target(e)
+        pl.when(((z == 3) & (z > t)) | ((z == 0) & (z < t)))(lambda: inward(e))
+
+    def line_wait(e, slot):
+        qi, m = UNITS[e]
+        ref = Z.at[slot, w_rows(qi, m)]
+        remote(ref, ref, zu_s.at[e], z_r.at[slot, e], (core, z)).wait_recv()
+
+    def stage3(e, depth):
+        qi, m = UNITS[e]
+        t = target(e)
+        mid = ((z > t) & (z == 3 - depth)) | ((z < t) & (z == depth))
+
+        @pl.when(mid)
+        def _():
+            line_wait(e, qi)
+            ref = part(qi, m, chip)
+            ref[...] = (ref[...].astype(F32) + Z[qi, w_rows(qi, m), :].astype(F32)).astype(BF)
+            inward(e)
+
+
+    def stage4(e):
+        qi, m = UNITS[e]
+        t = target(e)
+        rows = w_rows(qi, m)
+
+        @pl.when(z == t)
+        def _():
+            dst = dw4_o.at[rows]
+            gift = give.at[rows]
+            dst[...] = G[qi, rows, cols(dp * 128, 128)].astype(F32)
+            gift[...] = G[qi, rows, cols(core * 128, 128)].astype(F32)
+
+            def take(slot):
+                line_wait(e, slot)
+                for who, ref in ((c, dst), (1 - c, gift)):
+                    ref[...] = ref[...] + Z[slot, rows, cols(who * 128, 128)].astype(F32)
+
+            pl.when(z < 3)(lambda: take(qi))
+            pl.when(z > 0)(lambda: take(2))
+            remote(gift, dst, fin_s.at[m], fin_r.at[m], (core, z)).start()
+
+    d_norm(acc, other)
+    d_copy = remote(acc, dr, d_s, d_r, (core, z))
+    d_copy.start()
+    mlp_out(dxo, other)
+    u_copy = remote(dxo, ur, u_s, u_r, (core, z))
+    u_copy.start()
+    d_norm(dX1, own)
+    mlp_out(dtok_o, own, X1)
+    for e in range(2):
+        grads(*UNITS[e])
+        send_b(e)
+    d_copy.wait()
+
+    @pl.loop(0, 8)
+    def _(r):
+        dh2 = dX1[chunk(r), :] + dr[chunk(r), :]
+        xhat, rstd = norm_rows(X1[chunk(r), :])
+        e2 = dh2 * gain2
+        m1 = jnp.mean(e2, axis=-1, keepdims=True)
+        m2 = jnp.mean(e2 * xhat, axis=-1, keepdims=True)
+        dx = cot2[own_chunk(r), :].astype(F32) + rstd * (e2 - m1 - xhat * m2)
+        dX1[chunk(r), :] = dx
+        dya[own_chunk(r), :] = dx.astype(BF)
+
+    e_copy = remote(dya.at[own], dya.at[own], e_s, e_r, (core, z))
+    e_copy.start()
+    grads(*UNITS[2])
+    send_b(2)
+    e_copy.wait()
+    for qi in range(2):
+        dsend[qi] = lax.dot_general(dya[...], G[qi, w_rows(qi, 3), :], NT, preferred_element_type=F32).astype(BF)
+
+    def att_back(c0, qi):
+        dst = datt.at[cols(z * 256, 256)]
+        return remote(
+            dsend.at[qi, pl.ds(c0 * 256, 256)], dst, t_s.at[c0, qi], t_r.at[z], (2 * chip + c0, 2 * c + qi)
+        )
+
+    def is_self(c0, qi):
+        return (c == c0) & (z == 2 * c + qi)
+
+    for c0 in range(2):
+        for qi in range(2):
+            pl.when(jnp.logical_not(is_self(c0, qi)))(lambda c0=c0, qi=qi: att_back(c0, qi).start())
+
+            @pl.when(is_self(c0, qi))
+            def _(c0=c0, qi=qi):
+                datt[cols(z * 256, 256), :] = dsend[qi, c0 * 256 : (c0 + 1) * 256, :]
+
+    for e in range(3, 6):
+        grads(*UNITS[e])
+        send_b(e)
+    for e in (6, 7):
+        qi = UNITS[e][0]
+
+        @pl.loop(0, 4)
+        def _(t, qi=qi):
+            tc = cols(t * 256, 256)
+            G[qi, w_rows(qi, 3), tc] = tn(attn2[:, qi * 256 : (qi + 1) * 256], dya[:, tc]).astype(BF)
+
+        send_b(e)
+    u_copy.wait()
+    out_o[...] = (dtok_o[...] + ur[...]).astype(BF)
+    dq[...] = jnp.zeros_like(dq)
+    dk[...] = jnp.zeros_like(dk)
+    dv[...] = jnp.zeros_like(dv)
+    for i in range(4):
+
+        @pl.when(jnp.logical_not(org & (z == i)))
+        def _(i=i):
+            ref = datt.at[pl.ds(i * 256, 256)]
+            remote(ref, ref, t_s.at[0, 0], t_r.at[i], (core, z)).wait_recv()
+
+    @pl.loop(0, 4)
+    def _(i):
+        rows = pl.ds(pl.multiple_of(i * 256, 256), 256)
+        t = (datt[rows, :].astype(F32) * att[rows, :].astype(F32)).T
+        for h in range(4):
+            s = jnp.sum(t[h * 64 : (h + 1) * 64, :], axis=0, keepdims=True)
+            delta[h, i] = jnp.broadcast_to(s, (8, 256))
+
+    head_of = lax.div(lax.broadcasted_iota(jnp.int32, (256, 256), 1), HEAD_DIM)
+
+    def block_order(l):
+        return jnp.minimum(l, 1) * (lax.rem(l + 1, 3) + 1)
+
+    def pair(i, j):
+        ri = pl.ds(pl.multiple_of(i * 256, 256), 256)
+        rj = pl.ds(pl.multiple_of(j * 256, 256), 256)
+
+        @pl.loop(0, 4)
+        def _(h):
+            mine = head_of == h
+            kj, vj = k[rj, :], v[rj, :]
+            qh = jnp.where(mine, q[ri, :], jnp.zeros((), BF))
+            dah = jnp.where(mine, datt[ri, :], jnp.zeros((), BF))
+            s = lax.dot_general(kj, qh, NT, preferred_element_type=F32)
+            seg_k = segc[rj, :]
+            same = jnp.concatenate([seg_k, seg_k], axis=1) == segr[0:1, ri]
+            p = jnp.exp(jnp.where(same, s, masked_fill) - lse[h, i, 0:1, :])
+            dp_ = lax.dot_general(vj, dah, NT, preferred_element_type=F32)
+            dsc = (p * (dp_ - delta[h, i, 0:1, :])).astype(BF)
+            dv[rj, :] = dv[rj, :] + jnp.dot(p.astype(BF), dah, preferred_element_type=F32)
+            dk[rj, :] = dk[rj, :] + jnp.dot(dsc, qh, preferred_element_type=F32)
+            dq[ri, :] = dq[ri, :] + jnp.where(mine, tn(dsc, kj), 0.0)
+
+    def h_up(i, last):
+        if last:
+            return remote(Hs.at[i], Hx, hu_s.at[i], hx_r, (dp, z + 1))
+        return remote(Hs.at[i], Hi.at[i], hu_s.at[i], hi_r.at[i], (dp, z + 1))
+
+    def h_down(i):
+        return remote(Hs.at[i], Hi.at[i], hd_s.at[i], hi_r.at[i], (dp, z - 1))
+
+    def h_inward(i, act):
+        pl.when(z > i)(lambda: act(h_down(i)))
+        pl.when(z + 1 == i)(lambda: act(h_up(i, True)))
+        pl.when(z + 1 < i)(lambda: act(h_up(i, False)))
+
+    def begin(cp):
+        cp.start()
+
+    def h_wait(i):
+        remote(Hi.at[i], Hi.at[i], hd_s.at[i], hi_r.at[i], (core, z)).wait_recv()
+
+    def h_mid(i, depth):
+        mid = ((z > i) & (z == 3 - depth)) | ((z < i) & (z == depth))
+
+        @pl.when(mid)
+        def _():
+            h_wait(i)
+            Hs[i] = (Hs[i].astype(F32) + Hi[i].astype(F32)).astype(BF)
+            h_inward(i, begin)
+
+    def finish(i):
+        rows = pl.ds(pl.multiple_of(i * 256, 256), 256)
+        cb, sb = cs[rows, :], -sn[rows, :]
+        low = (
+            turn(dq[rows, :] * (HEAD_DIM**-0.5), cb, sb).astype(BF),
+            turn(dk[rows, :], cb, sb).astype(BF),
+            dv[rows, :].astype(BF),
+        )
+        for p in range(3):
+            dqkvT[p * 256 : (p + 1) * 256, rows] = low[p].T
+        for half in range(2):
+            hc = slice(half * 512, half * 512 + 512)
+            dh = sum(
+                lax.dot_general(low[p], wq[p, hc, :], NT, preferred_element_type=F32) for p in range(3)
+            )
+            Hs[i, :, hc] = dh.astype(BF)
+
+            @pl.when(z == i)
+            def _(dh=dh, hc=hc):
+                acc[:, hc] = dh
+
+        pl.when(((z == 3) & (z > i)) | ((z == 0) & (z < i)))(lambda: h_inward(i, begin))
+
+    def tick(t):
+        if t < 8:
+            stage1(t)
+        if 0 <= t - 1 < 8:
+            stage2(t - 1)
+        if 0 <= t - 2 < 8:
+            stage3(t - 2, 1)
+        if 0 <= t - 3 < 8:
+            stage3(t - 3, 2)
+        if 0 <= t - 4 < 8:
+            stage4(t - 4)
+
+    slots = {2: [lambda: tick(0)], 6: [lambda: tick(1)], 9: [lambda: tick(2)], 13: [lambda: tick(3)],
+             11: [lambda: h_mid(0, 1)], 14: [lambda: h_mid(0, 2), lambda: h_mid(3, 1)]}
+
+    @pl.loop(0, 16)
+    def _(n):
+        def past(v):
+            return lax.div(n + 16 - v, 16)
+
+        ph = past(7) + past(12) + past(15)
+        t = n - 7 * past(7) - 5 * past(12) - 3 * past(15)
+        left = 4 - ph
+        over = lax.div(t, left)
+        li = ph + over * (t - left + 1)
+        lj = ph + (1 - over) * t
+        pair(block_order(li), block_order(lj))
+        pl.when((n == 6) | (n == 11) | (n == 14) | (n == 15))(lambda: finish(block_order(ph)))
+        for s, ops in slots.items():
+
+            @pl.when(n == s)
+            def _(ops=ops):
+                for op in ops:
+                    op()
+
+    @pl.loop(0, 4)
+    def _(t):
+        tc = cols(t * 256, 256)
+        Wp[:, tc] = jnp.dot(dqkvT[...], h1[:, tc], preferred_element_type=F32).astype(BF)
+
+    def core_copy(w):
+        return remote(
+            Wp.at[:, cols(w * 256 + (1 - c) * 128, 128)], Wc.at[w], wc_s.at[w], wc_r.at[w], (core, z)
+        )
+
+    for w in range(4):
+        core_copy(w).start()
+    h_mid(3, 2)
+    h_mid(1, 1)
+    h_mid(2, 1)
+
+    def both(w):
+        Wc[w] = (Wc[w].astype(F32) + Wp[:, cols(w * 256 + c * 128, 128)].astype(F32)).astype(BF)
+
+    for w in range(4):
+        core_copy(w).wait_recv()
+    both(chip_d)
+    both(chip_b)
+    wb_copy = [
+        remote(Wc.at[where], Wb.at[slot], wb_s.at[slot], wb_r.at[slot], (b, z))
+        for slot, where in ((0, chip_b), (1, chip_d))
+    ]
+    wb_copy[1].start()
+    wb_copy[0].start()
+    both(chip_a)
+    both(chip)
+    wa_copy = remote(Wc.at[chip_a], Wa, wa_s, wa_r, (a, z))
+    tick(4)
+    wb_copy[1].wait_recv()
+    Wc[chip_a] = (Wc[chip_a].astype(F32) + Wb[1].astype(F32)).astype(BF)
+    wa_copy.start()
+    tick(5)
+
+    pl.when(z < 3)(lambda: h_wait(z))
+    pl.when(z > 0)(lambda: remote(Hx, Hx, hu_s.at[0], hx_r, (core, z)).wait_recv())
+    has_above, has_below = z < 3, z > 0
+
+    @pl.when(has_above)
+    def _():
+        acc[...] = acc[...] + Hi[z].astype(F32)
+
+    @pl.when(has_below)
+    def _():
+        acc[...] = acc[...] + Hx[...].astype(F32)
+
+    @pl.loop(0, 8)
+    def _(r):
+        xhat, rstd = norm_rows(tok[chunk(r), :].astype(F32))
+        e1 = acc[chunk(r), :] * gain1
+        m1 = jnp.mean(e1, axis=-1, keepdims=True)
+        m2 = jnp.mean(e1 * xhat, axis=-1, keepdims=True)
+        dtok_o[chunk(r), :] = dX1[chunk(r), :] + rstd * (e1 - m1 - xhat * m2)
+
+    wb_copy[0].wait_recv()
+    wa_copy.wait_recv()
+    total = Wc[chip].astype(F32) + Wb[0].astype(F32) + Wa[...].astype(F32)
+    dot_one = jnp.zeros((1, 128), F32)
+    for p in range(3):
+        piece = total[p * 256 : (p + 1) * 256, :]
+        dwq_o[p] = piece.T
+        dot_one = dot_one + jnp.sum(piece * wqkv[p].T.astype(F32), axis=0, keepdims=True)
+    for t in range(6, 12):
+        tick(t)
+    for m in range(4):
+
+        @pl.when(jnp.logical_not(org))
+        def _(m=m):
+            ref = dw4_o.at[w_rows(0, m)]
+            remote(ref, ref, fin_s.at[m], fin_r.at[m], (core, z)).wait_recv()
+
+    part_two = jnp.sum(dw4_o[0 : 2 * HID, :] * w4[0 : 2 * HID, :].astype(F32), axis=0, keepdims=True)
+    gz[z, 0:1, :] = dot_one / gains[dp, 0:1, :]
+    gz[z, 1:2, :] = part_two / gains[dp, 1:2, :]
+    gz[z, 2:8, :] = jnp.zeros((6, 128), F32)
+    gain_copy = [
+        remote(gz.at[z], gz.at[z], gz_s.at[n], gz_r.at[z], (dp, lax.rem(z + n, 4))) for n in range(1, 4)
+    ]
+    for cp in gain_copy:
+        cp.start()
+    for n in range(1, 4):
+        o = lax.rem(z + n, 4)
+        remote(gz.at[o], gz.at[o], gz_s.at[n], gz_r.at[o], (core, z)).wait_recv()
+    dg_o[...] = gz[0] + gz[1] + gz[2] + gz[3]
+
+    for cp in gain_copy:
+        cp.wait_send()
+    for w in range(4):
+        core_copy(w).wait_send()
+    wb_copy[0].wait_send()
+    wb_copy[1].wait_send()
+    wa_copy.wait_send()
+    for i in range(4):
+        h_inward(i, lambda cp: cp.wait_send())
+    for c0 in range(2):
+        for qi in range(2):
+            pl.when(jnp.logical_not(is_self(c0, qi)))(lambda c0=c0, qi=qi: att_back(c0, qi).wait_send())
+    for e in range(8):
+        qi, m = UNITS[e]
+        unit_b(e, 0).wait_send()
+        unit_b(e, 1).wait_send()
+        unit_a(e).wait_send()
+        t = target(e)
+        pl.when(z > t)(lambda e=e: line_down(e).wait_send())
+        pl.when(z + 1 == t)(lambda e=e: line_up(e, 2).wait_send())
+        pl.when(z + 1 < t)(lambda e=e, qi=qi: line_up(e, qi).wait_send())
+
+        @pl.when(z == t)
+        def _(m=m):
+            rows = w_rows(0, m)
+            remote(give.at[rows], dw4_o.at[rows], fin_s.at[m], fin_r.at[m], (core, z)).wait_send()
+
+
+def run_backward(*args):
+    V = pl.BlockSpec(memory_space=pltpu.VMEM)
+    A = pl.BlockSpec(memory_space=pl.ANY)
+    dma = pltpu.SemaphoreType.DMA
+    s = jax.ShapeDtypeStruct
+    vm = pltpu.VMEM
+    return pl.pallas_call(
+        backward_kernel,
+        out_shape=(
+            s((256, 1024), BF), s((256, 1024), F32), s((3, 128, 256), F32), s((PACK, 128), F32), s((8, 128), F32),
+        ),
+        in_specs=[V] * 8 + [A] + [V] * 9,
+        out_specs=[V] * 5,
+        scratch_shapes=[
+            vm((2, PACK, 1024), BF), vm((256, 1024), F32), vm((512, 1024), BF), vm((256, 1024), F32),
+            vm((256, 1024), F32), vm((256, 1024), F32), vm((256, 1024), F32), vm((2, HID, 512), BF),
+            vm((2, HID, 512), BF), vm((2, HID, 512), BF), vm((512, 1024), BF), vm((256, 1024), F32),
+            vm((256, 1024), F32), vm((2, 512, 256), BF), vm((1024, 256), BF), vm((4, 4, 8, 256), F32),
+            vm((1024, 256), F32), vm((1024, 256), F32), vm((1024, 256), F32), vm((768, 1024), BF),
+            vm((4, 256, 1024), BF), vm((4, 256, 1024), BF), vm((256, 1024), BF), vm((2, 2, PACK, 256), BF),
+            vm((2, PACK, 256), BF), vm((3, PACK, 256), BF), vm((PACK, 128), F32), vm((768, 1024), BF),
+            vm((4, 768, 128), BF), vm((2, 768, 128), BF), vm((768, 128), BF), vm((4, 8, 128), F32),
+            dma((2, 4)), dma, dma, dma, dma, dma, dma, dma, dma, dma, dma, dma((2, 2)), dma((4,)),
+            dma((2, 8)), dma((2, 8)), dma((8,)), dma((8,)), dma((8,)), dma((8,)), dma((3, 8)),
+            dma((4,)), dma((4,)), dma((4,)), dma((4,)), dma((4,)), dma,
+            dma((4,)), dma((4,)), dma((2,)), dma((2,)), dma, dma, dma((4,)), dma((4,)),
+        ],
+        compiler_params=pltpu.CompilerParams(
+            collective_id=2, has_side_effects=True, vmem_limit_bytes=62 << 20
+        ),
+        name="feed_forward_backward",
+    )(*args)
+
+
+def local_fast(
+    tokens, lengths, seq_order, gain_attn, w_qkv, w_attn_out, gain_mlp, w_in, w_mlp_out, cotangent
+):
+    w4, gains, cs, sn, segc, segr = prepare(
+        lengths, seq_order, gain_attn, w_attn_out, gain_mlp, w_in, w_mlp_out
+    )
+    q, k, v, lse, att, attn2, h1, wq, packed, all_gains, cot2 = run_forward(
+        tokens, w_qkv, w4, gains, cs, sn, segc, segr, cotangent
+    )
+    out, d_tok, d_qkv, d_pack, d_gain = run_backward(
+        q, k, v, lse, att, attn2, h1, wq, packed, all_gains, cot2, tokens, cs, sn, segc, segr, w_qkv, w4
+    )
+    d_in = d_pack[: 2 * HID].reshape(2, HID, 128).transpose(2, 0, 1)
+    return (
+        out, d_tok, d_gain[0], d_qkv, d_pack[3 * HID :], d_gain[1], d_in, d_pack[2 * HID : 3 * HID],
+    )
 
 
 def layer_norm(field_in, norm_gain):
@@ -39,20 +1057,6 @@
 
 def geglu(act_part, up_part):
     return jax.nn.gelu(act_part, approximate=False) * up_part
-
-
-def layout(lengths, seq_order, group_rows):
-    seq_total = seq_order.shape[0]
-    first_seq = lax.axis_index("dp") * SEQ_GRP
-    chosen = lax.dynamic_slice_in_dim(seq_order, first_seq, SEQ_GRP)
-    matched = chosen[:, None] == jnp.arange(seq_total, dtype=jnp.int32)[None, :]
-    dealt_lengths = jnp.sum(jnp.where(matched, lengths[None, :], 0), axis=1)
-    seq_ends = jnp.cumsum(dealt_lengths)
-    row_index = jnp.arange(group_rows, dtype=jnp.int32)
-    passed = row_index[:, None] >= seq_ends[None, :]
-    segment = jnp.sum(passed.astype(jnp.int32), axis=1)
-    row_start = jnp.sum(jnp.where(passed, dealt_lengths[None, :], 0), axis=1)
-    return (segment, (row_index - row_start).astype(jnp.float32))
 
 
 def item_layout(array_in, block_rows):
@@ -208,7 +1212,7 @@
     )
 
 
-def local(
+def local_plain(
     tokens, lengths, seq_order, gain_attn, w_qkv, w_attn_out, gain_mlp, w_in, w_mlp_out, cotangent
 ):
     row_count = tokens.shape[0]
@@ -291,8 +1295,9 @@
 
 
 def solution(mesh):
+    fast = mesh.shape["dp"] == 8 and mesh.shape["tensor"] == 4
     return jax.shard_map(
-        local,
+        local_fast if fast else local_plain,
         mesh=mesh,
         in_specs=(
             P(("dp", "tensor"), None),

time: 1060 us -> 311 us (0.29)
  waiting for transfers between devices: 675 us -> 0 us
  Pallas kernels: 0 us -> 289 us
  matrix products: 159 us -> 0 us
  loops' own time: 63.2 us -> 0 us
  blocking collectives: 56.6 us -> 0 us
  local copies, waits for them, and re-layouts: 45.3 us -> 11.9 us
  other arithmetic: 37.3 us -> 8.15 us
  between operations: 15.5 us -> 0.69 us
    reduce_scatter x8 -> x0, waiting for transfers between devices: 431 us -> none  [the longest x2 147 us: sum_grads(): lax.psum_scatter(row_term(jnp.int32(0), row_count * lax.axis_size('tensor...]
    pallas_call x0 -> x2, Pallas kernels: none -> 289 us  [the longest x1 169 us: run_backward(): pl.pallas_call(backward_kernel, out_shape=(s((256, 1024), BF), s((256, 10...]
    all_gather x7 -> x0, waiting for transfers between devices: 242 us -> none  [the longest x2 96.3 us: spread_rows(): return lax.all_gather(local_rows, 'tensor', axis=0, tiled=True)]
    dot_general x68 -> x0, matrix products: 159 us -> none  [the longest x16 26.8 us: masked_scores(): lax.dot_general(query_block, key_head, (((1,), (1,)), ((), ())), preferre...]
    another operation x2 -> x0, loops' own time: 63.2 us -> none  [the longest x1 31.6 us: attend_backward(): lax.scan(one_item, (zero_heads, zero_heads), jnp.arange(head_count * bloc...]
    all_gather x3 -> x0, blocking collectives: 31.1 us -> none  [the longest x1 12 us: local(): lax.all_gather(w_attn_out, 'dp', axis=1, tiled=True)]
    dynamic_slice x48 -> x0, local copies, waits for them, and re-layouts: 18.1 us -> none  [the longest x16 9.32 us: attend_forward(): lax.map(one_item, jnp.arange(head_count * block_count, dtype=jnp.int32))]
    reduce_sum x17 -> x1, other arithmetic: 15.8 us -> 0.09 us  [layout(): segment = jnp.sum(passed.astype(jnp.int32), axis=1)]
  transfers between devices with their start and end apart: 15 -> 0, of which waited for: 15 -> 0; matrix products, arithmetic and copies ran while one was open for 5% -> 0% of each run, Pallas kernels for 0% -> 0%
where the time goes in v1:
time: 311 us; the launch traced here: 310 us
  Pallas kernels  289 us (93%)
  local copies, waits for them, and re-layouts  11.9 us (4%)
  other arithmetic  8.15 us (3%)
    pallas_call x1, Pallas kernels, run_backward(): pl.pallas_call(backward_kernel, out_shape=(s((256, 1024), BF), s((256, 10...  169 us
    pallas_call x1, Pallas kernels, run_forward(): pl.pallas_call(forward_kernel, out_shape=(s((1024, 256), BF), s((1024, 25...  120 us

profile of v1, /device:TPU:0, one launch (start us, length us, event | category | flops | bytes accessed | tf_op | source)
XLA Modules:
  0.0 310.2 jit_solution(8028439851417752571)
XLA Ops:
  0.6 0.7 dynamic_slice.3
  1.4 0.8 select_reduce_fusion.1
  2.2 0.2 reduce-window.8
  2.4 0.1 pad.10.clone
  2.5 0.7 bitcast_convert_fusion
  3.2 0.7 maximum_maximum_fusion.gains
  3.8 0.1 convert_reduce_fusion
  3.9 0.6 broadcast_in_dim.55.segr
  4.6 1.0 broadcast_in_dim.54.segc
  5.6 1.9 pad_maximum_fusion.w4
  7.5 1.9 fusion
  9.4 1.8 pad_maximum_fusion.1
  11.3 120.2 %forward_attention.1 = (bf16[1024,256]{1,0:T(8,128)(2,1)}, bf16[1024,256]{1,0:T(8,128)(2,1)}, bf16[1024,256]{1,0:T(8,128)(2,1)}, f32[4,4,8,256]{3,2,1,0:T(8,128)...) custom-call(bf16[256,1024]{1,0:T(8,128)(2,1)} %tok.3, ...), custom_call_target="tpu_custom_call" | custom-call | tf_op jit(solution)/shard_map/forward_attention/pallas_call | solution.py:404
  131.4 169.3 %feed_forward_backward.1 = (bf16[256,1024]{1,0:T(8,128)(2,1)}, f32[256,1024]{1,0:T(8,128)}, f32[3,128,256]{2,1,0:T(8,128)}, f32[2224,128]{1,0:T(8,128)}, f32[8,128]{1,0:T(8,128)}) custom-call(bf16[1024,256]{1,0:T(8,128)(2,1)} %get-tuple-element.24.q, bf16[1024,256]{1,0:T(8,128)(2,1)} %get-tuple-element.25.k, bf16[1024,256]{1,0:T(8,128)(2,1)} %get-tuple-element.26.v, ...), custom_call_target="tpu_custom_call" | custom-call | tf_op jit(solution)/shard_map/feed_forward_backward/pallas_call | solution.py:987
  300.7 1.3 slice_bitcast_fusion
  302.0 1.6 slice.16
  303.6 1.7 slice.19
  305.3 2.1 slice.18
  307.4 0.0 copy-done.1
  307.4 0.8 copy.22
  308.2 0.0 copy-done
  308.2 1.0 copy.23
  309.2 0.3 copy-done.2
  309.4 0.7 copy.24
  (7 shorter events, 0.0 us)
Async XLA Ops:
  302.0 5.4 %copy-start.1 = (bf16[256,1024]{1,0:T(8,128)(2,1)S(1)}, bf16[256,1024]{1,0:T(8,128)(2,1)}, u32[]{:S(2)}) copy-start(bf16[256,1024]{1,0:T(8,128)(2,1)} %get-tuple-element.59) | copy-start | bytes 1572868
  305.3 2.9 copy-start
  308.2 1.2 copy-start.2

commit v2 on v1

v2 whole, which is shorter than its diff:
```python
import functools

import jax
import jax.numpy as jnp
from jax import lax
from jax.experimental import pallas as pl
from jax.experimental.pallas import tpu as pltpu
from jax.sharding import PartitionSpec as P

HEAD_DIM = 64
SEQ_GRP = 4
rope_base = 160000.0
norm_eps = 1e-05
masked_fill = -1e30
MESH = pl.DeviceIdType.MESH
BF = jnp.bfloat16
F32 = jnp.float32

NT = (((1,), (1,)), ((), ()))
TN = (((0,), (0,)), ((), ()))


def place():
    dp = lax.axis_index("dp")
    z = lax.axis_index("tensor")
    c = lax.rem(dp, 2)
    x = lax.rem(lax.div(dp, 2), 2)
    y = lax.div(dp, 4)
    return dp, z, c, x, y


def flip(dp, bits, distance):
    out = dp
    for b, bit in enumerate(bits):
        if (distance >> b) & 1:
            out = out + (1 << b) - (2 << b) * bit
    return out


def remote(src, dst, send, recv, dev):
    return pltpu.make_async_remote_copy(
        src_ref=src, dst_ref=dst, send_sem=send, recv_sem=recv, device_id=dev, device_id_type=MESH
    )


def cols(start, size):
    return pl.ds(pl.multiple_of(start, size), size)


def greet(dp, z, bits):
    c = bits[0]
    barrier = pltpu.get_barrier_semaphore()
    peers = [(flip(dp, bits, d), z) for d in range(1, 8)]
    core = flip(dp, bits, 1)
    for k in range(1, 4):
        peers.append((dp, lax.rem(z + k, 4)))
        peers.append((core, lax.rem(z + k, 4)))
    for p in peers:
        pl.semaphore_signal(barrier, inc=1, device_id=p, device_id_type=MESH)
    pl.semaphore_wait(barrier, len(peers))


def norm_rows(v):
    mean = jnp.mean(v, axis=-1, keepdims=True)
    centered = v - mean
    var = jnp.mean(centered * centered, axis=-1, keepdims=True)
    rstd = lax.rsqrt(var + norm_eps)
    return centered * rstd, rstd


def turn(v, cs, sn):
    lane = lax.broadcasted_iota(jnp.int32, cs.shape, 1)
    low_half = lax.rem(lane, HEAD_DIM) < HEAD_DIM // 2
    parts = []
    for t in range(v.shape[1] // 128):
        piece = v[:, t * 128 : (t + 1) * 128]
        swapped = jnp.where(low_half, pltpu.roll(piece, 96, 1), pltpu.roll(piece, 32, 1))
        parts.append(piece * cs + swapped * sn)
    return jnp.concatenate(parts, axis=1)


def gain_row(gains, row):
    return jnp.concatenate([gains[p, row : row + 1, :] for p in range(8)], axis=1)


HID = 656
PACK = 3 * HID + 256
ROWS = ((256, HID), (256 + HID, HID), (256 + 2 * HID, HID), (0, 256))
CUTS = ((0, 544), (544, 560), (1104, 560), (1664, 560))
HALVES = tuple((m, o, n) for m in (2, 0, 1) for o, n in ((0, 336), (336, 320))) + ((3, 0, 256),)
UNITS = tuple((q, k) for q in range(2) for k in range(6)) + ((0, 6), (1, 6))
NU = len(UNITS)
INV_SQRT2 = 0.7071067811865476
INV_SQRT_2PI = 0.3989422804014327


def layer_kernel(
    lengths, seq_order, tok, wqkv, win, wmlp, wout, gains_in, cot,
    out_o, dtok_o, dwq_o, dwin_o, dwmlp_o, dwout_o, dg_o,
    gains, w4, cs, sn, segc, segr, q, k, v, lse, att, attn2, h1, wq, cot2,
    G, X1, pool, yr, dr, acc, hidT, daT, duT, dX1, dxo, dsend, datt, delta,
    dq, dk, dv, Hs, Hi, Hx, Rb, Ra, Z, give, Wp, Wc, Wb, Wa, gz,
    us, ds, rb, ra, wr_s, wr_r, wx_s, wx_r, g_s, g_r, co_s, co_r, hop_s, hop_r,
    qu_s, qd_s, q_r, pa_s, pb_s, pf_s, pa_r, pb_r, at_s, at_r,
    y_s, y_r, h_s, h_r, d_s, d_r, u_s, u_r, e_s, e_r, t_s, t_r,
    b_s, b_r, a_s, a_r, zu_s, zd_s, z_r, fin_s, fin_r,
    hu_s, hd_s, hi_r, hx_r, wc_s, wc_r, wb_s, wb_r, wa_s, wa_r, gz_s, gz_r, lc,
):
    dp, z, c, x, y = place()
    bits = (c, x, y)
    core = flip(dp, bits, 1)
    px, py = flip(dp, bits, 2), flip(dp, bits, 4)
    a = (1 - c) * px + c * py
    b = (1 - c) * py + c * px
    chip, chip_a, chip_b = lax.div(dp, 2), lax.div(a, 2), lax.div(b, 2)
    chip_d = 3 - chip
    home = lax.div(z, 2)
    org = c == home
    zq = lax.rem(z, 2)
    end = (z == 0) | (z == 3)
    own = cols(c * 256, 256)
    other = cols((1 - c) * 256, 256)
    tall, vT, ur, oT = Hs, Hx, yr, acc.at[:, 0:256]
    h2a, dya, dqkvT = pool.at[0:512], pool.at[512:1024], pool.at[0:768]
    dw4 = (dwin_o.at[0:HID], dwin_o.at[HID : 2 * HID], dwmlp_o, dwout_o)
    greet(dp, z, bits)

    def no(cond):
        return jnp.logical_not(cond)

    def tok_up(k_, h):
        ref = tall.at[z - k_, pl.ds(h * 128, 128)]
        src = tok.at[pl.ds(h * 128, 128)] if k_ == 0 else ref
        return remote(src, ref, us.at[k_, h], rb.at[k_ + 1, h], (dp, z + 1))

    def tok_down(k_, h):
        ref = tall.at[z + k_, pl.ds(h * 128, 128)]
        src = tok.at[pl.ds(h * 128, 128)] if k_ == 0 else ref
        return remote(src, ref, ds.at[k_, h], ra.at[k_ + 1, h], (dp, z - 1))

    def up_ok(k_):
        return (z >= k_) & (z < 3)

    def down_ok(k_):
        return (z + k_ <= 3) & (z > 0)

    for h in range(2):
        pl.when(up_ok(0))(lambda h=h: tok_up(0, h).start())
        pl.when(down_ok(0))(lambda h=h: tok_down(0, h).start())

    for d in range(1, 8):
        remote(gains_in, gains.at[dp], g_s.at[d], g_r.at[d], (flip(dp, bits, d), z)).start()
    own_rows = cols(dp * 128, 128)
    for j, d in enumerate((2, 4, 6)):
        remote(wqkv, wq.at[:, own_rows], wr_s.at[j], wr_r.at[j], (flip(dp, bits, d), z)).start()
    remote(wqkv, wq.at[:, own_rows], wx_s.at[3], wx_r.at[3], (core, z)).start()
    cot_copy = remote(cot, cot2.at[own], co_s, co_r, (core, z))
    cot_copy.start()
    cot_local = pltpu.make_async_copy(cot, cot2.at[own], lc)
    cot_local.start()

    w4[0:256, :] = wout[...]
    w4[256 : 256 + 2 * HID, :] = win[...]
    w4[256 + 2 * HID : PACK, :] = wmlp[...]
    mine = G.at[zq, :, cols(dp * 128, 128)]
    hop = remote(w4, mine, hop_s, hop_r, (core, z))
    pl.when(no(org))(lambda: hop.start())

    @pl.when(org)
    def _():
        G[zq, :, cols(dp * 128, 128)] = w4[...]

    gains[dp] = gains_in[...]
    wq[:, own_rows, :] = wqkv[...]
    tall[z] = tok[...]
    cot_local.wait()

    def piece(qi, u, where):
        r0, n = CUTS[u]
        return G.at[qi, pl.ds(r0, n), cols(where * 256, 256)]

    def line_send(qi, u, up, act):
        ref = piece(qi, u, chip)
        if up:
            pl.when((z >= 2 * c + qi) & (z < 3))(
                lambda: act(remote(ref, ref, qu_s.at[qi, u], q_r.at[qi, u], (dp, z + 1)))
            )
        else:
            pl.when((z <= 2 * c + qi) & (z > 0))(
                lambda: act(remote(ref, ref, qd_s.at[qi, u], q_r.at[qi, u], (dp, z - 1)))
            )

    def plane_a(qi, u):
        return remote(piece(qi, u, chip), piece(qi, u, chip), pa_s.at[qi, u], pa_r.at[qi, u], (a, z))

    def plane_b(qi, u):
        return remote(piece(qi, u, chip), piece(qi, u, chip), pb_s.at[qi, u], pb_r.at[qi, 0, u], (b, z))

    def plane_f(qi, u):
        return remote(piece(qi, u, chip_a), piece(qi, u, chip_a), pf_s.at[qi, u], pb_r.at[qi, 1, u], (b, z))

    def spread(qi, u):
        plane_a(qi, u).start()
        plane_b(qi, u).start()

    near = (1 - c) * lax.div(z + 2, 3) + c * lax.div(z, 3)
    far = 1 - near

    def begin(cp):
        cp.start()

    def arrive(qi, u):
        ref = piece(qi, u, chip)
        remote(ref, ref, qu_s.at[qi, u], q_r.at[qi, u], (core, z)).wait_recv()

    def across(qi, u):
        ref = piece(qi, u, chip_a)
        remote(ref, ref, pa_s.at[qi, u], pa_r.at[qi, u], (a, z)).wait_recv()
        plane_f(qi, u).start()

    def stage(qi, u):
        arrive(qi, u)
        line_send(qi, u, True, begin)
        line_send(qi, u, False, begin)
        spread(qi, u)

    def stage_far(u):
        stage(far, u)

    def stage_near(u):
        stage(near, u)

    ends, starts, total = [], [], 0
    for j in range(SEQ_GRP):
        ends.append(total)
        total = total + lengths[seq_order[dp * SEQ_GRP + j]]
    for dst, shape, axis in ((segc, (1024, 128), 0), (segr, (8, 1024), 1)):
        row = lax.broadcasted_iota(jnp.int32, shape, axis)
        seg = jnp.zeros(shape, F32)
        start = jnp.zeros(shape, jnp.int32)
        for j in range(1, SEQ_GRP):
            passed = row >= ends[j]
            seg = jnp.where(passed, float(j), seg)
            start = jnp.where(passed, ends[j], start)
        dst[...] = seg
        if axis == 0:
            angle = (row - start).astype(F32) * gains_in[2:3, :]
            cs[...] = jnp.cos(angle)
            sn[...] = jnp.sin(angle) * gains_in[3:4, :]

    for d in range(1, 8):
        p = flip(dp, bits, d)
        remote(gains_in, gains.at[p], g_s.at[d], g_r.at[d], (p, z)).wait_recv()

    @pl.when(org)
    def _():
        remote(w4, G.at[zq, :, cols(core * 128, 128)], hop_s, hop_r, (core, z)).wait_recv()
        for u in range(4):
            spread(near, u)

    @pl.when(org)
    def _():
        for u in range(4):
            pl.when((z == 0) | (z == 2))(lambda u=u: line_send(near, u, True, begin))
            pl.when((z == 1) | (z == 3))(lambda u=u: line_send(near, u, False, begin))

    for j, d in enumerate((2, 4, 6)):
        p = flip(dp, bits, d)
        rows = wq.at[:, cols(p * 128, 128)]
        remote(wqkv, rows, wr_s.at[j], wr_r.at[j], (p, z)).wait_recv()
        remote(rows, rows, wx_s.at[j], wx_r.at[j], (core, z)).start()
    for j, d in enumerate((3, 5, 7, 1)):
        p = flip(dp, bits, d)
        remote(wqkv, wq.at[:, cols(p * 128, 128)], wx_s.at[j], wx_r.at[j], (core, z)).wait_recv()

    gain1, gain2 = gain_row(gains, 0), gain_row(gains, 1)

    def project(s):
        base = s * 256

        @pl.loop(0, 8)
        def _(r):
            xhat, _r = norm_rows(tall[s, pl.ds(pl.multiple_of(r * 32, 32), 32), :].astype(F32))
            h1[pl.ds(pl.multiple_of(base + r * 32, 32), 32), :] = (xhat * gain1).astype(BF)

        rows = pl.ds(pl.multiple_of(base, 256), 256)
        hb = h1[rows, :]
        cb, sb = cs[rows, :], sn[rows, :]
        for p, dst in enumerate((q, k, v)):
            r = jnp.dot(hb, wq[p], preferred_element_type=F32)
            if p < 2:
                r = turn(r, cb, sb)
            if p == 0:
                r = r * (HEAD_DIM**-0.5)
            dst[rows, :] = r.astype(BF)

    for k_ in range(4):
        if k_ > 0:
            below, above = z - k_ >= 0, z + k_ <= 3
            for h in range(2):

                @pl.when(below)
                def _(k_=k_, h=h):
                    ref = tall.at[z - k_, pl.ds(h * 128, 128)]
                    remote(ref, ref, us.at[k_, h], rb.at[k_, h], (core, z)).wait_recv()
                    if k_ < 3:
                        pl.when(up_ok(k_))(lambda: tok_up(k_, h).start())

                @pl.when(above)
                def _(k_=k_, h=h):
                    ref = tall.at[z + k_, pl.ds(h * 128, 128)]
                    remote(ref, ref, ds.at[k_, h], ra.at[k_, h], (core, z)).wait_recv()
                    if k_ < 3:
                        pl.when(down_ok(k_))(lambda: tok_down(k_, h).start())

        if k_ == 1:

            @pl.when(org & no(end))
            def _():
                for u in range(4):
                    pl.when(z == 1)(lambda u=u: line_send(near, u, True, begin))
                    pl.when(z == 2)(lambda u=u: line_send(near, u, False, begin))

        @pl.loop(0, 2)
        def _(t, k_=k_):
            s = z - k_ + 2 * k_ * t
            pl.when((s >= 0) & (s <= 3) & ((k_ > 0) | (t == 0)))(lambda: project(s))

        if k_ == 1:

            @pl.when(org)
            def _():
                for u in range(4):
                    across(near, u)
                for u in range(3):
                    stage_far(u)

        if k_ == 2:

            @pl.when(org)
            def _():
                stage_far(3)
                across(far, 0)
                across(far, 1)

            @pl.when(no(org) & no(end))
            def _():
                stage_near(0)
                stage_near(1)

        if k_ == 3:

            @pl.when(org)
            def _():
                across(far, 2)
                across(far, 3)

    for s in range(4):
        vT[:, s * 256 : (s + 1) * 256] = v[s * 256 : (s + 1) * 256, :].T
    head_of = lax.div(lax.broadcasted_iota(jnp.int32, (256, 256), 1), HEAD_DIM)

    def attend(i):
        rows = pl.ds(pl.multiple_of(i * 256, 256), 256)
        qb = q[rows, :]
        seg_q = segr[0:1, rows]
        heads = range(4)
        qh = [jnp.where(head_of == h, qb, jnp.zeros((), BF)) for h in heads]
        top = [jnp.full((1, 256), masked_fill, F32) for h in heads]
        tot = [jnp.zeros((1, 256), F32) for h in heads]
        out = [jnp.zeros((HEAD_DIM, 256), F32) for h in heads]
        for kc in range(4):
            keys = slice(kc * 256, kc * 256 + 256)
            kb = k[keys, :]
            seg_k = segc[keys, :]
            same = jnp.concatenate([seg_k, seg_k], axis=1) == seg_q
            for h in heads:
                s = lax.dot_general(kb, qh[h], NT, preferred_element_type=F32)
                s = jnp.where(same, s, masked_fill)
                new = jnp.maximum(top[h], jnp.max(s, axis=0, keepdims=True))
                p = jnp.exp(s - new)
                keep = jnp.exp(top[h] - new)
                tot[h] = tot[h] * keep + jnp.sum(p, axis=0, keepdims=True)
                vh = vT[h * HEAD_DIM : (h + 1) * HEAD_DIM, keys]
                out[h] = out[h] * keep + jnp.dot(vh, p.astype(BF), preferred_element_type=F32)
                top[h] = new
        for h in heads:
            oT[h * HEAD_DIM : (h + 1) * HEAD_DIM, :] = out[h] * (1.0 / tot[h])
            lse[h, i] = jnp.broadcast_to(top[h] + jnp.log(tot[h]), (8, 256))
        att[rows, :] = oT[...].T.astype(BF)

    def att_slot(src_core, q):
        return attn2.at[cols(src_core * 256, 256), cols(q * 256, 256)]

    def att_copy(n, i):
        rows = pl.ds(pl.multiple_of(i * 256, 256), 256)
        return remote(
            att.at[rows, :], att_slot(c, zq), at_s.at[n], at_r.at[c, zq], (2 * chip + home, i)
        )

    @pl.loop(0, 4)
    def _(n):
        i = lax.rem(z + 1 + n, 4)
        attend(i)
        for m in range(4):

            @pl.when((n == m) & ((m < 3) | no(org)))
            def _(m=m):
                att_copy(m, i).start()

        @pl.when((n == 3) & org)
        def _():
            attn2[own, cols(zq * 256, 256)] = att[pl.ds(pl.multiple_of(z * 256, 256), 256), :]

        sf, sn_, af, an = stage_far, stage_near, lambda u: across(far, u), lambda u: across(near, u)
        plans = (
            (no(org) & no(end), (((sn_, 2), (sn_, 3)), ((sf, 0), (sf, 1), (an, 0), (an, 1)),
                                 ((sf, 2), (an, 2), (an, 3)), ((sf, 3), (af, 0), (af, 1)))),
            (no(org) & end, (((sn_, 0),), ((sn_, 1), (sn_, 2)), ((sn_, 3), (an, 0), (an, 1)),
                             ((sf, 0), (an, 2)))),
        )
        for who, plan in plans:
            for m, ops in enumerate(plan):

                @pl.when(who & (n == m))
                def _(ops=ops):
                    for op, u in ops:
                        op(u)

    @pl.when(no(org) & no(end))
    def _():
        across(far, 2)
        across(far, 3)

    @pl.when(no(org) & end)
    def _():
        stage_far(1)
        across(near, 3)
        across(far, 0)
        stage_far(2)
        across(far, 1)
        stage_far(3)
        across(far, 2)
        across(far, 3)

    for k_ in range(3):
        for h in range(2):
            pl.when(up_ok(k_))(lambda k_=k_, h=h: tok_up(k_, h).wait_send())
            pl.when(down_ok(k_))(lambda k_=k_, h=h: tok_down(k_, h).wait_send())
    for src in range(2):
        for qi in range(2):
            mine_too = (c == src) & (z == 2 * c + qi)

            @pl.when(no(mine_too))
            def _(src=src, qi=qi):
                slot = att_slot(src, qi)
                remote(slot, slot, at_s.at[0], at_r.at[src, qi], (core, z)).wait_recv()

    def pack_wait(u):
        for qi in range(2):
            for w, where in enumerate((chip_b, chip_d)):
                ref = piece(qi, u, where)
                remote(ref, ref, pb_s.at[qi, u], pb_r.at[qi, w, u], (b, z)).wait_recv()

    def w_rows(qi, m):
        r0, n = ROWS[m]
        return pl.ds(r0, n)

    pack_wait(0)

    def out_proj(rows):
        return sum(
            jnp.dot(
                attn2[rows, qi * 256 : (qi + 1) * 256], G[qi, w_rows(qi, 3), :], preferred_element_type=F32
            )
            for qi in range(2)
        )

    acc[...] = out_proj(other)
    y_copy = remote(acc, yr, y_s, y_r, (core, z))
    y_copy.start()
    X1[...] = tok[...].astype(F32) + out_proj(own)
    y_copy.wait()

    def chunk(r):
        return pl.ds(pl.multiple_of(r * 32, 32), 32)

    def own_chunk(r):
        return pl.ds(pl.multiple_of(c * 256 + r * 32, 32), 32)

    @pl.loop(0, 8)
    def _(r):
        x1 = X1[chunk(r), :] + yr[chunk(r), :]
        X1[chunk(r), :] = x1
        xhat, _r = norm_rows(x1)
        h2a[own_chunk(r), :] = (xhat * gain2).astype(BF)

    h_copy = remote(h2a.at[own], h2a.at[own], h_s, h_r, (core, z))
    h_copy.start()
    remote(cot, cot2.at[other], co_s, co_r, (core, z)).wait_recv()
    for u in range(1, 4):
        pack_wait(u)
    h_copy.wait()

    TILES = ((0, 224), (224, 224), (448, 208))
    for r0, n in TILES:

        @pl.loop(0, 2)
        def _(qi, r0=r0, n=n):
            h2 = h2a[...]
            act = lax.dot_general(G[qi, pl.ds(ROWS[0][0] + r0, n), :], h2, NT, preferred_element_type=F32)
            up = lax.dot_general(G[qi, pl.ds(ROWS[1][0] + r0, n), :], h2, NT, preferred_element_type=F32)
            dh = lax.dot_general(G[qi, pl.ds(ROWS[2][0] + r0, n), :], cot2[...], NT, preferred_element_type=F32)
            Phi = 0.5 + 0.5 * lax.erf(act * INV_SQRT2)
            phi = jnp.exp(-0.5 * act * act) * INV_SQRT_2PI
            gel = act * Phi
            rr = pl.ds(r0, n)
            hidT[qi, rr, :] = (gel * up).astype(BF)
            daT[qi, rr, :] = (dh * up * (Phi + act * phi)).astype(BF)
            duT[qi, rr, :] = (dh * gel).astype(BF)

    def tn(lhs, rhs):
        return lax.dot_general(lhs, rhs, TN, preferred_element_type=F32)

    def d_norm(dst, rows):
        for half in range(2):
            hc = slice(half * 512, half * 512 + 512)
            dst[:, hc] = sum(
                tn(daT[qi, :, rows], G[qi, w_rows(qi, 0), hc]) + tn(duT[qi, :, rows], G[qi, w_rows(qi, 1), hc])
                for qi in range(2)
            )

    def mlp_out(dst, rows, plus=None):
        for half in range(2):
            hc = slice(half * 512, half * 512 + 512)
            r = sum(tn(hidT[qi, :, rows], G[qi, w_rows(qi, 2), hc]) for qi in range(2))
            dst[:, hc] = r if plus is None else r + plus[:, hc]

    def grads(qi, m):
        lhs, rhs = ((daT, h2a), (duT, h2a), (hidT, cot2))[m]

        @pl.loop(0, 4)
        def _(t):
            tc = cols(t * 256, 256)
            G[qi, w_rows(qi, m), tc] = jnp.dot(lhs[qi], rhs[:, tc], preferred_element_type=F32).astype(BF)

    def unit(e):
        qi, k_ = UNITS[e]
        m, o, n = HALVES[k_]
        return qi, pl.ds(ROWS[m][0] + o, n)

    def part(e, where):
        qi, rows = unit(e)
        return G.at[qi, rows, cols(where * 256, 256)]

    def unit_b(e, slot):
        qi, rows = unit(e)
        src = part(e, chip_b if slot == 0 else chip_d)
        return remote(src, Rb.at[slot, qi, rows], b_s.at[slot, e], b_r.at[slot, e], (b, z))

    def unit_a(e):
        qi, rows = unit(e)
        return remote(part(e, chip_a), Ra.at[qi, rows], a_s.at[e], a_r.at[e], (a, z))

    def send_b(e):
        unit_b(e, 1).start()
        unit_b(e, 0).start()

    def stage1(e):
        qi, rows = unit(e)
        unit_b(e, 1).wait_recv()
        ref = part(e, chip_a)
        ref[...] = (ref[...].astype(F32) + Rb[1, qi, rows, :].astype(F32)).astype(BF)
        unit_a(e).start()

    def line_up(e, slot):
        rows = unit(e)[1]
        return remote(part(e, chip), Z.at[slot, rows], zu_s.at[e], z_r.at[slot, e], (dp, z + 1))

    def line_down(e):
        qi, rows = unit(e)
        return remote(part(e, chip), Z.at[qi, rows], zd_s.at[e], z_r.at[qi, e], (dp, z - 1))

    def target(e):
        return 2 * c + UNITS[e][0]

    def inward(e, act):
        t = target(e)
        pl.when(z > t)(lambda: act(line_down(e)))
        pl.when(z + 1 == t)(lambda: act(line_up(e, 2)))
        pl.when(z + 1 < t)(lambda: act(line_up(e, UNITS[e][0])))

    def stage2(e):
        qi, rows = unit(e)
        unit_b(e, 0).wait_recv()
        unit_a(e).wait_recv()
        ref = part(e, chip)
        ref[...] = (ref[...].astype(F32) + Rb[0, qi, rows, :].astype(F32) + Ra[qi, rows, :].astype(F32)).astype(BF)
        t = target(e)
        pl.when(((z == 3) & (z > t)) | ((z == 0) & (z < t)))(lambda: inward(e, begin))

    def line_wait(e, slot):
        ref = Z.at[slot, unit(e)[1]]
        remote(ref, ref, zu_s.at[e], z_r.at[slot, e], (core, z)).wait_recv()

    def stage3(e, depth):
        qi, rows = unit(e)
        t = target(e)
        mid = ((z > t) & (z == 3 - depth)) | ((z < t) & (z == depth))

        @pl.when(mid)
        def _():
            line_wait(e, qi)
            ref = part(e, chip)
            ref[...] = (ref[...].astype(F32) + Z[qi, rows, :].astype(F32)).astype(BF)
            inward(e, begin)

    def final(k_):
        m, o, n = HALVES[k_]
        return give.at[pl.ds(ROWS[m][0] + o, n)], dw4[m].at[pl.ds(o, n)]

    def stage4(e):
        qi, rows = unit(e)
        k_ = UNITS[e][1]

        @pl.when(z == target(e))
        def _():
            gift, dst = final(k_)
            dst[...] = G[qi, rows, cols(dp * 128, 128)].astype(F32)
            gift[...] = G[qi, rows, cols(core * 128, 128)].astype(F32)

            def take(slot):
                line_wait(e, slot)
                for who, ref in ((c, dst), (1 - c, gift)):
                    ref[...] = ref[...] + Z[slot, rows, cols(who * 128, 128)].astype(F32)

            pl.when(z < 3)(lambda: take(qi))
            pl.when(z > 0)(lambda: take(2))
            remote(gift, dst, fin_s.at[k_], fin_r.at[k_], (core, z)).start()

    def tick(t):
        for lag, step in enumerate(
            (stage1, stage2, lambda e: stage3(e, 1), lambda e: stage3(e, 2), stage4)
        ):
            if 0 <= t - lag < NU:
                step(t - lag)

    d_norm(acc, other)
    d_copy = remote(acc, dr, d_s, d_r, (core, z))
    d_copy.start()
    mlp_out(dxo, other)
    u_copy = remote(dxo, ur, u_s, u_r, (core, z))
    u_copy.start()
    d_norm(dX1, own)
    mlp_out(dtok_o, own, X1)
    for u in range(4):
        for qi in range(2):
            line_send(qi, u, True, lambda cp: cp.wait_send())
            line_send(qi, u, False, lambda cp: cp.wait_send())
        for qi in range(2):
            plane_a(qi, u).wait_send()
            plane_b(qi, u).wait_send()
            plane_f(qi, u).wait_send()
    def ff_grads(qi, m):
        grads(qi, m)
        for e in range(NU):
            if UNITS[e][0] == qi and HALVES[UNITS[e][1]][0] == m:
                send_b(e)

    ff_grads(0, 2)
    ff_grads(0, 0)
    d_copy.wait()

    @pl.loop(0, 8)
    def _(r):
        dh2 = dX1[chunk(r), :] + dr[chunk(r), :]
        xhat, rstd = norm_rows(X1[chunk(r), :])
        e2 = dh2 * gain2
        m1 = jnp.mean(e2, axis=-1, keepdims=True)
        m2 = jnp.mean(e2 * xhat, axis=-1, keepdims=True)
        dx = cot2[own_chunk(r), :].astype(F32) + rstd * (e2 - m1 - xhat * m2)
        dX1[chunk(r), :] = dx
        dya[own_chunk(r), :] = dx.astype(BF)

    e_copy = remote(dya.at[own], dya.at[own], e_s, e_r, (core, z))
    e_copy.start()
    ff_grads(0, 1)
    e_copy.wait()
    for qi in range(2):
        dsend[qi] = lax.dot_general(dya[...], G[qi, w_rows(qi, 3), :], NT, preferred_element_type=F32).astype(BF)

    def att_back(c0, qi):
        dst = datt.at[cols(z * 256, 256)]
        return remote(
            dsend.at[qi, pl.ds(c0 * 256, 256)], dst, t_s.at[c0, qi], t_r.at[z], (2 * chip + c0, 2 * c + qi)
        )

    def is_self(c0, qi):
        return (c == c0) & (z == 2 * c + qi)

    for c0 in range(2):
        for qi in range(2):
            pl.when(no(is_self(c0, qi)))(lambda c0=c0, qi=qi: att_back(c0, qi).start())

            @pl.when(is_self(c0, qi))
            def _(c0=c0, qi=qi):
                datt[cols(z * 256, 256), :] = dsend[qi, c0 * 256 : (c0 + 1) * 256, :]

    for m in (2, 0, 1):
        ff_grads(1, m)
    for qi in range(2):

        @pl.loop(0, 4)
        def _(t, qi=qi):
            tc = cols(t * 256, 256)
            G[qi, w_rows(qi, 3), tc] = tn(attn2[:, qi * 256 : (qi + 1) * 256], dya[:, tc]).astype(BF)

        send_b(12 + qi)
    tick(0)
    u_copy.wait()
    out_o[...] = (dtok_o[...] + ur[...]).astype(BF)
    dq[...] = jnp.zeros_like(dq)
    dk[...] = jnp.zeros_like(dk)
    dv[...] = jnp.zeros_like(dv)
    for i in range(4):

        @pl.when(no(org & (z == i)))
        def _(i=i):
            ref = datt.at[pl.ds(i * 256, 256)]
            remote(ref, ref, t_s.at[0, 0], t_r.at[i], (core, z)).wait_recv()

    @pl.loop(0, 4)
    def _(i):
        rows = pl.ds(pl.multiple_of(i * 256, 256), 256)
        t = (datt[rows, :].astype(F32) * att[rows, :].astype(F32)).T
        for h in range(4):
            s = jnp.sum(t[h * 64 : (h + 1) * 64, :], axis=0, keepdims=True)
            delta[h, i] = jnp.broadcast_to(s, (8, 256))

    def block_order(l):
        return jnp.minimum(l, 1) * (lax.rem(l + 1, 3) + 1)

    def pair(i, j):
        ri = pl.ds(pl.multiple_of(i * 256, 256), 256)
        rj = pl.ds(pl.multiple_of(j * 256, 256), 256)

        kj, vj, qi_, dai = k[rj, :], v[rj, :], q[ri, :], datt[ri, :]
        seg_k = segc[rj, :]
        same = jnp.concatenate([seg_k, seg_k], axis=1) == segr[0:1, ri]
        none = jnp.zeros((), BF)
        dvs, dks, dqs = [], [], []
        for h in range(4):
            mine = head_of == h
            qh, dah = jnp.where(mine, qi_, none), jnp.where(mine, dai, none)
            s = lax.dot_general(kj, qh, NT, preferred_element_type=F32)
            p = jnp.exp(jnp.where(same, s, masked_fill) - lse[h, i, 0:1, :])
            dp_ = lax.dot_general(vj, dah, NT, preferred_element_type=F32)
            dsc = (p * (dp_ - delta[h, i, 0:1, :])).astype(BF)
            dvs.append(jnp.dot(p.astype(BF), dah, preferred_element_type=F32))
            dks.append(jnp.dot(dsc, qh, preferred_element_type=F32))
            dqs.append(tn(dsc, jnp.where(mine, kj, none)))
        dv[rj, :] = dv[rj, :] + (dvs[0] + dvs[1] + dvs[2] + dvs[3])
        dk[rj, :] = dk[rj, :] + (dks[0] + dks[1] + dks[2] + dks[3])
        dq[ri, :] = dq[ri, :] + (dqs[0] + dqs[1] + dqs[2] + dqs[3])

    def h_up(i, last):
        if last:
            return remote(Hs.at[i], Hx, hu_s.at[i], hx_r, (dp, z + 1))
        return remote(Hs.at[i], Hi.at[i], hu_s.at[i], hi_r.at[i], (dp, z + 1))

    def h_down(i):
        return remote(Hs.at[i], Hi.at[i], hd_s.at[i], hi_r.at[i], (dp, z - 1))

    def h_inward(i, act):
        pl.when(z > i)(lambda: act(h_down(i)))
        pl.when(z + 1 == i)(lambda: act(h_up(i, True)))
        pl.when(z + 1 < i)(lambda: act(h_up(i, False)))

    def h_wait(i):
        remote(Hi.at[i], Hi.at[i], hd_s.at[i], hi_r.at[i], (core, z)).wait_recv()

    def h_mid(i, depth):
        mid = ((z > i) & (z == 3 - depth)) | ((z < i) & (z == depth))

        @pl.when(mid)
        def _():
            h_wait(i)
            Hs[i] = (Hs[i].astype(F32) + Hi[i].astype(F32)).astype(BF)
            h_inward(i, begin)

    def finish(i):
        rows = pl.ds(pl.multiple_of(i * 256, 256), 256)
        cb, sb = cs[rows, :], -sn[rows, :]
        low = (
            turn(dq[rows, :] * (HEAD_DIM**-0.5), cb, sb).astype(BF),
            turn(dk[rows, :], cb, sb).astype(BF),
            dv[rows, :].astype(BF),
        )
        for p in range(3):
            dqkvT[p * 256 : (p + 1) * 256, rows] = low[p].T
        for half in range(2):
            hc = slice(half * 512, half * 512 + 512)
            dh = sum(
                lax.dot_general(low[p], wq[p, hc, :], NT, preferred_element_type=F32) for p in range(3)
            )
            Hs[i, :, hc] = dh.astype(BF)

            @pl.when(z == i)
            def _(dh=dh, hc=hc):
                acc[:, hc] = dh

        pl.when(((z == 3) & (z > i)) | ((z == 0) & (z < i)))(lambda: h_inward(i, begin))

    tick(1)
    slots = {1: [2], 4: [3], 7: [4], 9: [5], 11: [6], 13: [7], 15: [8]}
    h_slots = {11: [(0, 1)], 15: [(0, 2), (3, 1)]}

    @pl.loop(0, 16)
    def _(n):
        def past(v):
            return lax.div(n + 16 - v, 16)

        ph = past(7) + past(12) + past(15)
        t = n - 7 * past(7) - 5 * past(12) - 3 * past(15)
        left = 4 - ph
        over = lax.div(t, left)
        li = ph + over * (t - left + 1)
        lj = ph + (1 - over) * t
        pair(block_order(li), block_order(lj))
        pl.when((n == 6) | (n == 11) | (n == 14) | (n == 15))(lambda: finish(block_order(ph)))
        for s in range(16):
            todo = [lambda t=t: tick(t) for t in slots.get(s, ())]
            todo += [lambda i=i, d=d: h_mid(i, d) for i, d in h_slots.get(s, ())]

            @pl.when(n == s)
            def _(todo=todo):
                for op in todo:
                    op()

    @pl.loop(0, 4)
    def _(t):
        tc = cols(t * 256, 256)
        Wp[:, tc] = jnp.dot(dqkvT[...], h1[:, tc], preferred_element_type=F32).astype(BF)

    def core_copy(w):
        return remote(
            Wp.at[:, cols(w * 256 + (1 - c) * 128, 128)], Wc.at[w], wc_s.at[w], wc_r.at[w], (core, z)
        )

    for w in range(4):
        core_copy(w).start()
    tick(9)
    h_mid(3, 2)
    h_mid(1, 1)
    h_mid(2, 1)

    def both(w):
        Wc[w] = (Wc[w].astype(F32) + Wp[:, cols(w * 256 + c * 128, 128)].astype(F32)).astype(BF)

    for w in range(4):
        core_copy(w).wait_recv()
    both(chip_d)
    both(chip_b)
    wb_copy = [
        remote(Wc.at[where], Wb.at[slot], wb_s.at[slot], wb_r.at[slot], (b, z))
        for slot, where in ((0, chip_b), (1, chip_d))
    ]
    wb_copy[1].start()
    wb_copy[0].start()
    both(chip_a)
    both(chip)
    wa_copy = remote(Wc.at[chip_a], Wa, wa_s, wa_r, (a, z))
    for t in range(10, 14):
        tick(t)
    wb_copy[1].wait_recv()
    Wc[chip_a] = (Wc[chip_a].astype(F32) + Wb[1].astype(F32)).astype(BF)
    wa_copy.start()
    tick(14)
    tick(15)

    pl.when(z < 3)(lambda: h_wait(z))
    pl.when(z > 0)(lambda: remote(Hx, Hx, hu_s.at[0], hx_r, (core, z)).wait_recv())
    has_above, has_below = z < 3, z > 0

    @pl.when(has_above)
    def _():
        acc[...] = acc[...] + Hi[z].astype(F32)

    @pl.when(has_below)
    def _():
        acc[...] = acc[...] + Hx[...].astype(F32)

    @pl.loop(0, 8)
    def _(r):
        xhat, rstd = norm_rows(tok[chunk(r), :].astype(F32))
        e1 = acc[chunk(r), :] * gain1
        m1 = jnp.mean(e1, axis=-1, keepdims=True)
        m2 = jnp.mean(e1 * xhat, axis=-1, keepdims=True)
        dtok_o[chunk(r), :] = dX1[chunk(r), :] + rstd * (e1 - m1 - xhat * m2)

    wb_copy[0].wait_recv()
    wa_copy.wait_recv()
    total = Wc[chip].astype(F32) + Wb[0].astype(F32) + Wa[...].astype(F32)
    dot_one = jnp.zeros((1, 128), F32)
    for p in range(3):
        piece = total[p * 256 : (p + 1) * 256, :]
        dwq_o[p] = piece.T
        dot_one = dot_one + jnp.sum(piece * wqkv[p].T.astype(F32), axis=0, keepdims=True)
    for t in range(16, NU + 4):
        tick(t)
    for k_ in range(7):

        @pl.when(no(org))
        def _(k_=k_):
            ref = final(k_)[1]
            remote(ref, ref, fin_s.at[k_], fin_r.at[k_], (core, z)).wait_recv()

    part_two = jnp.sum(dwin_o[...] * w4[256 : 256 + 2 * HID, :].astype(F32), axis=0, keepdims=True)
    gz[z, 0:1, :] = dot_one / gains[dp, 0:1, :]
    gz[z, 1:2, :] = part_two / gains[dp, 1:2, :]
    gz[z, 2:8, :] = jnp.zeros((6, 128), F32)
    gain_copy = [
        remote(gz.at[z], gz.at[z], gz_s.at[n], gz_r.at[z], (dp, lax.rem(z + n, 4))) for n in range(1, 4)
    ]
    for cp in gain_copy:
        cp.start()
    for n in range(1, 4):
        o = lax.rem(z + n, 4)
        remote(gz.at[o], gz.at[o], gz_s.at[n], gz_r.at[o], (core, z)).wait_recv()
    dg_o[...] = gz[0] + gz[1] + gz[2] + gz[3]

    for cp in gain_copy:
        cp.wait_send()
    for w in range(4):
        core_copy(w).wait_send()
    wb_copy[0].wait_send()
    wb_copy[1].wait_send()
    wa_copy.wait_send()
    for i in range(4):
        h_inward(i, lambda cp: cp.wait_send())
    for c0 in range(2):
        for qi in range(2):
            pl.when(no(is_self(c0, qi)))(lambda c0=c0, qi=qi: att_back(c0, qi).wait_send())
    for e in range(NU):
        unit_b(e, 0).wait_send()
        unit_b(e, 1).wait_send()
        unit_a(e).wait_send()
        inward(e, lambda cp: cp.wait_send())

        @pl.when(z == target(e))
        def _(e=e):
            k_ = UNITS[e][1]
            gift, dst = final(k_)
            remote(gift, dst, fin_s.at[k_], fin_r.at[k_], (core, z)).wait_send()

    for d in range(1, 8):
        remote(gains_in, gains.at[dp], g_s.at[d], g_r.at[d], (core, z)).wait_send()
    for j in range(3):
        remote(wqkv, wq.at[:, own_rows], wr_s.at[j], wr_r.at[j], (core, z)).wait_send()
    for j in range(4):
        remote(wqkv, wq.at[:, own_rows], wx_s.at[j], wx_r.at[j], (core, z)).wait_send()
    pl.when(no(org))(lambda: hop.wait_send())
    cot_copy.wait_send()
    for n in range(3):
        att_copy(n, lax.rem(z + 1 + n, 4)).wait_send()
    pl.when(no(org))(lambda: att_copy(3, z).wait_send())


def run_layer(*args):
    V = pl.BlockSpec(memory_space=pltpu.VMEM)
    S = pl.BlockSpec(memory_space=pltpu.SMEM)
    dma = pltpu.SemaphoreType.DMA
    s = jax.ShapeDtypeStruct
    vm = pltpu.VMEM
    return pl.pallas_call(
        layer_kernel,
        out_shape=(
            s((256, 1024), BF), s((256, 1024), F32), s((3, 128, 256), F32), s((2 * HID, 128), F32),
            s((HID, 128), F32), s((256, 128), F32), s((8, 128), F32),
        ),
        in_specs=[S, S] + [V] * 6 + [pl.BlockSpec(memory_space=pl.ANY)],
        out_specs=[V] * 7,
        scratch_shapes=[
            vm((8, 8, 128), F32), vm((PACK, 128), BF), vm((1024, 128), F32), vm((1024, 128), F32),
            vm((1024, 128), F32), vm((8, 1024), F32), vm((1024, 256), BF), vm((1024, 256), BF),
            vm((1024, 256), BF), vm((4, 4, 8, 256), F32), vm((1024, 256), BF), vm((512, 512), BF),
            vm((1024, 1024), BF), vm((3, 1024, 256), BF), vm((512, 1024), BF),
            vm((2, PACK, 1024), BF), vm((256, 1024), F32), vm((1024, 1024), BF), vm((256, 1024), F32),
            vm((256, 1024), F32), vm((256, 1024), F32), vm((2, HID, 512), BF), vm((2, HID, 512), BF),
            vm((2, HID, 512), BF), vm((256, 1024), F32), vm((256, 1024), F32), vm((2, 512, 256), BF),
            vm((1024, 256), BF), vm((4, 4, 8, 256), F32),
            vm((1024, 256), F32), vm((1024, 256), F32), vm((1024, 256), F32),
            vm((4, 256, 1024), BF), vm((4, 256, 1024), BF), vm((256, 1024), BF), vm((2, 2, PACK, 256), BF),
            vm((2, PACK, 256), BF), vm((3, PACK, 256), BF), vm((PACK, 128), F32),
            vm((768, 1024), BF), vm((4, 768, 128), BF), vm((2, 768, 128), BF), vm((768, 128), BF), vm((4, 8, 128), F32),
            dma((4, 2)), dma((4, 2)), dma((4, 2)), dma((4, 2)),
            dma((3,)), dma((3,)), dma((4,)), dma((4,)), dma((8,)), dma((8,)), dma, dma, dma, dma,
            dma((2, 4)), dma((2, 4)), dma((2, 4)), dma((2, 4)), dma((2, 4)), dma((2, 4)),
            dma((2, 4)), dma((2, 2, 4)), dma((4,)), dma((2, 2)),
            dma, dma, dma, dma, dma, dma, dma, dma, dma, dma, dma((2, 2)), dma((4,)),
            dma((2, NU)), dma((2, NU)), dma((NU,)), dma((NU,)), dma((NU,)), dma((NU,)), dma((3, NU)),
            dma((7,)), dma((7,)), dma((4,)), dma((4,)), dma((4,)), dma,
            dma((4,)), dma((4,)), dma((2,)), dma((2,)), dma, dma, dma((4,)), dma((4,)), dma,
        ],
        compiler_params=pltpu.CompilerParams(
            collective_id=1, has_side_effects=True, vmem_limit_bytes=63 << 20
        ),
        name="layer",
    )(*args)


def local_fast(
    tokens, lengths, seq_order, gain_attn, w_qkv, w_attn_out, gain_mlp, w_in, w_mlp_out, cotangent
):
    half = HEAD_DIM // 2
    frequency = jnp.tile(rope_base ** (-2.0 * jnp.arange(half, dtype=F32) / HEAD_DIM), 4)
    sign = jnp.tile(jnp.repeat(jnp.array([-1.0, 1.0], F32), half), 2)
    rows = (gain_attn.astype(F32), gain_mlp.astype(F32), frequency, sign)
    gains = jnp.concatenate([r[None, :] for r in rows] + [jnp.zeros((4, 128), F32)], axis=0)
    out, d_tok, d_qkv, d_in, d_down, d_out, d_gain = run_layer(
        lengths, seq_order, tokens, w_qkv, w_in.transpose(1, 2, 0).reshape(2 * HID, 128), w_mlp_out, w_attn_out, gains, cotangent
    )
    return (out, d_tok, d_gain[0], d_qkv, d_out, d_gain[1], d_in.reshape(2, HID, 128).transpose(2, 0, 1), d_down)


def layer_norm(field_in, norm_gain):
    row_mean = jnp.mean(field_in, axis=-1, keepdims=True)
    centered = field_in - row_mean
    variance = jnp.mean(centered * centered, axis=-1, keepdims=True)
    return centered * lax.rsqrt(variance + norm_eps) * norm_gain


def rotate(field_in, position):
    half_size = field_in.shape[-1] // 2
    index_range = jnp.arange(half_size, dtype=jnp.float32)
    frequency = rope_base ** (-2.0 * index_range / field_in.shape[-1])
    angles = position[:, None] * frequency[None, :]
    cosine = jnp.cos(angles)[:, None, :]
    sine_part = jnp.sin(angles)[:, None, :]
    first_half = field_in[..., :half_size]
    second_half = field_in[..., half_size:]
    return jnp.concatenate(
        [
            first_half * cosine - second_half * sine_part,
            second_half * cosine + first_half * sine_part,
        ],
        axis=-1,
    )


def geglu(act_part, up_part):
    return jax.nn.gelu(act_part, approximate=False) * up_part


def layout(lengths, seq_order, group_rows):
    seq_total = seq_order.shape[0]
    first_seq = lax.axis_index("dp") * SEQ_GRP
    chosen = lax.dynamic_slice_in_dim(seq_order, first_seq, SEQ_GRP)
    matched = chosen[:, None] == jnp.arange(seq_total, dtype=jnp.int32)[None, :]
    dealt_lengths = jnp.sum(jnp.where(matched, lengths[None, :], 0), axis=1)
    seq_ends = jnp.cumsum(dealt_lengths)
    row_index = jnp.arange(group_rows, dtype=jnp.int32)
    passed = row_index[:, None] >= seq_ends[None, :]
    segment = jnp.sum(passed.astype(jnp.int32), axis=1)
    row_start = jnp.sum(jnp.where(passed, dealt_lengths[None, :], 0), axis=1)
    return (segment, (row_index - row_start).astype(jnp.float32))


def item_layout(array_in, block_rows):
    group_rows, head_count, head_size = array_in.shape
    block_count = group_rows // block_rows
    shaped = array_in.reshape(block_count, block_rows, head_count, head_size)
    return shaped.transpose(2, 0, 1, 3).reshape(head_count * block_count, block_rows, head_size)


def from_items(items, group_rows):
    item_count, block_rows, head_size = items.shape
    block_count = group_rows // block_rows
    head_count = item_count // block_count
    shaped = items.reshape(head_count, block_count, block_rows, head_size)
    return shaped.transpose(1, 2, 0, 3).reshape(group_rows, head_count, head_size)


def masked_scores(query_block, key_head, segment_block, segment):
    score_scale = query_block.shape[-1] ** (-0.5)
    raw_scores = lax.dot_general(
        query_block, key_head, (((1,), (1,)), ((), ())), preferred_element_type=jnp.float32
    )
    allowed = segment_block[:, None] == segment[None, :]
    return jnp.where(allowed, raw_scores * score_scale, masked_fill)


def attend_forward(query_rot, key_rot, value_low, segment, block_rows):
    group_rows, head_count, head_size = query_rot.shape
    block_count = group_rows // block_rows
    query_items = item_layout(query_rot, block_rows)
    key_heads = key_rot.transpose(1, 0, 2)
    value_heads = value_low.transpose(1, 0, 2)
    segment_blocks = segment.reshape(block_count, block_rows)

    def one_item(item_index):
        head_index = item_index // block_count
        block_index = item_index % block_count
        query_block = lax.dynamic_index_in_dim(query_items, item_index, 0, False)
        key_head = lax.dynamic_index_in_dim(key_heads, head_index, 0, False)
        value_head = lax.dynamic_index_in_dim(value_heads, head_index, 0, False)
        segment_block = lax.dynamic_index_in_dim(segment_blocks, block_index, 0, False)
        scores = masked_scores(query_block, key_head, segment_block, segment)
        row_top = jnp.max(scores, axis=1, keepdims=True)
        weights = jnp.exp(scores - row_top)
        row_total = jnp.sum(weights, axis=1, keepdims=True)
        probs_low = (weights / row_total).astype(jnp.bfloat16)
        result = jnp.dot(probs_low, value_head, preferred_element_type=jnp.float32)
        return (result, row_top[:, 0] + jnp.log(row_total[:, 0]))

    results, log_totals = lax.map(one_item, jnp.arange(head_count * block_count, dtype=jnp.int32))
    return (from_items(results, group_rows), log_totals)


def attend_backward(query_rot, key_rot, value_low, grad_out, log_totals, segment, block_rows):
    group_rows, head_count, head_size = query_rot.shape
    block_count = group_rows // block_rows
    score_scale = head_size ** (-0.5)
    query_items = item_layout(query_rot, block_rows)
    grad_items = item_layout(grad_out, block_rows)
    key_heads = key_rot.transpose(1, 0, 2)
    value_heads = value_low.transpose(1, 0, 2)
    segment_blocks = segment.reshape(block_count, block_rows)

    def one_item(carried, item_index):
        key_grads, value_grads = carried
        head_index = item_index // block_count
        block_index = item_index % block_count
        query_block = lax.dynamic_index_in_dim(query_items, item_index, 0, False)
        grad_block = lax.dynamic_index_in_dim(grad_items, item_index, 0, False)
        log_row = lax.dynamic_index_in_dim(log_totals, item_index, 0, False)
        key_head = lax.dynamic_index_in_dim(key_heads, head_index, 0, False)
        value_head = lax.dynamic_index_in_dim(value_heads, head_index, 0, False)
        segment_block = lax.dynamic_index_in_dim(segment_blocks, block_index, 0, False)
        scores = masked_scores(query_block, key_head, segment_block, segment)
        prob_full = jnp.exp(scores - log_row[:, None])
        probs_low = prob_full.astype(jnp.bfloat16)
        grad_probs = lax.dot_general(
            grad_block, value_head, (((1,), (1,)), ((), ())), preferred_element_type=jnp.float32
        )
        row_delta = jnp.sum(prob_full * grad_probs, axis=1, keepdims=True)
        grad_scores = (prob_full * (grad_probs - row_delta)).astype(jnp.bfloat16)
        grad_query = (
            jnp.dot(grad_scores, key_head, preferred_element_type=jnp.float32) * score_scale
        )
        grad_key = (
            lax.dot_general(
                grad_scores,
                query_block,
                (((0,), (0,)), ((), ())),
                preferred_element_type=jnp.float32,
            )
            * score_scale
        )
        grad_value = lax.dot_general(
            probs_low, grad_block, (((0,), (0,)), ((), ())), preferred_element_type=jnp.float32
        )
        key_grads = lax.dynamic_update_index_in_dim(
            key_grads,
            lax.dynamic_index_in_dim(key_grads, head_index, 0, False) + grad_key,
            head_index,
            0,
        )
        value_grads = lax.dynamic_update_index_in_dim(
            value_grads,
            lax.dynamic_index_in_dim(value_grads, head_index, 0, False) + grad_value,
            head_index,
            0,
        )
        return ((key_grads, value_grads), grad_query)

    zero_heads = jnp.zeros((head_count, group_rows, head_size), jnp.float32)
    (key_grads, value_grads), query_grads = lax.scan(
        one_item, (zero_heads, zero_heads), jnp.arange(head_count * block_count, dtype=jnp.int32)
    )
    return (
        from_items(query_grads, group_rows),
        key_grads.transpose(1, 0, 2),
        value_grads.transpose(1, 0, 2),
    )


def spread_rows(local_rows):
    return lax.all_gather(local_rows, "tensor", axis=0, tiled=True)


def spread_grads(local_grads):
    return lax.all_gather(local_grads, "tensor", axis=0, tiled=True)


def sum_heads(activations, weight_part, row_count):

    def row_term(first_row, row_number):
        return jnp.dot(activations, weight_part, preferred_element_type=jnp.float32)

    return lax.psum_scatter(
        row_term(jnp.int32(0), row_count * lax.axis_size("tensor")),
        "tensor",
        scatter_dimension=0,
        tiled=True,
    )


def sum_grads(grads_low, weight_full, einsum_form, row_count):

    def row_term(first_row, row_number):
        return jnp.einsum(einsum_form, grads_low, weight_full, preferred_element_type=jnp.float32)

    return lax.psum_scatter(
        row_term(jnp.int32(0), row_count * lax.axis_size("tensor")),
        "tensor",
        scatter_dimension=0,
        tiled=True,
    )


def local_plain(
    tokens, lengths, seq_order, gain_attn, w_qkv, w_attn_out, gain_mlp, w_in, w_mlp_out, cotangent
):
    row_count = tokens.shape[0]
    group_rows = row_count * lax.axis_size("tensor")
    block_rows = min(512, group_rows)
    segment, position = layout(lengths, seq_order, group_rows)
    gain_low_one, qkv_weight, out_weight, gain_low_two, in_weight, down_weight = (
        lax.all_gather(gain_attn, "dp", axis=0, tiled=True),
        lax.all_gather(w_qkv, "dp", axis=1, tiled=True),
        lax.all_gather(w_attn_out, "dp", axis=1, tiled=True),
        lax.all_gather(gain_mlp, "dp", axis=0, tiled=True),
        lax.all_gather(w_in, "dp", axis=0, tiled=True),
        lax.all_gather(w_mlp_out, "dp", axis=1, tiled=True),
    )
    gain_one = gain_low_one.astype(jnp.float32)
    gain_two = gain_low_two.astype(jnp.float32)
    residual = tokens.astype(jnp.float32)
    normed_one = spread_rows(layer_norm(residual, gain_one).astype(jnp.bfloat16))
    qkv = jnp.einsum("rd,pdc->rpc", normed_one, qkv_weight, preferred_element_type=jnp.float32)
    head_count = qkv.shape[2] // HEAD_DIM
    head_shape = (group_rows, head_count, HEAD_DIM)
    query_rot = rotate(qkv[:, 0].reshape(head_shape), position).astype(jnp.bfloat16)
    key_rot = rotate(qkv[:, 1].reshape(head_shape), position).astype(jnp.bfloat16)
    value_low = qkv[:, 2].reshape(head_shape).astype(jnp.bfloat16)
    attended, log_totals = attend_forward(query_rot, key_rot, value_low, segment, block_rows)
    attn_low = attended.reshape(group_rows, head_count * HEAD_DIM).astype(jnp.bfloat16)
    resid_mid = residual + sum_heads(attn_low, out_weight, row_count)
    normed_two = spread_rows(layer_norm(resid_mid, gain_two).astype(jnp.bfloat16))
    gate_up = jnp.einsum("rd,dpc->rpc", normed_two, in_weight, preferred_element_type=jnp.float32)
    hidden = geglu(gate_up[:, 0], gate_up[:, 1]).astype(jnp.bfloat16)
    output = (resid_mid + sum_heads(hidden, down_weight, row_count)).astype(jnp.bfloat16)
    grad_two = spread_grads(cotangent)
    d_hidden = lax.dot_general(
        grad_two, down_weight, (((1,), (1,)), ((), ())), preferred_element_type=jnp.float32
    )
    d_down = lax.dot_general(
        hidden, grad_two, (((0,), (0,)), ((), ())), preferred_element_type=jnp.float32
    )
    geglu_pull = jax.vjp(geglu, gate_up[:, 0], gate_up[:, 1])[1]
    d_act, d_up = geglu_pull(d_hidden)
    d_gate_up = jnp.stack([d_act, d_up], axis=1).astype(jnp.bfloat16)
    d_in = jnp.einsum("rd,rpc->dpc", normed_two, d_gate_up, preferred_element_type=jnp.float32)
    d_normed_two = sum_grads(d_gate_up, in_weight, "rpc,dpc->rd", row_count)
    norm_pull_two = jax.vjp(layer_norm, resid_mid, gain_two)[1]
    d_mid_norm, d_gain_two = norm_pull_two(d_normed_two)
    d_mid = cotangent.astype(jnp.float32) + d_mid_norm
    grad_one = spread_grads(d_mid.astype(jnp.bfloat16))
    d_out = lax.dot_general(
        attn_low, grad_one, (((0,), (0,)), ((), ())), preferred_element_type=jnp.float32
    )
    d_att = lax.dot_general(
        grad_one, out_weight, (((1,), (1,)), ((), ())), preferred_element_type=jnp.float32
    ).astype(jnp.bfloat16)
    d_query_rot, d_key_rot, d_value = attend_backward(
        query_rot, key_rot, value_low, d_att.reshape(head_shape), log_totals, segment, block_rows
    )
    rotate_pull = jax.vjp(lambda field_in: rotate(field_in, position), d_query_rot)[1]
    d_query = rotate_pull(d_query_rot)[0]
    d_key = rotate_pull(d_key_rot)[0]
    flat_shape = (group_rows, head_count * HEAD_DIM)
    d_qkv = jnp.stack(
        [d_query.reshape(flat_shape), d_key.reshape(flat_shape), d_value.reshape(flat_shape)],
        axis=1,
    ).astype(jnp.bfloat16)
    d_qkv_weight = jnp.einsum("rd,rpc->pdc", normed_one, d_qkv, preferred_element_type=jnp.float32)
    d_normed_one = sum_grads(d_qkv, qkv_weight, "rpc,pdc->rd", row_count)
    norm_pull_one = jax.vjp(layer_norm, residual, gain_one)[1]
    d_first, d_gain_one = norm_pull_one(d_normed_one)
    d_tokens = d_mid + d_first
    gain_sums = lax.psum((d_gain_one, d_gain_two), "tensor")
    shares = (
        lax.psum_scatter(gain_sums[0], "dp", scatter_dimension=0, tiled=True),
        lax.psum_scatter(d_qkv_weight, "dp", scatter_dimension=1, tiled=True),
        lax.psum_scatter(d_out, "dp", scatter_dimension=1, tiled=True),
        lax.psum_scatter(gain_sums[1], "dp", scatter_dimension=0, tiled=True),
        lax.psum_scatter(d_in, "dp", scatter_dimension=0, tiled=True),
        lax.psum_scatter(d_down, "dp", scatter_dimension=1, tiled=True),
    )
    return (output, d_tokens, shares[0], shares[1], shares[2], shares[3], shares[4], shares[5])


def solution(mesh):
    fast = mesh.shape["dp"] == 8 and mesh.shape["tensor"] == 4
    return jax.shard_map(
        local_fast if fast else local_plain,
        mesh=mesh,
        in_specs=(
            P(("dp", "tensor"), None),
            P(),
            P(),
            P("dp"),
            P(None, "dp", "tensor"),
            P("tensor", "dp"),
            P("dp"),
            P("dp", None, "tensor"),
            P("tensor", "dp"),
            P(("dp", "tensor"), None),
        ),
        out_specs=(
            P(("dp", "tensor"), None),
            P(("dp", "tensor"), None),
            P("dp"),
            P(None, "dp", "tensor"),
            P("tensor", "dp"),
            P("dp"),
            P("dp", None, "tensor"),
            P("tensor", "dp"),
        ),
        check_vma=False,
    )
```

time: 311 us -> 261 us (0.84)
  Pallas kernels: 289 us -> 250 us
  other arithmetic: 8.15 us -> 0.01 us
    pallas_call x2 -> x1, Pallas kernels: 289 us -> 250 us  [run_layer(): pl.pallas_call(layer_kernel, out_shape=(s((256, 1024), BF), s((256, 1024)...]
    slice x3 -> x0, local copies, waits for them, and re-layouts: 5.41 us -> none  [the longest x1 2.07 us: local_fast(): d_in = d_pack[:2 * HID].reshape(2, HID, 128).transpose(2, 0, 1)]
    unnamed x9 -> x22, local copies, waits for them, and re-layouts: 2.78 us -> 7.65 us
    concatenate x3 -> x0, other arithmetic: 4.45 us -> none  [the longest x1 1.94 us: prepare(): jnp.concatenate([w_in.transpose(1, 2, 0).reshape(2 * HID, 128), w_mlp_out...]
where the time goes in v2:
time: 261 us
  Pallas kernels  250 us (96%)
  local copies, waits for them, and re-layouts  9.86 us (4%)
    pallas_call x1, Pallas kernels, run_layer(): pl.pallas_call(layer_kernel, out_shape=(s((256, 1024), BF), s((256, 1024)...  250 us
    unnamed x22, local copies, waits for them, and re-layouts  7.65 us

profile of v2, /device:TPU:0, one launch (start us, length us, event | category | flops | bytes accessed | tf_op | source)
XLA Modules:
  0.0 261.0 jit_solution(5502597437712167106)
XLA Ops:
  0.6 0.0 copy-start.7
  0.7 0.6 copy-done.7
  1.3 0.1 broadcast_in_dim.22
  1.4 0.1 tile.14
  1.5 0.0 copy-start.5
  1.5 0.1 broadcast_in_dim_tile.7
  1.5 0.6 copy-done.5
  2.1 0.0 copy-done.6
  2.1 0.1 broadcast_in_dim_tile.6
  2.2 0.6 concatenate.3.gains_in
  2.8 250.5 %layer.1 = (bf16[256,1024]{1,0:T(8,128)(2,1)}, f32[256,1024]{1,0:T(8,128)}, f32[3,128,256]{2,1,0:T(8,128)}, f32[1312,128]{1,0:T(8,128)}, f32[656,128]{1,0:T(8,12...) custom-call(s32[32]{0:T(128)} %lengths.1, s32[32]{0:T(128)} %seq_order.1, bf16[256,1024]{1,0:T(8,128)(2,1)} %tok.1, ...), custom_call_target="tpu_custom_call" | custom-call | tf_op jit(solution)/shard_map/layer/pallas_call | solution.py:974
  253.3 0.0 copy-start
  253.3 1.3 slice_bitcast_fusion
  254.6 1.9 copy.25
  256.5 0.0 copy-done
  256.5 1.0 copy.26
  257.5 0.3 copy-done.2
  257.7 0.7 copy.27
  258.5 0.0 copy-done.4
  258.5 0.7 copy.28
  259.1 0.0 copy-done.1
  259.1 0.8 copy.29
  260.0 0.3 copy-done.3
  260.3 0.7 copy.30
  (10 shorter events, 0.0 us)
Async XLA Ops:
  0.6 0.7 copy-start.7
  1.5 0.7 copy-start.5
  1.5 0.7 copy-start.6
  253.3 3.2 %copy-start = (f32[256,1024]{1,0:T(8,128)S(1)}, f32[256,1024]{1,0:T(8,128)}, u32[]{:S(2)}) copy-start(f32[256,1024]{1,0:T(8,128)} %get-tuple-element.35) | copy-start | bytes 3145732
  256.5 1.2 copy-start.2
  256.5 2.0 copy-start.4
  257.7 1.4 copy-start.1
  259.1 1.2 copy-start.3

commit v3 on v2

--- a/solution.py
+++ b/solution.py
@@ -84,12 +84,12 @@
 
 
 HID = 656
-PACK = 3 * HID + 256
-ROWS = ((256, HID), (256 + HID, HID), (256 + 2 * HID, HID), (0, 256))
-CUTS = ((0, 544), (544, 560), (1104, 560), (1664, 560))
-HALVES = tuple((m, o, n) for m in (2, 0, 1) for o, n in ((0, 336), (336, 320))) + ((3, 0, 256),)
-UNITS = tuple((q, k) for q in range(2) for k in range(6)) + ((0, 6), (1, 6))
-NU = len(UNITS)
+FF3 = 3 * HID
+FROWS = ((0, HID), (HID, HID), (2 * HID, HID))
+CUTS = ((0, 496), (496, 496), (992, 496), (1488, 480))
+HALVES = tuple((m, o, n) for m in (2, 0, 1) for o, n in ((0, 336), (336, 320)))
+NF = len(HALVES)
+NU = NF + 2
 INV_SQRT2 = 0.7071067811865476
 INV_SQRT_2PI = 0.3989422804014327
 
@@ -97,13 +97,14 @@
 def layer_kernel(
     lengths, seq_order, tok, wqkv, win, wmlp, wout, gains_in, cot,
     out_o, dtok_o, dwq_o, dwin_o, dwmlp_o, dwout_o, dg_o,
-    gains, w4, cs, sn, segc, segr, q, k, v, lse, att, attn2, h1, wq, cot2,
-    G, X1, pool, yr, dr, acc, hidT, daT, duT, dX1, dxo, dsend, datt, delta,
-    dq, dk, dv, Hs, Hi, Hx, Rb, Ra, Z, give, Wp, Wc, Wb, Wa, gz,
-    us, ds, rb, ra, wr_s, wr_r, wx_s, wx_r, g_s, g_r, co_s, co_r, hop_s, hop_r,
-    qu_s, qd_s, q_r, pa_s, pb_s, pf_s, pa_r, pb_r, at_s, at_r,
-    y_s, y_r, h_s, h_r, d_s, d_r, u_s, u_r, e_s, e_r, t_s, t_r,
-    b_s, b_r, a_s, a_r, zu_s, zd_s, z_r, fin_s, fin_r,
+    gains, w3, cs, sn, segc, segr, q, k, v, lse, att, attn2, h1, wq, cot4,
+    G, Wo, X1, h2a, dya, yr, acc, hidT, daT, duT, dX1, dsb, dr, dzs, dzr, usb, ur, uzs, uzr, dsend, datt, delta,
+    dq, dk, dv, Hs, Hi, Hx, Rb, Ra, Z, Rbo, Rao, Zo, give, Wp, Wc, Wb, Wa, gz,
+    us, ds, rb, ra, wr_s, wr_r, wx_s, wx_r, g_s, g_r, cx_s, cx_r, hop_s, hop_r,
+    ou_s, o_r, oa_s, ob_s, of_s, oa_r, ob_r,
+    fz_s, fz_r, pa_s, pb_s, pf_s, pa_r, pb_r, at_s, at_r,
+    y_s, y_r, n_s, n_r, d_s, d_r, u_s, u_r, e_s, e_r, t_s, t_r,
+    b_s, b_r, a_s, a_r, zu_s, z_r, fin_s, fin_r,
     hu_s, hd_s, hi_r, hx_r, wc_s, wc_r, wb_s, wb_r, wa_s, wa_r, gz_s, gz_r, lc,
 ):
     dp, z, c, x, y = place()
@@ -117,12 +118,18 @@
     home = lax.div(z, 2)
     org = c == home
     zq = lax.rem(z, 2)
+    zp = z + 1 - 2 * zq
+    z2 = z + 2 - 4 * home
     end = (z == 0) | (z == 3)
     own = cols(c * 256, 256)
     other = cols((1 - c) * 256, 256)
-    tall, vT, ur, oT = Hs, Hx, yr, acc.at[:, 0:256]
-    h2a, dya, dqkvT = pool.at[0:512], pool.at[512:1024], pool.at[0:768]
-    dw4 = (dwin_o.at[0:HID], dwin_o.at[HID : 2 * HID], dwmlp_o, dwout_o)
+
+    def block(core_bit, line_bit):
+        return cols((2 * line_bit + core_bit) * 256, 256)
+
+    ob, cb, zb, db = block(c, zq), block(1 - c, zq), block(c, 1 - zq), block(1 - c, 1 - zq)
+    tall, vT, oT, dqkvT = Hs, Hx, acc.at[:, 0:256], h2a.at[0:768]
+    dw4 = (dwin_o.at[0:HID], dwin_o.at[HID : 2 * HID], dwmlp_o)
     greet(dp, z, bits)
 
     def no(cond):
@@ -154,81 +161,105 @@
     for j, d in enumerate((2, 4, 6)):
         remote(wqkv, wq.at[:, own_rows], wr_s.at[j], wr_r.at[j], (flip(dp, bits, d), z)).start()
     remote(wqkv, wq.at[:, own_rows], wx_s.at[3], wx_r.at[3], (core, z)).start()
-    cot_copy = remote(cot, cot2.at[own], co_s, co_r, (core, z))
-    cot_copy.start()
-    cot_local = pltpu.make_async_copy(cot, cot2.at[own], lc)
+    cot_copy = (
+        remote(cot, cot4.at[ob], cx_s.at[0], cx_r.at[0], (core, z)),
+        remote(cot, cot4.at[ob], cx_s.at[1], cx_r.at[1], (dp, zp)),
+        remote(cot4.at[zb], cot4.at[zb], cx_s.at[2], cx_r.at[2], (core, z)),
+    )
+    cot_copy[0].start()
+    cot_local = pltpu.make_async_copy(cot, cot4.at[ob], lc)
     cot_local.start()
 
-    w4[0:256, :] = wout[...]
-    w4[256 : 256 + 2 * HID, :] = win[...]
-    w4[256 + 2 * HID : PACK, :] = wmlp[...]
-    mine = G.at[zq, :, cols(dp * 128, 128)]
-    hop = remote(w4, mine, hop_s, hop_r, (core, z))
-    pl.when(no(org))(lambda: hop.start())
+    w3[0 : 2 * HID, :] = win[...]
+    w3[2 * HID : FF3, :] = wmlp[...]
+    lanes = cols(dp * 128, 128)
+    hop = (
+        remote(w3, G.at[:, lanes], hop_s.at[0], hop_r.at[0], (core, z)),
+        remote(wout, Wo.at[zq, :, lanes], hop_s.at[1], hop_r.at[1], (core, z)),
+    )
+
+    @pl.when(no(org))
+    def _():
+        hop[1].start()
+        hop[0].start()
 
     @pl.when(org)
     def _():
-        G[zq, :, cols(dp * 128, 128)] = w4[...]
+        G[:, lanes] = w3[...]
+        Wo[zq, :, lanes] = wout[...]
 
     gains[dp] = gains_in[...]
     wq[:, own_rows, :] = wqkv[...]
     tall[z] = tok[...]
     cot_local.wait()
 
-    def piece(qi, u, where):
+    def begin(cp):
+        cp.start()
+
+    def done(cp):
+        cp.wait_send()
+
+    def piece(u, where):
         r0, n = CUTS[u]
-        return G.at[qi, pl.ds(r0, n), cols(where * 256, 256)]
-
-    def line_send(qi, u, up, act):
-        ref = piece(qi, u, chip)
-        if up:
-            pl.when((z >= 2 * c + qi) & (z < 3))(
-                lambda: act(remote(ref, ref, qu_s.at[qi, u], q_r.at[qi, u], (dp, z + 1)))
-            )
-        else:
-            pl.when((z <= 2 * c + qi) & (z > 0))(
-                lambda: act(remote(ref, ref, qd_s.at[qi, u], q_r.at[qi, u], (dp, z - 1)))
-            )
-
-    def plane_a(qi, u):
-        return remote(piece(qi, u, chip), piece(qi, u, chip), pa_s.at[qi, u], pa_r.at[qi, u], (a, z))
-
-    def plane_b(qi, u):
-        return remote(piece(qi, u, chip), piece(qi, u, chip), pb_s.at[qi, u], pb_r.at[qi, 0, u], (b, z))
-
-    def plane_f(qi, u):
-        return remote(piece(qi, u, chip_a), piece(qi, u, chip_a), pf_s.at[qi, u], pb_r.at[qi, 1, u], (b, z))
-
-    def spread(qi, u):
-        plane_a(qi, u).start()
-        plane_b(qi, u).start()
+        return G.at[pl.ds(r0, n), cols(where * 256, 256)]
+
+    def plane_a(u):
+        return remote(piece(u, chip), piece(u, chip), pa_s.at[u], pa_r.at[u], (a, z))
+
+    def plane_b(u):
+        return remote(piece(u, chip), piece(u, chip), pb_s.at[u], pb_r.at[0, u], (b, z))
+
+    def plane_f(u):
+        return remote(piece(u, chip_a), piece(u, chip_a), pf_s.at[u], pb_r.at[1, u], (b, z))
+
+    def leap(u):
+        return remote(piece(u, chip), piece(u, chip), fz_s.at[u], fz_r.at[u], (dp, z2))
+
+    def spread(u):
+        plane_a(u).start()
+        plane_b(u).start()
+
+    def across(u):
+        ref = piece(u, chip_a)
+        remote(ref, ref, pa_s.at[u], pa_r.at[u], (a, z)).wait_recv()
+        plane_f(u).start()
+
+    def land(u):
+        leap(u).wait_recv()
+        spread(u)
 
     near = (1 - c) * lax.div(z + 2, 3) + c * lax.div(z, 3)
     far = 1 - near
 
-    def begin(cp):
-        cp.start()
-
-    def arrive(qi, u):
-        ref = piece(qi, u, chip)
-        remote(ref, ref, qu_s.at[qi, u], q_r.at[qi, u], (core, z)).wait_recv()
-
-    def across(qi, u):
-        ref = piece(qi, u, chip_a)
-        remote(ref, ref, pa_s.at[qi, u], pa_r.at[qi, u], (a, z)).wait_recv()
-        plane_f(qi, u).start()
-
-    def stage(qi, u):
-        arrive(qi, u)
-        line_send(qi, u, True, begin)
-        line_send(qi, u, False, begin)
-        spread(qi, u)
-
-    def stage_far(u):
-        stage(far, u)
-
-    def stage_near(u):
-        stage(near, u)
+    def opiece(qi, where):
+        return Wo.at[qi, :, cols(where * 256, 256)]
+
+    def ofar(k_):
+        ref = opiece(zq, chip)
+        return remote(ref, ref, ou_s.at[k_], o_r.at[zq], (dp, lax.rem(z + k_, 4)))
+
+    def oplane(qi):
+        ref, ref_a = opiece(qi, chip), opiece(qi, chip_a)
+        return (
+            remote(ref, ref, oa_s.at[qi], oa_r.at[qi], (a, z)),
+            remote(ref, ref, ob_s.at[qi], ob_r.at[0, qi], (b, z)),
+            remote(ref_a, ref_a, of_s.at[qi], ob_r.at[1, qi], (b, z)),
+        )
+
+    def ospread(qi):
+        cps = oplane(qi)
+        cps[0].start()
+        cps[1].start()
+
+    def oland(qi):
+        ref = opiece(qi, chip)
+        remote(ref, ref, ou_s.at[1], o_r.at[qi], (core, z)).wait_recv()
+        ospread(qi)
+
+    def oacross(qi):
+        ref = opiece(qi, chip_a)
+        remote(ref, ref, oa_s.at[qi], oa_r.at[qi], (a, z)).wait_recv()
+        oplane(qi)[2].start()
 
     ends, starts, total = [], [], 0
     for j in range(SEQ_GRP):
@@ -254,15 +285,11 @@
 
     @pl.when(org)
     def _():
-        remote(w4, G.at[zq, :, cols(core * 128, 128)], hop_s, hop_r, (core, z)).wait_recv()
+        remote(wout, Wo.at[zq, :, cols(core * 128, 128)], hop_s.at[1], hop_r.at[1], (core, z)).wait_recv()
+        ospread(near)
+        remote(w3, G.at[:, cols(core * 128, 128)], hop_s.at[0], hop_r.at[0], (core, z)).wait_recv()
         for u in range(4):
-            spread(near, u)
-
-    @pl.when(org)
-    def _():
-        for u in range(4):
-            pl.when((z == 0) | (z == 2))(lambda u=u: line_send(near, u, True, begin))
-            pl.when((z == 1) | (z == 3))(lambda u=u: line_send(near, u, False, begin))
+            spread(u)
 
     for j, d in enumerate((2, 4, 6)):
         p = flip(dp, bits, d)
@@ -313,14 +340,6 @@
                     if k_ < 3:
                         pl.when(down_ok(k_))(lambda: tok_down(k_, h).start())
 
-        if k_ == 1:
-
-            @pl.when(org & no(end))
-            def _():
-                for u in range(4):
-                    pl.when(z == 1)(lambda u=u: line_send(near, u, True, begin))
-                    pl.when(z == 2)(lambda u=u: line_send(near, u, False, begin))
-
         @pl.loop(0, 2)
         def _(t, k_=k_):
             s = z - k_ + 2 * k_ * t
@@ -330,30 +349,18 @@
 
             @pl.when(org)
             def _():
+                oacross(near)
                 for u in range(4):
-                    across(near, u)
-                for u in range(3):
-                    stage_far(u)
+                    across(u)
 
         if k_ == 2:
 
-            @pl.when(org)
+            @pl.when(org & end)
             def _():
-                stage_far(3)
-                across(far, 0)
-                across(far, 1)
-
-            @pl.when(no(org) & no(end))
-            def _():
-                stage_near(0)
-                stage_near(1)
-
-        if k_ == 3:
-
-            @pl.when(org)
-            def _():
-                across(far, 2)
-                across(far, 3)
+                for n in range(1, 4):
+                    ofar(n).start()
+                for u in range(4):
+                    leap(u).start()
 
     for s in range(4):
         vT[:, s * 256 : (s + 1) * 256] = v[s * 256 : (s + 1) * 256, :].T
@@ -411,36 +418,33 @@
         def _():
             attn2[own, cols(zq * 256, 256)] = att[pl.ds(pl.multiple_of(z * 256, 256), 256), :]
 
-        sf, sn_, af, an = stage_far, stage_near, lambda u: across(far, u), lambda u: across(near, u)
-        plans = (
-            (no(org) & no(end), (((sn_, 2), (sn_, 3)), ((sf, 0), (sf, 1), (an, 0), (an, 1)),
-                                 ((sf, 2), (an, 2), (an, 3)), ((sf, 3), (af, 0), (af, 1)))),
-            (no(org) & end, (((sn_, 0),), ((sn_, 1), (sn_, 2)), ((sn_, 3), (an, 0), (an, 1)),
-                             ((sf, 0), (an, 2)))),
-        )
-        for who, plan in plans:
-            for m, ops in enumerate(plan):
-
-                @pl.when(who & (n == m))
-                def _(ops=ops):
-                    for op, u in ops:
-                        op(u)
-
-    @pl.when(no(org) & no(end))
+        @pl.when((n == 0) & org & no(end))
+        def _():
+            for m in range(1, 4):
+                ofar(m).start()
+            for u in range(4):
+                leap(u).start()
+
+        pl.when(n == 1)(lambda: cot_copy[1].start())
+
+    @pl.when(org)
     def _():
-        across(far, 2)
-        across(far, 3)
-
-    @pl.when(no(org) & end)
+        oland(far)
+        oacross(far)
+
+    @pl.when(no(org))
     def _():
-        stage_far(1)
-        across(near, 3)
-        across(far, 0)
-        stage_far(2)
-        across(far, 1)
-        stage_far(3)
-        across(far, 2)
-        across(far, 3)
+        land(0)
+        oland(near)
+        oland(far)
+        for u in range(1, 4):
+            land(u)
+        oacross(near)
+        oacross(far)
+        across(0)
+
+    def late_across(u):
+        pl.when(no(org))(lambda: across(u))
 
     for k_ in range(3):
         for h in range(2):
@@ -455,29 +459,20 @@
                 slot = att_slot(src, qi)
                 remote(slot, slot, at_s.at[0], at_r.at[src, qi], (core, z)).wait_recv()
 
-    def pack_wait(u):
-        for qi in range(2):
-            for w, where in enumerate((chip_b, chip_d)):
-                ref = piece(qi, u, where)
-                remote(ref, ref, pb_s.at[qi, u], pb_r.at[qi, w, u], (b, z)).wait_recv()
-
-    def w_rows(qi, m):
-        r0, n = ROWS[m]
-        return pl.ds(r0, n)
-
-    pack_wait(0)
+    for qi in range(2):
+        for w, where in enumerate((chip_b, chip_d)):
+            ref = opiece(qi, where)
+            remote(ref, ref, ob_s.at[qi], ob_r.at[w, qi], (core, z)).wait_recv()
 
     def out_proj(rows):
         return sum(
-            jnp.dot(
-                attn2[rows, qi * 256 : (qi + 1) * 256], G[qi, w_rows(qi, 3), :], preferred_element_type=F32
-            )
-            for qi in range(2)
+            jnp.dot(attn2[rows, qi * 256 : (qi + 1) * 256], Wo[qi], preferred_element_type=F32) for qi in range(2)
         )
 
     acc[...] = out_proj(other)
     y_copy = remote(acc, yr, y_s, y_r, (core, z))
     y_copy.start()
+    late_across(1)
     X1[...] = tok[...].astype(F32) + out_proj(own)
     y_copy.wait()
 
@@ -486,207 +481,237 @@
 
     def own_chunk(r):
         return pl.ds(pl.multiple_of(c * 256 + r * 32, 32), 32)
+
+    def block_chunk(r):
+        return pl.ds(pl.multiple_of((2 * zq + c) * 256 + r * 32, 32), 32)
 
     @pl.loop(0, 8)
     def _(r):
         x1 = X1[chunk(r), :] + yr[chunk(r), :]
         X1[chunk(r), :] = x1
         xhat, _r = norm_rows(x1)
-        h2a[own_chunk(r), :] = (xhat * gain2).astype(BF)
-
-    h_copy = remote(h2a.at[own], h2a.at[own], h_s, h_r, (core, z))
-    h_copy.start()
-    remote(cot, cot2.at[other], co_s, co_r, (core, z)).wait_recv()
-    for u in range(1, 4):
-        pack_wait(u)
-    h_copy.wait()
-
-    TILES = ((0, 224), (224, 224), (448, 208))
-    for r0, n in TILES:
-
-        @pl.loop(0, 2)
-        def _(qi, r0=r0, n=n):
-            h2 = h2a[...]
-            act = lax.dot_general(G[qi, pl.ds(ROWS[0][0] + r0, n), :], h2, NT, preferred_element_type=F32)
-            up = lax.dot_general(G[qi, pl.ds(ROWS[1][0] + r0, n), :], h2, NT, preferred_element_type=F32)
-            dh = lax.dot_general(G[qi, pl.ds(ROWS[2][0] + r0, n), :], cot2[...], NT, preferred_element_type=F32)
-            Phi = 0.5 + 0.5 * lax.erf(act * INV_SQRT2)
-            phi = jnp.exp(-0.5 * act * act) * INV_SQRT_2PI
-            gel = act * Phi
-            rr = pl.ds(r0, n)
-            hidT[qi, rr, :] = (gel * up).astype(BF)
-            daT[qi, rr, :] = (dh * up * (Phi + act * phi)).astype(BF)
-            duT[qi, rr, :] = (dh * gel).astype(BF)
+        h2a[block_chunk(r), :] = (xhat * gain2).astype(BF)
+
+    h_copy = (
+        remote(h2a.at[ob], h2a.at[ob], n_s.at[0], n_r.at[0], (core, z)),
+        remote(h2a.at[ob], h2a.at[ob], n_s.at[1], n_r.at[1], (dp, zp)),
+        remote(h2a.at[zb], h2a.at[zb], n_s.at[2], n_r.at[2], (core, z)),
+    )
+    h_copy[1].start()
+    h_copy[0].start()
+    late_across(2)
+    late_across(3)
+    remote(cot, cot4.at[zb], cx_s.at[1], cx_r.at[1], (dp, zp)).wait_recv()
+    cot_copy[2].start()
+    remote(cot, cot4.at[cb], cx_s.at[0], cx_r.at[0], (core, z)).wait_recv()
+    remote(cot, cot4.at[db], cx_s.at[2], cx_r.at[2], (core, z)).wait_recv()
+    for u in range(4):
+        for w, where in enumerate((chip_b, chip_d)):
+            ref = piece(u, where)
+            remote(ref, ref, pb_s.at[u], pb_r.at[w, u], (core, z)).wait_recv()
+    remote(h2a.at[zb], h2a.at[zb], n_s.at[1], n_r.at[1], (dp, zp)).wait_recv()
+    h_copy[2].start()
+    remote(h2a.at[cb], h2a.at[cb], n_s.at[0], n_r.at[0], (core, z)).wait_recv()
+
+    def tile(r0, n, tokens):
+        h2 = h2a[tokens, :]
+        act = lax.dot_general(G[r0 : r0 + n, :], h2, NT, preferred_element_type=F32)
+        up = lax.dot_general(G[HID + r0 : HID + r0 + n, :], h2, NT, preferred_element_type=F32)
+        dh = lax.dot_general(
+            G[2 * HID + r0 : 2 * HID + r0 + n, :], cot4[tokens, :], NT, preferred_element_type=F32
+        )
+        Phi = 0.5 + 0.5 * lax.erf(act * INV_SQRT2)
+        phi = jnp.exp(-0.5 * act * act) * INV_SQRT_2PI
+        gel = act * Phi
+        rr = slice(r0, r0 + n)
+        hidT[rr, tokens] = (gel * up).astype(BF)
+        daT[rr, tokens] = (dh * up * (Phi + act * phi)).astype(BF)
+        duT[rr, tokens] = (dh * gel).astype(BF)
+
+    @pl.loop(0, 2)
+    def _(t):
+        there = lax.rem(zq + t, 2)
+
+        @pl.when(t == 1)
+        def _():
+            remote(h2a.at[db], h2a.at[db], n_s.at[2], n_r.at[2], (core, z)).wait_recv()
+
+        for r0, n in ((0, 224), (224, 224), (448, 208)):
+            tile(r0, n, cols(there * 512, 512))
 
     def tn(lhs, rhs):
         return lax.dot_general(lhs, rhs, TN, preferred_element_type=F32)
 
-    def d_norm(dst, rows):
-        for half in range(2):
-            hc = slice(half * 512, half * 512 + 512)
-            dst[:, hc] = sum(
-                tn(daT[qi, :, rows], G[qi, w_rows(qi, 0), hc]) + tn(duT[qi, :, rows], G[qi, w_rows(qi, 1), hc])
-                for qi in range(2)
-            )
-
-    def mlp_out(dst, rows, plus=None):
-        for half in range(2):
-            hc = slice(half * 512, half * 512 + 512)
-            r = sum(tn(hidT[qi, :, rows], G[qi, w_rows(qi, 2), hc]) for qi in range(2))
+    def f_rows(m):
+        return pl.ds(FROWS[m][0], HID)
+
+    def d_norm(rows, hc):
+        return tn(daT[:, rows], G[f_rows(0), hc]) + tn(duT[:, rows], G[f_rows(1), hc])
+
+    def mlp_out(rows, hc):
+        return tn(hidT[:, rows], G[f_rows(2), hc])
+
+    def quad(term, sb, got, zs, zgot, ss, rs):
+        halves = (slice(0, 512), slice(512, 1024))
+        copies = (
+            remote(sb.at[0], got.at[0], ss.at[0], rs.at[0], (core, z)),
+            remote(sb.at[1], got.at[1], ss.at[1], rs.at[1], (core, z)),
+            remote(zs, zgot, ss.at[2], rs.at[2], (dp, zp)),
+        )
+        for j, rows in enumerate((db, cb)):
+            for hc in halves:
+                sb[j, :, hc] = term(rows, hc).astype(BF)
+            copies[j].start()
+        copies[0].wait_recv()
+        for hc in halves:
+            zs[:, hc] = (term(zb, hc) + got[0, :, hc].astype(F32)).astype(BF)
+        copies[2].start()
+        return copies
+
+    def keep(term, dst, plus=None):
+        for hc in (slice(0, 512), slice(512, 1024)):
+            r = term(ob, hc)
             dst[:, hc] = r if plus is None else r + plus[:, hc]
 
-    def grads(qi, m):
-        lhs, rhs = ((daT, h2a), (duT, h2a), (hidT, cot2))[m]
+    def grads(m):
+        lhs, rhs = ((daT, h2a), (duT, h2a), (hidT, cot4))[m]
 
         @pl.loop(0, 4)
         def _(t):
             tc = cols(t * 256, 256)
-            G[qi, w_rows(qi, m), tc] = jnp.dot(lhs[qi], rhs[:, tc], preferred_element_type=F32).astype(BF)
-
-    def unit(e):
-        qi, k_ = UNITS[e]
-        m, o, n = HALVES[k_]
-        return qi, pl.ds(ROWS[m][0] + o, n)
+            G[f_rows(m), tc] = jnp.dot(lhs[...], rhs[:, tc], preferred_element_type=F32).astype(BF)
+
+    def rows_of(e):
+        m, o, n = HALVES[e]
+        return pl.ds(FROWS[m][0] + o, n)
 
     def part(e, where):
-        qi, rows = unit(e)
-        return G.at[qi, rows, cols(where * 256, 256)]
+        if e < NF:
+            return G.at[rows_of(e), cols(where * 256, 256)]
+        return opiece(e - NF, where)
+
+    def from_b(e, slot):
+        return Rb.at[slot, rows_of(e)] if e < NF else Rbo.at[slot, e - NF]
+
+    def from_a(e):
+        return Ra.at[rows_of(e)] if e < NF else Rao.at[e - NF]
 
     def unit_b(e, slot):
-        qi, rows = unit(e)
         src = part(e, chip_b if slot == 0 else chip_d)
-        return remote(src, Rb.at[slot, qi, rows], b_s.at[slot, e], b_r.at[slot, e], (b, z))
+        return remote(src, from_b(e, slot), b_s.at[slot, e], b_r.at[slot, e], (b, z))
 
     def unit_a(e):
-        qi, rows = unit(e)
-        return remote(part(e, chip_a), Ra.at[qi, rows], a_s.at[e], a_r.at[e], (a, z))
+        return remote(part(e, chip_a), from_a(e), a_s.at[e], a_r.at[e], (a, z))
 
     def send_b(e):
         unit_b(e, 1).start()
         unit_b(e, 0).start()
 
     def stage1(e):
-        qi, rows = unit(e)
         unit_b(e, 1).wait_recv()
         ref = part(e, chip_a)
-        ref[...] = (ref[...].astype(F32) + Rb[1, qi, rows, :].astype(F32)).astype(BF)
+        ref[...] = (ref[...].astype(F32) + from_b(e, 1)[...].astype(F32)).astype(BF)
         unit_a(e).start()
 
-    def line_up(e, slot):
-        rows = unit(e)[1]
-        return remote(part(e, chip), Z.at[slot, rows], zu_s.at[e], z_r.at[slot, e], (dp, z + 1))
-
-    def line_down(e):
-        qi, rows = unit(e)
-        return remote(part(e, chip), Z.at[qi, rows], zd_s.at[e], z_r.at[qi, e], (dp, z - 1))
-
-    def target(e):
-        return 2 * c + UNITS[e][0]
-
-    def inward(e, act):
-        t = target(e)
-        pl.when(z > t)(lambda: act(line_down(e)))
-        pl.when(z + 1 == t)(lambda: act(line_up(e, 2)))
-        pl.when(z + 1 < t)(lambda: act(line_up(e, UNITS[e][0])))
+    def unit_z(e):
+        return remote(part(e, chip), Z.at[rows_of(e)], zu_s.at[e], z_r.at[0, e], (dp, z2))
+
+    def unit_o(e):
+        t = 2 * c + e - NF
+        slot = lax.rem(z - t + 4, 4) - 1
+        return remote(part(e, chip), Zo.at[slot], zu_s.at[e], z_r.at[slot, e], (dp, t))
 
     def stage2(e):
-        qi, rows = unit(e)
         unit_b(e, 0).wait_recv()
         unit_a(e).wait_recv()
         ref = part(e, chip)
-        ref[...] = (ref[...].astype(F32) + Rb[0, qi, rows, :].astype(F32) + Ra[qi, rows, :].astype(F32)).astype(BF)
-        t = target(e)
-        pl.when(((z == 3) & (z > t)) | ((z == 0) & (z < t)))(lambda: inward(e, begin))
+        ref[...] = (
+            ref[...].astype(F32) + from_b(e, 0)[...].astype(F32) + from_a(e)[...].astype(F32)
+        ).astype(BF)
+        if e < NF:
+            pl.when(no(org))(lambda: unit_z(e).start())
+        else:
+            pl.when(z != 2 * c + e - NF)(lambda: unit_o(e).start())
 
     def line_wait(e, slot):
-        ref = Z.at[slot, unit(e)[1]]
-        remote(ref, ref, zu_s.at[e], z_r.at[slot, e], (core, z)).wait_recv()
-
-    def stage3(e, depth):
-        qi, rows = unit(e)
-        t = target(e)
-        mid = ((z > t) & (z == 3 - depth)) | ((z < t) & (z == depth))
-
-        @pl.when(mid)
+        remote(Zo.at[slot], Zo.at[slot], zu_s.at[e], z_r.at[slot, e], (core, z)).wait_recv()
+
+    def final(e):
+        if e < NF:
+            m, o, n = HALVES[e]
+            return e, give.at[rows_of(e)], dw4[m].at[pl.ds(o, n)]
+        return NF, give.at[FF3 : FF3 + 256], dwout_o
+
+    def stage4(e):
+        here = org if e < NF else z == 2 * c + e - NF
+
+        @pl.when(here)
         def _():
-            line_wait(e, qi)
-            ref = part(e, chip)
-            ref[...] = (ref[...].astype(F32) + Z[qi, rows, :].astype(F32)).astype(BF)
-            inward(e, begin)
-
-    def final(k_):
-        m, o, n = HALVES[k_]
-        return give.at[pl.ds(ROWS[m][0] + o, n)], dw4[m].at[pl.ds(o, n)]
-
-    def stage4(e):
-        qi, rows = unit(e)
-        k_ = UNITS[e][1]
-
-        @pl.when(z == target(e))
-        def _():
-            gift, dst = final(k_)
-            dst[...] = G[qi, rows, cols(dp * 128, 128)].astype(F32)
-            gift[...] = G[qi, rows, cols(core * 128, 128)].astype(F32)
-
-            def take(slot):
-                line_wait(e, slot)
+            slot, gift, dst = final(e)
+            if e < NF:
+                unit_z(e).wait_recv()
+            for who, ref in ((c, dst), (1 - c, gift)):
+                ref[...] = part(e, chip)[:, cols(who * 128, 128)].astype(F32)
+
+            def take(got):
                 for who, ref in ((c, dst), (1 - c, gift)):
-                    ref[...] = ref[...] + Z[slot, rows, cols(who * 128, 128)].astype(F32)
-
-            pl.when(z < 3)(lambda: take(qi))
-            pl.when(z > 0)(lambda: take(2))
-            remote(gift, dst, fin_s.at[k_], fin_r.at[k_], (core, z)).start()
+                    ref[...] = ref[...] + got[:, cols(who * 128, 128)].astype(F32)
+
+            def line_take(where):
+                line_wait(e, where)
+                take(Zo.at[where])
+
+            if e < NF:
+                take(Z.at[rows_of(e)])
+            else:
+                for slot_ in range(3):
+                    line_take(slot_)
+            remote(gift, dst, fin_s.at[slot], fin_r.at[slot], (core, z)).start()
 
     def tick(t):
-        for lag, step in enumerate(
-            (stage1, stage2, lambda e: stage3(e, 1), lambda e: stage3(e, 2), stage4)
-        ):
+        for lag, step in ((0, stage1), (1, stage2), (4, stage4)):
             if 0 <= t - lag < NU:
                 step(t - lag)
 
-    d_norm(acc, other)
-    d_copy = remote(acc, dr, d_s, d_r, (core, z))
-    d_copy.start()
-    mlp_out(dxo, other)
-    u_copy = remote(dxo, ur, u_s, u_r, (core, z))
-    u_copy.start()
-    d_norm(dX1, own)
-    mlp_out(dtok_o, own, X1)
+    d_copies = quad(d_norm, dsb, dr, dzs, dzr, d_s, d_r)
+    keep(d_norm, dX1)
+    u_copies = quad(mlp_out, usb, ur, uzs, uzr, u_s, u_r)
+    keep(mlp_out, dtok_o, X1)
     for u in range(4):
-        for qi in range(2):
-            line_send(qi, u, True, lambda cp: cp.wait_send())
-            line_send(qi, u, False, lambda cp: cp.wait_send())
-        for qi in range(2):
-            plane_a(qi, u).wait_send()
-            plane_b(qi, u).wait_send()
-            plane_f(qi, u).wait_send()
-    def ff_grads(qi, m):
-        grads(qi, m)
-        for e in range(NU):
-            if UNITS[e][0] == qi and HALVES[UNITS[e][1]][0] == m:
+        plane_a(u).wait_send()
+        plane_b(u).wait_send()
+        plane_f(u).wait_send()
+        pl.when(org)(lambda u=u: leap(u).wait_send())
+
+    def ff_grads(m):
+        grads(m)
+        for e in range(NF):
+            if HALVES[e][0] == m:
                 send_b(e)
 
-    ff_grads(0, 2)
-    ff_grads(0, 0)
-    d_copy.wait()
+    ff_grads(2)
+    ff_grads(0)
+    ff_grads(1)
+    d_copies[1].wait_recv()
+    d_copies[2].wait_recv()
 
     @pl.loop(0, 8)
     def _(r):
-        dh2 = dX1[chunk(r), :] + dr[chunk(r), :]
+        dh2 = dX1[chunk(r), :] + dr[1, chunk(r), :].astype(F32) + dzr[chunk(r), :].astype(F32)
         xhat, rstd = norm_rows(X1[chunk(r), :])
         e2 = dh2 * gain2
         m1 = jnp.mean(e2, axis=-1, keepdims=True)
         m2 = jnp.mean(e2 * xhat, axis=-1, keepdims=True)
-        dx = cot2[own_chunk(r), :].astype(F32) + rstd * (e2 - m1 - xhat * m2)
+        dx = cot4[block_chunk(r), :].astype(F32) + rstd * (e2 - m1 - xhat * m2)
         dX1[chunk(r), :] = dx
         dya[own_chunk(r), :] = dx.astype(BF)
 
     e_copy = remote(dya.at[own], dya.at[own], e_s, e_r, (core, z))
     e_copy.start()
-    ff_grads(0, 1)
+    tick(0)
     e_copy.wait()
     for qi in range(2):
-        dsend[qi] = lax.dot_general(dya[...], G[qi, w_rows(qi, 3), :], NT, preferred_element_type=F32).astype(BF)
+        dsend[qi] = lax.dot_general(dya[...], Wo[qi], NT, preferred_element_type=F32).astype(BF)
 
     def att_back(c0, qi):
         dst = datt.at[cols(z * 256, 256)]
@@ -705,19 +730,22 @@
             def _(c0=c0, qi=qi):
                 datt[cols(z * 256, 256), :] = dsend[qi, c0 * 256 : (c0 + 1) * 256, :]
 
-    for m in (2, 0, 1):
-        ff_grads(1, m)
+    for n in range(1, 4):
+        pl.when(org)(lambda n=n: ofar(n).wait_send())
     for qi in range(2):
+        for cp in oplane(qi):
+            cp.wait_send()
 
         @pl.loop(0, 4)
         def _(t, qi=qi):
             tc = cols(t * 256, 256)
-            G[qi, w_rows(qi, 3), tc] = tn(attn2[:, qi * 256 : (qi + 1) * 256], dya[:, tc]).astype(BF)
-
-        send_b(12 + qi)
-    tick(0)
-    u_copy.wait()
-    out_o[...] = (dtok_o[...] + ur[...]).astype(BF)
+            Wo[qi, :, tc] = tn(attn2[:, qi * 256 : (qi + 1) * 256], dya[:, tc]).astype(BF)
+
+        send_b(NF + qi)
+    tick(1)
+    tick(2)
+    for cp in h_copy:
+        cp.wait_send()
     dq[...] = jnp.zeros_like(dq)
     dk[...] = jnp.zeros_like(dk)
     dv[...] = jnp.zeros_like(dv)
@@ -737,7 +765,9 @@
             delta[h, i] = jnp.broadcast_to(s, (8, 256))
 
     def block_order(l):
-        return jnp.minimum(l, 1) * (lax.rem(l + 1, 3) + 1)
+        inner = lax.div(z * (3 - z), 2)
+        base = inner * jnp.minimum(l, 1) * (lax.rem(l + 1, 3) + 1) + (1 - inner) * l
+        return (1 - home) * (3 - base) + home * base
 
     def pair(i, j):
         ri = pl.ds(pl.multiple_of(i * 256, 256), 256)
@@ -762,30 +792,38 @@
         dk[rj, :] = dk[rj, :] + (dks[0] + dks[1] + dks[2] + dks[3])
         dq[ri, :] = dq[ri, :] + (dqs[0] + dqs[1] + dqs[2] + dqs[3])
 
-    def h_up(i, last):
+    def quarter(t):
+        return pl.ds(pl.multiple_of(t * 64, 64), 64)
+
+    def h_up(i, t, last):
         if last:
-            return remote(Hs.at[i], Hx, hu_s.at[i], hx_r, (dp, z + 1))
-        return remote(Hs.at[i], Hi.at[i], hu_s.at[i], hi_r.at[i], (dp, z + 1))
-
-    def h_down(i):
-        return remote(Hs.at[i], Hi.at[i], hd_s.at[i], hi_r.at[i], (dp, z - 1))
-
-    def h_inward(i, act):
-        pl.when(z > i)(lambda: act(h_down(i)))
-        pl.when(z + 1 == i)(lambda: act(h_up(i, True)))
-        pl.when(z + 1 < i)(lambda: act(h_up(i, False)))
-
-    def h_wait(i):
-        remote(Hi.at[i], Hi.at[i], hd_s.at[i], hi_r.at[i], (core, z)).wait_recv()
+            return remote(Hs.at[i, quarter(t)], Hx.at[quarter(t)], hu_s.at[i, t], hx_r.at[t], (dp, z + 1))
+        return remote(Hs.at[i, quarter(t)], Hi.at[i, quarter(t)], hu_s.at[i, t], hi_r.at[i, t], (dp, z + 1))
+
+    def h_down(i, t):
+        return remote(Hs.at[i, quarter(t)], Hi.at[i, quarter(t)], hd_s.at[i, t], hi_r.at[i, t], (dp, z - 1))
+
+    def h_inward(i, t, act):
+        pl.when(z > i)(lambda: act(h_down(i, t)))
+        pl.when(z + 1 == i)(lambda: act(h_up(i, t, True)))
+        pl.when(z + 1 < i)(lambda: act(h_up(i, t, False)))
+
+    def h_wait(i, t):
+        ref = Hi.at[i, quarter(t)]
+        remote(ref, ref, hd_s.at[i, t], hi_r.at[i, t], (core, z)).wait_recv()
 
     def h_mid(i, depth):
         mid = ((z > i) & (z == 3 - depth)) | ((z < i) & (z == depth))
 
         @pl.when(mid)
         def _():
-            h_wait(i)
-            Hs[i] = (Hs[i].astype(F32) + Hi[i].astype(F32)).astype(BF)
-            h_inward(i, begin)
+            @pl.loop(0, 4)
+            def _(t):
+                h_wait(i, t)
+                Hs[i, quarter(t), :] = (
+                    Hs[i, quarter(t), :].astype(F32) + Hi[i, quarter(t), :].astype(F32)
+                ).astype(BF)
+                h_inward(i, t, begin)
 
     def finish(i):
         rows = pl.ds(pl.multiple_of(i * 256, 256), 256)
@@ -808,11 +846,14 @@
             def _(dh=dh, hc=hc):
                 acc[:, hc] = dh
 
-        pl.when(((z == 3) & (z > i)) | ((z == 0) & (z < i)))(lambda: h_inward(i, begin))
-
-    tick(1)
-    slots = {1: [2], 4: [3], 7: [4], 9: [5], 11: [6], 13: [7], 15: [8]}
-    h_slots = {11: [(0, 1)], 15: [(0, 2), (3, 1)]}
+        @pl.when(((z == 3) & (z > i)) | ((z == 0) & (z < i)))
+        def _():
+            for t in range(4):
+                h_inward(i, t, begin)
+
+
+    slots = {0: [3], 2: [4], 5: [5], 8: [6], 11: [7], 14: [8]}
+    h_slots = {12: [(0, 1), (3, 1)]}
 
     @pl.loop(0, 16)
     def _(n):
@@ -848,10 +889,11 @@
 
     for w in range(4):
         core_copy(w).start()
-    tick(9)
     h_mid(3, 2)
-    h_mid(1, 1)
-    h_mid(2, 1)
+    h_mid(0, 2)
+    u_copies[1].wait_recv()
+    u_copies[2].wait_recv()
+    out_o[...] = (dtok_o[...] + ur[1].astype(F32) + uzr[...].astype(F32)).astype(BF)
 
     def both(w):
         Wc[w] = (Wc[w].astype(F32) + Wp[:, cols(w * 256 + c * 128, 128)].astype(F32)).astype(BF)
@@ -869,16 +911,17 @@
     both(chip_a)
     both(chip)
     wa_copy = remote(Wc.at[chip_a], Wa, wa_s, wa_r, (a, z))
-    for t in range(10, 14):
-        tick(t)
+    h_mid(2, 1)
+    h_mid(1, 1)
+    tick(9)
     wb_copy[1].wait_recv()
     Wc[chip_a] = (Wc[chip_a].astype(F32) + Wb[1].astype(F32)).astype(BF)
     wa_copy.start()
-    tick(14)
-    tick(15)
-
-    pl.when(z < 3)(lambda: h_wait(z))
-    pl.when(z > 0)(lambda: remote(Hx, Hx, hu_s.at[0], hx_r, (core, z)).wait_recv())
+
+    for t in range(4):
+        ref = Hx.at[quarter(t)]
+        pl.when(z < 3)(lambda t=t: h_wait(z, t))
+        pl.when(z > 0)(lambda t=t, ref=ref: remote(ref, ref, hu_s.at[0, t], hx_r.at[t], (core, z)).wait_recv())
     has_above, has_below = z < 3, z > 0
 
     @pl.when(has_above)
@@ -905,16 +948,16 @@
         piece = total[p * 256 : (p + 1) * 256, :]
         dwq_o[p] = piece.T
         dot_one = dot_one + jnp.sum(piece * wqkv[p].T.astype(F32), axis=0, keepdims=True)
-    for t in range(16, NU + 4):
+    for t in range(10, NU + 4):
         tick(t)
-    for k_ in range(7):
+    for e in range(NF + 1):
 
         @pl.when(no(org))
-        def _(k_=k_):
-            ref = final(k_)[1]
-            remote(ref, ref, fin_s.at[k_], fin_r.at[k_], (core, z)).wait_recv()
-
-    part_two = jnp.sum(dwin_o[...] * w4[256 : 256 + 2 * HID, :].astype(F32), axis=0, keepdims=True)
+        def _(e=e):
+            slot, _, ref = final(e)
+            remote(ref, ref, fin_s.at[slot], fin_r.at[slot], (core, z)).wait_recv()
+
+    part_two = jnp.sum(dwin_o[...] * w3[0 : 2 * HID, :].astype(F32), axis=0, keepdims=True)
     gz[z, 0:1, :] = dot_one / gains[dp, 0:1, :]
     gz[z, 1:2, :] = part_two / gains[dp, 1:2, :]
     gz[z, 2:8, :] = jnp.zeros((6, 128), F32)
@@ -936,21 +979,26 @@
     wb_copy[1].wait_send()
     wa_copy.wait_send()
     for i in range(4):
-        h_inward(i, lambda cp: cp.wait_send())
+        for t in range(4):
+            h_inward(i, t, done)
     for c0 in range(2):
         for qi in range(2):
             pl.when(no(is_self(c0, qi)))(lambda c0=c0, qi=qi: att_back(c0, qi).wait_send())
+    for cp in d_copies + u_copies:
+        cp.wait_send()
     for e in range(NU):
         unit_b(e, 0).wait_send()
         unit_b(e, 1).wait_send()
         unit_a(e).wait_send()
-        inward(e, lambda cp: cp.wait_send())
-
-        @pl.when(z == target(e))
+        if e < NF:
+            pl.when(no(org))(lambda e=e: unit_z(e).wait_send())
+        else:
+            pl.when(z != 2 * c + e - NF)(lambda e=e: unit_o(e).wait_send())
+
+        @pl.when(org if e < NF else z == 2 * c + e - NF)
         def _(e=e):
-            k_ = UNITS[e][1]
-            gift, dst = final(k_)
-            remote(gift, dst, fin_s.at[k_], fin_r.at[k_], (core, z)).wait_send()
+            slot, gift, dst = final(e)
+            remote(gift, dst, fin_s.at[slot], fin_r.at[slot], (core, z)).wait_send()
 
     for d in range(1, 8):
         remote(gains_in, gains.at[dp], g_s.at[d], g_r.at[d], (core, z)).wait_send()
@@ -958,8 +1006,10 @@
         remote(wqkv, wq.at[:, own_rows], wr_s.at[j], wr_r.at[j], (core, z)).wait_send()
     for j in range(4):
         remote(wqkv, wq.at[:, own_rows], wx_s.at[j], wx_r.at[j], (core, z)).wait_send()
-    pl.when(no(org))(lambda: hop.wait_send())
-    cot_copy.wait_send()
+    for cp in hop:
+        pl.when(no(org))(lambda cp=cp: cp.wait_send())
+    for cp in cot_copy:
+        cp.wait_send()
     for n in range(3):
         att_copy(n, lax.rem(z + 1 + n, 4)).wait_send()
     pl.when(no(org))(lambda: att_copy(3, z).wait_send())
@@ -980,25 +1030,28 @@
         in_specs=[S, S] + [V] * 6 + [pl.BlockSpec(memory_space=pl.ANY)],
         out_specs=[V] * 7,
         scratch_shapes=[
-            vm((8, 8, 128), F32), vm((PACK, 128), BF), vm((1024, 128), F32), vm((1024, 128), F32),
+            vm((8, 8, 128), F32), vm((FF3, 128), BF), vm((1024, 128), F32), vm((1024, 128), F32),
             vm((1024, 128), F32), vm((8, 1024), F32), vm((1024, 256), BF), vm((1024, 256), BF),
             vm((1024, 256), BF), vm((4, 4, 8, 256), F32), vm((1024, 256), BF), vm((512, 512), BF),
-            vm((1024, 1024), BF), vm((3, 1024, 256), BF), vm((512, 1024), BF),
-            vm((2, PACK, 1024), BF), vm((256, 1024), F32), vm((1024, 1024), BF), vm((256, 1024), F32),
-            vm((256, 1024), F32), vm((256, 1024), F32), vm((2, HID, 512), BF), vm((2, HID, 512), BF),
-            vm((2, HID, 512), BF), vm((256, 1024), F32), vm((256, 1024), F32), vm((2, 512, 256), BF),
-            vm((1024, 256), BF), vm((4, 4, 8, 256), F32),
+            vm((1024, 1024), BF), vm((3, 1024, 256), BF), vm((1024, 1024), BF),
+            vm((FF3, 1024), BF), vm((2, 256, 1024), BF), vm((256, 1024), F32), vm((1024, 1024), BF), vm((512, 1024), BF),
+            vm((256, 1024), F32), vm((256, 1024), F32), vm((HID, 1024), BF), vm((HID, 1024), BF),
+            vm((HID, 1024), BF), vm((256, 1024), F32),
+            vm((2, 256, 1024), BF), vm((2, 256, 1024), BF), vm((256, 1024), BF), vm((256, 1024), BF),
+            vm((2, 256, 1024), BF), vm((2, 256, 1024), BF), vm((256, 1024), BF), vm((256, 1024), BF),
+            vm((2, 512, 256), BF), vm((1024, 256), BF), vm((4, 4, 8, 256), F32),
             vm((1024, 256), F32), vm((1024, 256), F32), vm((1024, 256), F32),
-            vm((4, 256, 1024), BF), vm((4, 256, 1024), BF), vm((256, 1024), BF), vm((2, 2, PACK, 256), BF),
-            vm((2, PACK, 256), BF), vm((3, PACK, 256), BF), vm((PACK, 128), F32),
+            vm((4, 256, 1024), BF), vm((4, 256, 1024), BF), vm((256, 1024), BF),
+            vm((2, FF3, 256), BF), vm((FF3, 256), BF), vm((FF3, 256), BF),
+            vm((2, 2, 256, 256), BF), vm((2, 256, 256), BF), vm((3, 256, 256), BF), vm((FF3 + 256, 128), F32),
             vm((768, 1024), BF), vm((4, 768, 128), BF), vm((2, 768, 128), BF), vm((768, 128), BF), vm((4, 8, 128), F32),
             dma((4, 2)), dma((4, 2)), dma((4, 2)), dma((4, 2)),
-            dma((3,)), dma((3,)), dma((4,)), dma((4,)), dma((8,)), dma((8,)), dma, dma, dma, dma,
-            dma((2, 4)), dma((2, 4)), dma((2, 4)), dma((2, 4)), dma((2, 4)), dma((2, 4)),
-            dma((2, 4)), dma((2, 2, 4)), dma((4,)), dma((2, 2)),
-            dma, dma, dma, dma, dma, dma, dma, dma, dma, dma, dma((2, 2)), dma((4,)),
-            dma((2, NU)), dma((2, NU)), dma((NU,)), dma((NU,)), dma((NU,)), dma((NU,)), dma((3, NU)),
-            dma((7,)), dma((7,)), dma((4,)), dma((4,)), dma((4,)), dma,
+            dma((3,)), dma((3,)), dma((4,)), dma((4,)), dma((8,)), dma((8,)), dma((3,)), dma((3,)), dma((2,)), dma((2,)),
+            dma((4,)), dma((2,)), dma((2,)), dma((2,)), dma((2,)), dma((2,)), dma((2, 2)),
+            dma((4,)), dma((4,)), dma((4,)), dma((4,)), dma((4,)), dma((4,)), dma((2, 4)), dma((4,)), dma((2, 2)),
+            dma, dma, dma((3,)), dma((3,)), dma((3,)), dma((3,)), dma((3,)), dma((3,)), dma, dma, dma((2, 2)), dma((4,)),
+            dma((2, NU)), dma((2, NU)), dma((NU,)), dma((NU,)), dma((NU,)), dma((3, NU)),
+            dma((NF + 1,)), dma((NF + 1,)), dma((4, 4)), dma((4, 4)), dma((4, 4)), dma((4,)),
             dma((4,)), dma((4,)), dma((2,)), dma((2,)), dma, dma, dma((4,)), dma((4,)), dma,
         ],
         compiler_params=pltpu.CompilerParams(

time: 261 us -> 224 us (0.86)
  Pallas kernels: 250 us -> 213 us
    pallas_call x1, Pallas kernels: 250 us -> 213 us  [run_layer(): pl.pallas_call(layer_kernel, out_shape=(s((256, 1024), BF), s((256, 1024)...]
where the time goes in v3:
time: 224 us; the launch traced here: 223 us
  Pallas kernels  213 us (95%)
  local copies, waits for them, and re-layouts  9.86 us (4%)
    pallas_call x1, Pallas kernels, run_layer(): pl.pallas_call(layer_kernel, out_shape=(s((256, 1024), BF), s((256, 1024)...  213 us
    unnamed x22, local copies, waits for them, and re-layouts  7.65 us

profile of v3, /device:TPU:0, one launch (start us, length us, event | category | flops | bytes accessed | tf_op | source)
XLA Modules:
  0.0 223.2 jit_solution(17420273052816957556)
XLA Ops:
  0.6 0.0 copy-start.7
  0.7 0.6 copy-done.7
  1.3 0.1 broadcast_in_dim.22
  1.4 0.1 tile.14
  1.5 0.0 copy-start.5
  1.5 0.1 broadcast_in_dim_tile.7
  1.5 0.6 copy-done.5
  2.1 0.0 copy-done.6
  2.1 0.1 broadcast_in_dim_tile.6
  2.2 0.6 concatenate.3.gains_in
  2.8 212.6 %layer.1 = (bf16[256,1024]{1,0:T(8,128)(2,1)}, f32[256,1024]{1,0:T(8,128)}, f32[3,128,256]{2,1,0:T(8,128)}, f32[1312,128]{1,0:T(8,128)}, f32[656,128]{1,0:T(8,12...) custom-call(s32[32]{0:T(128)} %lengths.1, s32[32]{0:T(128)} %seq_order.1, bf16[256,1024]{1,0:T(8,128)(2,1)} %tok.1, ...), custom_call_target="tpu_custom_call" | custom-call | tf_op jit(solution)/shard_map/layer/pallas_call | solution.py:1024
  215.5 0.0 copy-start
  215.5 1.3 slice_bitcast_fusion
  216.7 1.9 copy.25
  218.6 0.0 copy-done
  218.6 1.0 copy.26
  219.6 0.3 copy-done.2
  219.8 0.7 copy.27
  220.6 0.0 copy-done.4
  220.6 0.7 copy.28
  221.3 0.0 copy-done.1
  221.3 0.8 copy.29
  222.1 0.3 copy-done.3
  222.4 0.7 copy.30
  (10 shorter events, 0.0 us)
Async XLA Ops:
  0.6 0.7 copy-start.7
  1.5 0.7 copy-start.5
  1.5 0.7 copy-start.6
  215.5 3.2 %copy-start = (f32[256,1024]{1,0:T(8,128)S(1)}, f32[256,1024]{1,0:T(8,128)}, u32[]{:S(2)}) copy-start(f32[256,1024]{1,0:T(8,128)} %get-tuple-element.35) | copy-start | bytes 3145732
  218.6 1.2 copy-start.2
  218.6 2.0 copy-start.4
  219.8 1.4 copy-start.1
  221.3 1.2 copy-start.3

commit v4 on v3

--- a/solution.py
+++ b/solution.py
@@ -128,7 +128,7 @@
         return cols((2 * line_bit + core_bit) * 256, 256)
 
     ob, cb, zb, db = block(c, zq), block(1 - c, zq), block(c, 1 - zq), block(1 - c, 1 - zq)
-    tall, vT, oT, dqkvT = Hs, Hx, acc.at[:, 0:256], h2a.at[0:768]
+    tall, vT, kT, oT, dqkvT = Hs, Hx, dzs, acc.at[:, 0:256], h2a.at[0:768]
     dw4 = (dwin_o.at[0:HID], dwin_o.at[HID : 2 * HID], dwmlp_o)
     greet(dp, z, bits)
 
@@ -203,14 +203,21 @@
         r0, n = CUTS[u]
         return G.at[pl.ds(r0, n), cols(where * 256, 256)]
 
+    def way(u):
+        s = lax.rem(c + u, 2)
+        one = (1 - s) * px + s * py
+        two = (1 - s) * py + s * px
+        return one, two, lax.div(one, 2), lax.div(two, 2)
+
     def plane_a(u):
-        return remote(piece(u, chip), piece(u, chip), pa_s.at[u], pa_r.at[u], (a, z))
+        return remote(piece(u, chip), piece(u, chip), pa_s.at[u], pa_r.at[u], (way(u)[0], z))
 
     def plane_b(u):
-        return remote(piece(u, chip), piece(u, chip), pb_s.at[u], pb_r.at[0, u], (b, z))
+        return remote(piece(u, chip), piece(u, chip), pb_s.at[u], pb_r.at[0, u], (way(u)[1], z))
 
     def plane_f(u):
-        return remote(piece(u, chip_a), piece(u, chip_a), pf_s.at[u], pb_r.at[1, u], (b, z))
+        ref = piece(u, way(u)[2])
+        return remote(ref, ref, pf_s.at[u], pb_r.at[1, u], (way(u)[1], z))
 
     def leap(u):
         return remote(piece(u, chip), piece(u, chip), fz_s.at[u], fz_r.at[u], (dp, z2))
@@ -220,8 +227,8 @@
         plane_b(u).start()
 
     def across(u):
-        ref = piece(u, chip_a)
-        remote(ref, ref, pa_s.at[u], pa_r.at[u], (a, z)).wait_recv()
+        ref = piece(u, way(u)[2])
+        remote(ref, ref, pa_s.at[u], pa_r.at[u], (way(u)[0], z)).wait_recv()
         plane_f(u).start()
 
     def land(u):
@@ -340,6 +347,13 @@
                     if k_ < 3:
                         pl.when(down_ok(k_))(lambda: tok_down(k_, h).start())
 
+        if k_ == 1:
+
+            @pl.when(org)
+            def _():
+                for n in range(1, 4):
+                    ofar(n).start()
+
         @pl.loop(0, 2)
         def _(t, k_=k_):
             s = z - k_ + 2 * k_ * t
@@ -357,8 +371,6 @@
 
             @pl.when(org & end)
             def _():
-                for n in range(1, 4):
-                    ofar(n).start()
                 for u in range(4):
                     leap(u).start()
 
@@ -372,27 +384,25 @@
         seg_q = segr[0:1, rows]
         heads = range(4)
         qh = [jnp.where(head_of == h, qb, jnp.zeros((), BF)) for h in heads]
-        top = [jnp.full((1, 256), masked_fill, F32) for h in heads]
-        tot = [jnp.zeros((1, 256), F32) for h in heads]
-        out = [jnp.zeros((HEAD_DIM, 256), F32) for h in heads]
-        for kc in range(4):
-            keys = slice(kc * 256, kc * 256 + 256)
-            kb = k[keys, :]
-            seg_k = segc[keys, :]
-            same = jnp.concatenate([seg_k, seg_k], axis=1) == seg_q
-            for h in heads:
-                s = lax.dot_general(kb, qh[h], NT, preferred_element_type=F32)
+        chunks = [slice(kc * 256, kc * 256 + 256) for kc in range(4)]
+        for h in heads:
+            hr = slice(h * HEAD_DIM, (h + 1) * HEAD_DIM)
+            scores, tops = [], []
+            for keys in chunks:
+                seg_k = segc[keys, :]
+                same = jnp.concatenate([seg_k, seg_k], axis=1) == seg_q
+                s = lax.dot_general(k[keys, :], qh[h], NT, preferred_element_type=F32)
                 s = jnp.where(same, s, masked_fill)
-                new = jnp.maximum(top[h], jnp.max(s, axis=0, keepdims=True))
-                p = jnp.exp(s - new)
-                keep = jnp.exp(top[h] - new)
-                tot[h] = tot[h] * keep + jnp.sum(p, axis=0, keepdims=True)
-                vh = vT[h * HEAD_DIM : (h + 1) * HEAD_DIM, keys]
-                out[h] = out[h] * keep + jnp.dot(vh, p.astype(BF), preferred_element_type=F32)
-                top[h] = new
-        for h in heads:
-            oT[h * HEAD_DIM : (h + 1) * HEAD_DIM, :] = out[h] * (1.0 / tot[h])
-            lse[h, i] = jnp.broadcast_to(top[h] + jnp.log(tot[h]), (8, 256))
+                scores.append(s)
+                tops.append(jnp.max(s, axis=0, keepdims=True))
+            top = jnp.maximum(jnp.maximum(tops[0], tops[1]), jnp.maximum(tops[2], tops[3]))
+            tot, out = 0.0, 0.0
+            for keys, s in zip(chunks, scores):
+                p = jnp.exp(s - top)
+                tot = tot + jnp.sum(p, axis=0, keepdims=True)
+                out = out + jnp.dot(vT[hr, keys], p.astype(BF), preferred_element_type=F32)
+            oT[hr, :] = out * (1.0 / tot)
+            lse[h, i] = jnp.broadcast_to(top + jnp.log(tot), (8, 256))
         att[rows, :] = oT[...].T.astype(BF)
 
     def att_slot(src_core, q):
@@ -418,33 +428,41 @@
         def _():
             attn2[own, cols(zq * 256, 256)] = att[pl.ds(pl.multiple_of(z * 256, 256), 256), :]
 
-        @pl.when((n == 0) & org & no(end))
+        @pl.when((n == 1) & org & no(end))
         def _():
-            for m in range(1, 4):
-                ofar(m).start()
             for u in range(4):
                 leap(u).start()
 
-        pl.when(n == 1)(lambda: cot_copy[1].start())
-
-    @pl.when(org)
+        pl.when(n == 3)(lambda: cot_copy[1].start())
+
+        @pl.when((n == 1) & end)
+        def _():
+            oland(far)
+            pl.when(no(org))(lambda: oland(near))
+
+        @pl.when((n == 3) & end)
+        def _():
+            oacross(far)
+            pl.when(no(org))(lambda: oacross(near))
+
+    @pl.when(no(end))
     def _():
         oland(far)
+        pl.when(no(org))(lambda: oland(near))
+
+    @pl.when(no(end))
+    def _():
         oacross(far)
-
-    @pl.when(no(org))
-    def _():
-        land(0)
-        oland(near)
-        oland(far)
-        for u in range(1, 4):
-            land(u)
-        oacross(near)
-        oacross(far)
-        across(0)
-
-    def late_across(u):
-        pl.when(no(org))(lambda: across(u))
+        pl.when(no(org))(lambda: oacross(near))
+
+    def late(*ops):
+        @pl.when(no(org))
+        def _():
+            for op, u in ops:
+                op(u)
+
+    pl.when(no(end))(lambda: late((land, 0), (land, 1), (land, 2), (land, 3), (across, 0), (across, 1)))
+    pl.when(end)(lambda: late((land, 0)))
 
     for k_ in range(3):
         for h in range(2):
@@ -459,6 +477,7 @@
                 slot = att_slot(src, qi)
                 remote(slot, slot, at_s.at[0], at_r.at[src, qi], (core, z)).wait_recv()
 
+    pl.when(end)(lambda: late((land, 1)))
     for qi in range(2):
         for w, where in enumerate((chip_b, chip_d)):
             ref = opiece(qi, where)
@@ -472,9 +491,10 @@
     acc[...] = out_proj(other)
     y_copy = remote(acc, yr, y_s, y_r, (core, z))
     y_copy.start()
-    late_across(1)
+    pl.when(end)(lambda: late((land, 2)))
     X1[...] = tok[...].astype(F32) + out_proj(own)
     y_copy.wait()
+    pl.when(end)(lambda: late((land, 3)))
 
     def chunk(r):
         return pl.ds(pl.multiple_of(r * 32, 32), 32)
@@ -499,18 +519,16 @@
     )
     h_copy[1].start()
     h_copy[0].start()
-    late_across(2)
-    late_across(3)
+    pl.when(end)(lambda: late((across, 0), (across, 1)))
+    late((across, 2), (across, 3))
     remote(cot, cot4.at[zb], cx_s.at[1], cx_r.at[1], (dp, zp)).wait_recv()
     cot_copy[2].start()
     remote(cot, cot4.at[cb], cx_s.at[0], cx_r.at[0], (core, z)).wait_recv()
     remote(cot, cot4.at[db], cx_s.at[2], cx_r.at[2], (core, z)).wait_recv()
     for u in range(4):
-        for w, where in enumerate((chip_b, chip_d)):
+        for w, where in enumerate((way(u)[3], chip_d)):
             ref = piece(u, where)
             remote(ref, ref, pb_s.at[u], pb_r.at[w, u], (core, z)).wait_recv()
-    remote(h2a.at[zb], h2a.at[zb], n_s.at[1], n_r.at[1], (dp, zp)).wait_recv()
-    h_copy[2].start()
     remote(h2a.at[cb], h2a.at[cb], n_s.at[0], n_r.at[0], (core, z)).wait_recv()
 
     def tile(r0, n, tokens):
@@ -534,6 +552,8 @@
 
         @pl.when(t == 1)
         def _():
+            remote(h2a.at[zb], h2a.at[zb], n_s.at[1], n_r.at[1], (dp, zp)).wait_recv()
+            h_copy[2].start()
             remote(h2a.at[db], h2a.at[db], n_s.at[2], n_r.at[2], (core, z)).wait_recv()
 
         for r0, n in ((0, 224), (224, 224), (448, 208)):
@@ -551,7 +571,7 @@
     def mlp_out(rows, hc):
         return tn(hidT[:, rows], G[f_rows(2), hc])
 
-    def quad(term, sb, got, zs, zgot, ss, rs):
+    def quad(term, sb, got, zs, zgot, ss, rs, hold=False):
         halves = (slice(0, 512), slice(512, 1024))
         copies = (
             remote(sb.at[0], got.at[0], ss.at[0], rs.at[0], (core, z)),
@@ -565,7 +585,8 @@
         copies[0].wait_recv()
         for hc in halves:
             zs[:, hc] = (term(zb, hc) + got[0, :, hc].astype(F32)).astype(BF)
-        copies[2].start()
+        if not hold:
+            copies[2].start()
         return copies
 
     def keep(term, dst, plus=None):
@@ -675,7 +696,7 @@
 
     d_copies = quad(d_norm, dsb, dr, dzs, dzr, d_s, d_r)
     keep(d_norm, dX1)
-    u_copies = quad(mlp_out, usb, ur, uzs, uzr, u_s, u_r)
+    u_copies = quad(mlp_out, usb, ur, uzs, uzr, u_s, u_r, hold=True)
     keep(mlp_out, dtok_o, X1)
     for u in range(4):
         plane_a(u).wait_send()
@@ -730,6 +751,7 @@
             def _(c0=c0, qi=qi):
                 datt[cols(z * 256, 256), :] = dsend[qi, c0 * 256 : (c0 + 1) * 256, :]
 
+    u_copies[2].start()
     for n in range(1, 4):
         pl.when(org)(lambda n=n: ofar(n).wait_send())
     for qi in range(2):
@@ -746,6 +768,9 @@
     tick(2)
     for cp in h_copy:
         cp.wait_send()
+    d_copies[2].wait_send()
+    for s in range(4):
+        kT[:, s * 256 : (s + 1) * 256] = k[s * 256 : (s + 1) * 256, :].T
     dq[...] = jnp.zeros_like(dq)
     dk[...] = jnp.zeros_like(dk)
     dv[...] = jnp.zeros_like(dv)
@@ -787,10 +812,13 @@
             dsc = (p * (dp_ - delta[h, i, 0:1, :])).astype(BF)
             dvs.append(jnp.dot(p.astype(BF), dah, preferred_element_type=F32))
             dks.append(jnp.dot(dsc, qh, preferred_element_type=F32))
-            dqs.append(tn(dsc, jnp.where(mine, kj, none)))
+            hr = slice(h * HEAD_DIM, (h + 1) * HEAD_DIM)
+            dqs.append(jnp.dot(kT[hr, rj], dsc, preferred_element_type=F32))
         dv[rj, :] = dv[rj, :] + (dvs[0] + dvs[1] + dvs[2] + dvs[3])
         dk[rj, :] = dk[rj, :] + (dks[0] + dks[1] + dks[2] + dks[3])
-        dq[ri, :] = dq[ri, :] + (dqs[0] + dqs[1] + dqs[2] + dqs[3])
+        for h in range(4):
+            hr = slice(h * HEAD_DIM, (h + 1) * HEAD_DIM)
+            dq[hr, ri] = dq[hr, ri] + dqs[h]
 
     def quarter(t):
         return pl.ds(pl.multiple_of(t * 64, 64), 64)
@@ -829,7 +857,7 @@
         rows = pl.ds(pl.multiple_of(i * 256, 256), 256)
         cb, sb = cs[rows, :], -sn[rows, :]
         low = (
-            turn(dq[rows, :] * (HEAD_DIM**-0.5), cb, sb).astype(BF),
+            turn(dq[:, rows].T * (HEAD_DIM**-0.5), cb, sb).astype(BF),
             turn(dk[rows, :], cb, sb).astype(BF),
             dv[rows, :].astype(BF),
         )
@@ -853,7 +881,7 @@
 
 
     slots = {0: [3], 2: [4], 5: [5], 8: [6], 11: [7], 14: [8]}
-    h_slots = {12: [(0, 1), (3, 1)]}
+    h_slots = {14: [(0, 1), (3, 1)]}
 
     @pl.loop(0, 16)
     def _(n):
@@ -889,11 +917,7 @@
 
     for w in range(4):
         core_copy(w).start()
-    h_mid(3, 2)
-    h_mid(0, 2)
-    u_copies[1].wait_recv()
-    u_copies[2].wait_recv()
-    out_o[...] = (dtok_o[...] + ur[1].astype(F32) + uzr[...].astype(F32)).astype(BF)
+    tick(9)
 
     def both(w):
         Wc[w] = (Wc[w].astype(F32) + Wp[:, cols(w * 256 + c * 128, 128)].astype(F32)).astype(BF)
@@ -911,12 +935,16 @@
     both(chip_a)
     both(chip)
     wa_copy = remote(Wc.at[chip_a], Wa, wa_s, wa_r, (a, z))
-    h_mid(2, 1)
-    h_mid(1, 1)
-    tick(9)
+    h_mid(3, 2)
+    h_mid(0, 2)
     wb_copy[1].wait_recv()
     Wc[chip_a] = (Wc[chip_a].astype(F32) + Wb[1].astype(F32)).astype(BF)
     wa_copy.start()
+    h_mid(2, 1)
+    h_mid(1, 1)
+    u_copies[1].wait_recv()
+    u_copies[2].wait_recv()
+    out_o[...] = (dtok_o[...] + ur[1].astype(F32) + uzr[...].astype(F32)).astype(BF)
 
     for t in range(4):
         ref = Hx.at[quarter(t)]
@@ -948,8 +976,8 @@
         piece = total[p * 256 : (p + 1) * 256, :]
         dwq_o[p] = piece.T
         dot_one = dot_one + jnp.sum(piece * wqkv[p].T.astype(F32), axis=0, keepdims=True)
-    for t in range(10, NU + 4):
-        tick(t)
+    tick(10)
+    tick(11)
     for e in range(NF + 1):
 
         @pl.when(no(org))
@@ -984,7 +1012,7 @@
     for c0 in range(2):
         for qi in range(2):
             pl.when(no(is_self(c0, qi)))(lambda c0=c0, qi=qi: att_back(c0, qi).wait_send())
-    for cp in d_copies + u_copies:
+    for cp in d_copies[:2] + u_copies:
         cp.wait_send()
     for e in range(NU):
         unit_b(e, 0).wait_send()
@@ -1040,7 +1068,7 @@
             vm((2, 256, 1024), BF), vm((2, 256, 1024), BF), vm((256, 1024), BF), vm((256, 1024), BF),
             vm((2, 256, 1024), BF), vm((2, 256, 1024), BF), vm((256, 1024), BF), vm((256, 1024), BF),
             vm((2, 512, 256), BF), vm((1024, 256), BF), vm((4, 4, 8, 256), F32),
-            vm((1024, 256), F32), vm((1024, 256), F32), vm((1024, 256), F32),
+            vm((256, 1024), F32), vm((1024, 256), F32), vm((1024, 256), F32),
             vm((4, 256, 1024), BF), vm((4, 256, 1024), BF), vm((256, 1024), BF),
             vm((2, FF3, 256), BF), vm((FF3, 256), BF), vm((FF3, 256), BF),
             vm((2, 2, 256, 256), BF), vm((2, 256, 256), BF), vm((3, 256, 256), BF), vm((FF3 + 256, 128), F32),

time: 224 us -> 212 us (0.946)
  Pallas kernels: 213 us -> 201 us
    pallas_call x1, Pallas kernels: 213 us -> 201 us  [run_layer(): pl.pallas_call(layer_kernel, out_shape=(s((256, 1024), BF), s((256, 1024)...]
where the time goes in v4:
time: 212 us
  Pallas kernels  201 us (95%)
  local copies, waits for them, and re-layouts  9.86 us (5%)
    pallas_call x1, Pallas kernels, run_layer(): pl.pallas_call(layer_kernel, out_shape=(s((256, 1024), BF), s((256, 1024)...  201 us
    unnamed x22, local copies, waits for them, and re-layouts  7.65 us

profile of v4, /device:TPU:0, one launch (start us, length us, event | category | flops | bytes accessed | tf_op | source)
XLA Modules:
  0.0 211.6 jit_solution(4718282723142109425)
XLA Ops:
  0.6 0.0 copy-start.7
  0.7 0.6 copy-done.7
  1.3 0.1 broadcast_in_dim.22
  1.4 0.1 tile.14
  1.5 0.0 copy-start.5
  1.5 0.1 broadcast_in_dim_tile.7
  1.5 0.6 copy-done.5
  2.1 0.0 copy-done.6
  2.1 0.1 broadcast_in_dim_tile.6
  2.2 0.6 concatenate.3.gains_in
  2.8 201.1 %layer.1 = (bf16[256,1024]{1,0:T(8,128)(2,1)}, f32[256,1024]{1,0:T(8,128)}, f32[3,128,256]{2,1,0:T(8,128)}, f32[1312,128]{1,0:T(8,128)}, f32[656,128]{1,0:T(8,12...) custom-call(s32[32]{0:T(128)} %lengths.1, s32[32]{0:T(128)} %seq_order.1, bf16[256,1024]{1,0:T(8,128)(2,1)} %tok.1, ...), custom_call_target="tpu_custom_call" | custom-call | tf_op jit(solution)/shard_map/layer/pallas_call | solution.py:1052
  203.9 0.0 copy-start
  203.9 1.3 slice_bitcast_fusion
  205.2 1.9 copy.25
  207.1 0.0 copy-done
  207.1 1.0 copy.26
  208.0 0.3 copy-done.2
  208.3 0.7 copy.27
  209.0 0.0 copy-done.4
  209.0 0.7 copy.28
  209.7 0.0 copy-done.1
  209.7 0.8 copy.29
  210.5 0.3 copy-done.3
  210.9 0.7 copy.30
  (10 shorter events, 0.0 us)
Async XLA Ops:
  0.6 0.7 copy-start.7
  1.5 0.7 copy-start.5
  1.5 0.7 copy-start.6
  203.9 3.2 %copy-start = (f32[256,1024]{1,0:T(8,128)S(1)}, f32[256,1024]{1,0:T(8,128)}, u32[]{:S(2)}) copy-start(f32[256,1024]{1,0:T(8,128)} %get-tuple-element.35) | copy-start | bytes 3145732
  207.1 1.2 copy-start.2
  207.1 2.0 copy-start.4
  208.3 1.4 copy-start.1
  209.7 1.2 copy-start.3

commit v5 on v4

--- a/solution.py
+++ b/solution.py
@@ -802,18 +802,18 @@
         seg_k = segc[rj, :]
         same = jnp.concatenate([seg_k, seg_k], axis=1) == segr[0:1, ri]
         none = jnp.zeros((), BF)
-        dvs, dks, dqs = [], [], []
-        for h in range(4):
-            mine = head_of == h
-            qh, dah = jnp.where(mine, qi_, none), jnp.where(mine, dai, none)
-            s = lax.dot_general(kj, qh, NT, preferred_element_type=F32)
-            p = jnp.exp(jnp.where(same, s, masked_fill) - lse[h, i, 0:1, :])
-            dp_ = lax.dot_general(vj, dah, NT, preferred_element_type=F32)
-            dsc = (p * (dp_ - delta[h, i, 0:1, :])).astype(BF)
-            dvs.append(jnp.dot(p.astype(BF), dah, preferred_element_type=F32))
-            dks.append(jnp.dot(dsc, qh, preferred_element_type=F32))
-            hr = slice(h * HEAD_DIM, (h + 1) * HEAD_DIM)
-            dqs.append(jnp.dot(kT[hr, rj], dsc, preferred_element_type=F32))
+        heads = range(4)
+        qh = [jnp.where(head_of == h, qi_, none) for h in heads]
+        dah = [jnp.where(head_of == h, dai, none) for h in heads]
+        ss = [lax.dot_general(kj, qh[h], NT, preferred_element_type=F32) for h in heads]
+        dps = [lax.dot_general(vj, dah[h], NT, preferred_element_type=F32) for h in heads]
+        ps = [jnp.exp(jnp.where(same, ss[h], masked_fill) - lse[h, i, 0:1, :]) for h in heads]
+        dss = [(ps[h] * (dps[h] - delta[h, i, 0:1, :])).astype(BF) for h in heads]
+        dvs = [jnp.dot(ps[h].astype(BF), dah[h], preferred_element_type=F32) for h in heads]
+        dks = [jnp.dot(dss[h], qh[h], preferred_element_type=F32) for h in heads]
+        dqs = [
+            jnp.dot(kT[h * HEAD_DIM : (h + 1) * HEAD_DIM, rj], dss[h], preferred_element_type=F32) for h in heads
+        ]
         dv[rj, :] = dv[rj, :] + (dvs[0] + dvs[1] + dvs[2] + dvs[3])
         dk[rj, :] = dk[rj, :] + (dks[0] + dks[1] + dks[2] + dks[3])
         for h in range(4):
@@ -946,28 +946,6 @@
     u_copies[2].wait_recv()
     out_o[...] = (dtok_o[...] + ur[1].astype(F32) + uzr[...].astype(F32)).astype(BF)
 
-    for t in range(4):
-        ref = Hx.at[quarter(t)]
-        pl.when(z < 3)(lambda t=t: h_wait(z, t))
-        pl.when(z > 0)(lambda t=t, ref=ref: remote(ref, ref, hu_s.at[0, t], hx_r.at[t], (core, z)).wait_recv())
-    has_above, has_below = z < 3, z > 0
-
-    @pl.when(has_above)
-    def _():
-        acc[...] = acc[...] + Hi[z].astype(F32)
-
-    @pl.when(has_below)
-    def _():
-        acc[...] = acc[...] + Hx[...].astype(F32)
-
-    @pl.loop(0, 8)
-    def _(r):
-        xhat, rstd = norm_rows(tok[chunk(r), :].astype(F32))
-        e1 = acc[chunk(r), :] * gain1
-        m1 = jnp.mean(e1, axis=-1, keepdims=True)
-        m2 = jnp.mean(e1 * xhat, axis=-1, keepdims=True)
-        dtok_o[chunk(r), :] = dX1[chunk(r), :] + rstd * (e1 - m1 - xhat * m2)
-
     wb_copy[0].wait_recv()
     wa_copy.wait_recv()
     total = Wc[chip].astype(F32) + Wb[0].astype(F32) + Wa[...].astype(F32)
@@ -976,15 +954,15 @@
         piece = total[p * 256 : (p + 1) * 256, :]
         dwq_o[p] = piece.T
         dot_one = dot_one + jnp.sum(piece * wqkv[p].T.astype(F32), axis=0, keepdims=True)
-    tick(10)
-    tick(11)
-    for e in range(NF + 1):
-
-        @pl.when(no(org))
-        def _(e=e):
-            slot, _, ref = final(e)
-            remote(ref, ref, fin_s.at[slot], fin_r.at[slot], (core, z)).wait_recv()
-
+    def finals(slots_):
+        for e in slots_:
+
+            @pl.when(no(org))
+            def _(e=e):
+                slot, _, ref = final(e)
+                remote(ref, ref, fin_s.at[slot], fin_r.at[slot], (core, z)).wait_recv()
+
+    finals(range(NF))
     part_two = jnp.sum(dwin_o[...] * w3[0 : 2 * HID, :].astype(F32), axis=0, keepdims=True)
     gz[z, 0:1, :] = dot_one / gains[dp, 0:1, :]
     gz[z, 1:2, :] = part_two / gains[dp, 1:2, :]
@@ -994,6 +972,31 @@
     ]
     for cp in gain_copy:
         cp.start()
+    for t in range(4):
+        ref = Hx.at[quarter(t)]
+        pl.when(z < 3)(lambda t=t: h_wait(z, t))
+        pl.when(z > 0)(lambda t=t, ref=ref: remote(ref, ref, hu_s.at[0, t], hx_r.at[t], (core, z)).wait_recv())
+    has_above, has_below = z < 3, z > 0
+
+    @pl.when(has_above)
+    def _():
+        acc[...] = acc[...] + Hi[z].astype(F32)
+
+    @pl.when(has_below)
+    def _():
+        acc[...] = acc[...] + Hx[...].astype(F32)
+
+    @pl.loop(0, 8)
+    def _(r):
+        xhat, rstd = norm_rows(tok[chunk(r), :].astype(F32))
+        e1 = acc[chunk(r), :] * gain1
+        m1 = jnp.mean(e1, axis=-1, keepdims=True)
+        m2 = jnp.mean(e1 * xhat, axis=-1, keepdims=True)
+        dtok_o[chunk(r), :] = dX1[chunk(r), :] + rstd * (e1 - m1 - xhat * m2)
+
+    tick(10)
+    tick(11)
+    finals((NF,))
     for n in range(1, 4):
         o = lax.rem(z + n, 4)
         remote(gz.at[o], gz.at[o], gz_s.at[n], gz_r.at[o], (core, z)).wait_recv()

time: 212 us -> 204 us (0.962)
  Pallas kernels: 201 us -> 192 us
    pallas_call x1, Pallas kernels: 201 us -> 192 us  [run_layer(): pl.pallas_call(layer_kernel, out_shape=(s((256, 1024), BF), s((256, 1024)...]
where the time goes in v5:
time: 204 us; the launch traced here: 203 us
  Pallas kernels  192 us (94%)
  local copies, waits for them, and re-layouts  9.86 us (5%)
    pallas_call x1, Pallas kernels, run_layer(): pl.pallas_call(layer_kernel, out_shape=(s((256, 1024), BF), s((256, 1024)...  192 us
    unnamed x22, local copies, waits for them, and re-layouts  7.65 us

profile of v5, /device:TPU:0, one launch (start us, length us, event | category | flops | bytes accessed | tf_op | source)
XLA Modules:
  0.0 202.7 jit_solution(6270129653250347630)
XLA Ops:
  0.6 0.0 copy-start.7
  0.7 0.6 copy-done.7
  1.3 0.1 broadcast_in_dim.22
  1.4 0.1 tile.14
  1.5 0.0 copy-start.5
  1.5 0.1 broadcast_in_dim_tile.7
  1.5 0.6 copy-done.5
  2.1 0.0 copy-done.6
  2.1 0.1 broadcast_in_dim_tile.6
  2.2 0.6 concatenate.3.gains_in
  2.8 192.2 %layer.1 = (bf16[256,1024]{1,0:T(8,128)(2,1)}, f32[256,1024]{1,0:T(8,128)}, f32[3,128,256]{2,1,0:T(8,128)}, f32[1312,128]{1,0:T(8,128)}, f32[656,128]{1,0:T(8,12...) custom-call(s32[32]{0:T(128)} %lengths.1, s32[32]{0:T(128)} %seq_order.1, bf16[256,1024]{1,0:T(8,128)(2,1)} %tok.1, ...), custom_call_target="tpu_custom_call" | custom-call | tf_op jit(solution)/shard_map/layer/pallas_call | solution.py:1055
  195.0 0.0 copy-start
  195.0 1.3 slice_bitcast_fusion
  196.3 1.9 copy.25
  198.2 0.0 copy-done
  198.2 1.0 copy.26
  199.2 0.3 copy-done.2
  199.4 0.7 copy.27
  200.2 0.0 copy-done.4
  200.2 0.7 copy.28
  200.8 0.0 copy-done.1
  200.8 0.8 copy.29
  201.7 0.3 copy-done.3
  202.0 0.7 copy.30
  (10 shorter events, 0.0 us)
Async XLA Ops:
  0.6 0.7 copy-start.7
  1.5 0.7 copy-start.5
  1.5 0.7 copy-start.6
  195.0 3.2 %copy-start = (f32[256,1024]{1,0:T(8,128)S(1)}, f32[256,1024]{1,0:T(8,128)}, u32[]{:S(2)}) copy-start(f32[256,1024]{1,0:T(8,128)} %get-tuple-element.35) | copy-start | bytes 3145732
  198.2 1.2 copy-start.2
  198.2 2.0 copy-start.4
  199.4 1.4 copy-start.1
  200.8 1.2 copy-start.3

commit v6 on v5

--- a/solution.py
+++ b/solution.py
@@ -328,24 +328,27 @@
                 r = r * (HEAD_DIM**-0.5)
             dst[rows, :] = r.astype(BF)
 
+    def receive(k_):
+        below, above = z - k_ >= 0, z + k_ <= 3
+        for h in range(2):
+
+            @pl.when(below)
+            def _(k_=k_, h=h):
+                ref = tall.at[z - k_, pl.ds(h * 128, 128)]
+                remote(ref, ref, us.at[k_, h], rb.at[k_, h], (core, z)).wait_recv()
+                if k_ < 3:
+                    pl.when(up_ok(k_))(lambda: tok_up(k_, h).start())
+
+            @pl.when(above)
+            def _(k_=k_, h=h):
+                ref = tall.at[z + k_, pl.ds(h * 128, 128)]
+                remote(ref, ref, ds.at[k_, h], ra.at[k_, h], (core, z)).wait_recv()
+                if k_ < 3:
+                    pl.when(down_ok(k_))(lambda: tok_down(k_, h).start())
+
     for k_ in range(4):
-        if k_ > 0:
-            below, above = z - k_ >= 0, z + k_ <= 3
-            for h in range(2):
-
-                @pl.when(below)
-                def _(k_=k_, h=h):
-                    ref = tall.at[z - k_, pl.ds(h * 128, 128)]
-                    remote(ref, ref, us.at[k_, h], rb.at[k_, h], (core, z)).wait_recv()
-                    if k_ < 3:
-                        pl.when(up_ok(k_))(lambda: tok_up(k_, h).start())
-
-                @pl.when(above)
-                def _(k_=k_, h=h):
-                    ref = tall.at[z + k_, pl.ds(h * 128, 128)]
-                    remote(ref, ref, ds.at[k_, h], ra.at[k_, h], (core, z)).wait_recv()
-                    if k_ < 3:
-                        pl.when(down_ok(k_))(lambda: tok_down(k_, h).start())
+        if k_ != 1:
+            receive(max(k_, 1))
 
         if k_ == 1:
 

time: 204 us -> 201 us (0.985)
    pallas_call x1, Pallas kernels: 192 us -> 190 us  [run_layer(): pl.pallas_call(layer_kernel, out_shape=(s((256, 1024), BF), s((256, 1024)...]
where the time goes in v6:
time: 201 us; the launch traced here: 200 us
  Pallas kernels  190 us (95%)
  local copies, waits for them, and re-layouts  9.86 us (5%)
    pallas_call x1, Pallas kernels, run_layer(): pl.pallas_call(layer_kernel, out_shape=(s((256, 1024), BF), s((256, 1024)...  190 us
    unnamed x22, local copies, waits for them, and re-layouts  7.65 us

profile of v6, /device:TPU:0, one launch (start us, length us, event | category | flops | bytes accessed | tf_op | source)
XLA Modules:
  0.0 200.5 jit_solution(3265100209505227515)
XLA Ops:
  0.6 0.0 copy-start.7
  0.7 0.6 copy-done.7
  1.3 0.1 broadcast_in_dim.22
  1.4 0.1 tile.14
  1.5 0.0 copy-start.6
  1.5 0.1 broadcast_in_dim_tile.7
  1.5 0.6 copy-done.5
  2.1 0.0 copy-done.6
  2.1 0.1 broadcast_in_dim_tile.6
  2.2 0.6 concatenate.3.gains_in
  2.8 189.9 %layer.1 = (bf16[256,1024]{1,0:T(8,128)(2,1)}, f32[256,1024]{1,0:T(8,128)}, f32[3,128,256]{2,1,0:T(8,128)}, f32[1312,128]{1,0:T(8,128)}, f32[656,128]{1,0:T(8,12...) custom-call(s32[32]{0:T(128)} %lengths.1, s32[32]{0:T(128)} %seq_order.1, bf16[256,1024]{1,0:T(8,128)(2,1)} %tok.1, ...), custom_call_target="tpu_custom_call" | custom-call | tf_op jit(solution)/shard_map/layer/pallas_call | solution.py:1058
  192.7 0.0 copy-start
  192.8 1.3 slice_bitcast_fusion
  194.0 1.9 copy.25
  195.9 0.0 copy-done
  195.9 1.0 copy.26
  196.9 0.3 copy-done.2
  197.1 0.7 copy.27
  197.9 0.0 copy-done.4
  197.9 0.7 copy.28
  198.5 0.0 copy-done.1
  198.5 0.8 copy.29
  199.4 0.3 copy-done.3
  199.7 0.7 copy.30
  (10 shorter events, 0.0 us)
Async XLA Ops:
  0.6 0.7 copy-start.7
  1.5 0.7 copy-start.5
  1.5 0.7 copy-start.6
  192.7 3.2 %copy-start = (f32[256,1024]{1,0:T(8,128)S(1)}, f32[256,1024]{1,0:T(8,128)}, u32[]{:S(2)}) copy-start(f32[256,1024]{1,0:T(8,128)} %get-tuple-element.35) | copy-start | bytes 3145732
  195.9 1.2 copy-start.2
  195.9 2.0 copy-start.4
  197.1 1.4 copy-start.1
  198.5 1.2 copy-start.3

commit v7 on v6

--- a/solution.py
+++ b/solution.py
@@ -559,7 +559,7 @@
             h_copy[2].start()
             remote(h2a.at[db], h2a.at[db], n_s.at[2], n_r.at[2], (core, z)).wait_recv()
 
-        for r0, n in ((0, 224), (224, 224), (448, 208)):
+        for r0, n in ((0, 336), (336, 320)):
             tile(r0, n, cols(there * 512, 512))
 
     def tn(lhs, rhs):

time: 201 us -> 200 us (level)
  no operation moved by 1% of the time
where the time goes in v7:
time: 200 us
  Pallas kernels  189 us (94%)
  local copies, waits for them, and re-layouts  9.86 us (5%)
    pallas_call x1, Pallas kernels, run_layer(): pl.pallas_call(layer_kernel, out_shape=(s((256, 1024), BF), s((256, 1024)...  189 us
    unnamed x22, local copies, waits for them, and re-layouts  7.65 us

profile of v7, /device:TPU:0, one launch (start us, length us, event | category | flops | bytes accessed | tf_op | source)
XLA Modules:
  0.0 199.7 jit_solution(10222923793865413794)
XLA Ops:
  0.6 0.0 copy-start.7
  0.7 0.6 copy-done.7
  1.3 0.1 broadcast_in_dim.22
  1.4 0.1 tile.14
  1.5 0.0 copy-start.5
  1.5 0.1 broadcast_in_dim_tile.7
  1.5 0.6 copy-done.5
  2.1 0.0 copy-done.6
  2.1 0.1 broadcast_in_dim_tile.6
  2.2 0.6 concatenate.3.gains_in
  2.8 189.2 %layer.1 = (bf16[256,1024]{1,0:T(8,128)(2,1)}, f32[256,1024]{1,0:T(8,128)}, f32[3,128,256]{2,1,0:T(8,128)}, f32[1312,128]{1,0:T(8,128)}, f32[656,128]{1,0:T(8,12...) custom-call(s32[32]{0:T(128)} %lengths.1, s32[32]{0:T(128)} %seq_order.1, bf16[256,1024]{1,0:T(8,128)(2,1)} %tok.1, ...), custom_call_target="tpu_custom_call" | custom-call | tf_op jit(solution)/shard_map/layer/pallas_call | solution.py:1058
  192.0 0.0 copy-start
  192.0 1.3 slice_bitcast_fusion
  193.3 1.9 copy.25
  195.1 0.0 copy-done
  195.2 1.0 copy.26
  196.1 0.3 copy-done.2
  196.4 0.7 copy.27
  197.1 0.0 copy-done.4
  197.1 0.7 copy.28
  197.8 0.0 copy-done.1
  197.8 0.8 copy.29
  198.6 0.3 copy-done.3
  199.0 0.7 copy.30
  (10 shorter events, 0.0 us)
Async XLA Ops:
  0.6 0.7 copy-start.7
  1.5 0.7 copy-start.5
  1.5 0.7 copy-start.6
  192.0 3.2 %copy-start = (f32[256,1024]{1,0:T(8,128)S(1)}, f32[256,1024]{1,0:T(8,128)}, u32[]{:S(2)}) copy-start(f32[256,1024]{1,0:T(8,128)} %get-tuple-element.35) | copy-start | bytes 3145732
  195.1 1.2 copy-start.2
  195.1 2.0 copy-start.4
  196.4 1.4 copy-start.1
  197.8 1.2 copy-start.3
